TPU v7x, 256 devices: a whole 4x4x8 slice. The times are simulated.
256 devices in a mesh: view: 2 (over core), sky: 128 (over z, x, y).
Axes of the slice: x: 4, y: 4, z: 8, core: 2. Of those that a mesh axis runs over, the one named last changes fastest.
Arguments:
- pixels: bfloat16 [2, 262144, 128], P('view', 'sky'), may hold values from -6 to 6
- cotangent: bfloat16 [2, 262144, 128], P('view', 'sky'), may hold values from -6 to 6
- filters: bfloat16 [4, 128, 128], replicated, may hold values from -0.25 to 0.25
- lap_tiles: bfloat16 [128, 24, 256, 256], P('sky'), may hold values from -0.15625 to 0.15625
- tile_target: int32 [128, 24], P('sky'), may hold values from 0 to 7
- tile_source: int32 [128, 24], P('sky'), may hold values from 0 to 15
- tile_count: int32 [128], P('sky'), may hold values from 12 to 24, as said below
- send_blocks: int32 [128, 4, 2], P('sky'), may hold values from 0 to 7
Outputs:
- outputs: bfloat16 [2, 262144, 128], P('view', 'sky')
- pixel_grad: bfloat16 [2, 262144, 128], P('view', 'sky')
- filter_grad: float32 [4, 128, 128], replicated
Inputs may be any that keep to these rules, and one draw needn't show every extreme that they name: `tile_count`: every device has at least half of 24 live tiles, and some device has exactly 24. `tile_source`: indices below 8 are own blocks, the others received ones.
All inputs are finite; a program needn't handle non-finite values.
Results may differ from a plain program's by a relative error of at most 0.017.
Values may be sent and summed in bfloat16 or wider, within the bound.
No kernel may reach another device: no remote copies, remote signals or barrier semaphores. Data moves between devices by JAX's collectives and lax.ppermute only.
A program may use at most 64 MiB of HBM per device.

v0:
```python
import math

import jax
import jax.numpy as jnp
from jax import lax
from jax.sharding import PartitionSpec as P

OFFSETS = (1, -1, 2, -2)


def passed_along(array, axis, by):
    size = lax.axis_size(axis)
    pairs = [(i, i + by) for i in range(size) if 0 <= i + by < size]
    return lax.ppermute(array, axis, pairs)


def spread_forward(pieces):
    return [passed_along(portion, "sky", offset) for offset, portion in zip(OFFSETS, pieces)]


def spread_backward(pieces):
    return [passed_along(portion, "sky", -offset) for offset, portion in zip(OFFSETS, pieces)]


def tile_products(values, tile_set, target, source, live_count, out_count, transposed):
    contraction = "tpq,tpc->tqc" if transposed else "tpq,tqc->tpc"
    picked = values[target] if transposed else values[source]
    routed = source if transposed else target
    products = jnp.einsum(contraction, tile_set, picked, preferred_element_type=jnp.float32)
    live_mask = jnp.arange(routed.shape[0]) < live_count
    routing = ((routed[None, :] == jnp.arange(out_count)[:, None]) & live_mask[None, :]).astype(
        jnp.float32
    )
    return jnp.einsum("bt,tpc->bpc", routing, products)


def per_device(
    pixels, cotangent, filters, lap_tiles, tile_target, tile_source, tile_count, send_blocks
):
    block_size = lap_tiles.shape[2]
    channels = pixels.shape[2]
    row_count = pixels.shape[1]
    block_count = row_count // block_size
    send_count = send_blocks.shape[2]
    ext_count = block_count + 4 * send_count
    tile_set = lap_tiles[0]
    target = tile_target[0]
    source = tile_source[0]
    live_count = tile_count[0]
    chosen = send_blocks[0]

    def forward_pieces(blocks):
        return [blocks[chosen[number]] for number in range(4)]

    def forward_finish(blocks, arrived):
        extended = jnp.concatenate([blocks] + arrived, axis=0)
        return tile_products(extended, tile_set, target, source, live_count, block_count, False)

    def transposed_start(blocks):
        slot_sums = tile_products(blocks, tile_set, target, source, live_count, ext_count, True)
        pieces = [
            slot_sums[block_count + number * send_count : block_count + (number + 1) * send_count]
            for number in range(4)
        ]
        return (slot_sums, pieces)

    def transposed_finish(slot_sums, arrived):
        combined = slot_sums[:block_count]
        for number in range(4):
            routing = (chosen[number][None, :] == jnp.arange(block_count)[:, None]).astype(
                jnp.float32
            )
            combined = combined + jnp.einsum("bj,jqc->bqc", routing, arrived[number])
        return combined

    def apply_forward(blocks):
        return forward_finish(blocks, spread_forward(forward_pieces(blocks)))

    def apply_transposed(blocks):
        slot_sums, pieces = transposed_start(blocks)
        return transposed_finish(slot_sums, spread_backward(pieces))

    upstream = cotangent[0]

    def filter_term(member):
        return jnp.einsum("pc,pd->cd", member, upstream, preferred_element_type=jnp.float32)

    base = pixels[0].reshape(block_count, block_size, channels)
    pulled = [
        jnp.einsum(
            "pd,cd->pc", upstream, filters[order], preferred_element_type=jnp.float32
        ).reshape(block_count, block_size, channels)
        for order in range(4)
    ]
    adj_three = pulled[3]
    grad_terms = [filter_term(pixels[0])]
    cheb_one = apply_forward(base).astype(jnp.bfloat16)
    grad_terms.append(filter_term(cheb_one.reshape(row_count, channels)))
    cheb_two = (2.0 * apply_forward(cheb_one) - base.astype(jnp.float32)).astype(jnp.bfloat16)
    grad_terms.append(filter_term(cheb_two.reshape(row_count, channels)))
    cheb_three = (2.0 * apply_forward(cheb_two) - cheb_one.astype(jnp.float32)).astype(jnp.bfloat16)
    grad_terms.append(filter_term(cheb_three.reshape(row_count, channels)))
    adj_two = pulled[2] + 2.0 * apply_transposed(adj_three.astype(jnp.bfloat16))
    adj_one = pulled[1] + 2.0 * apply_transposed(adj_two.astype(jnp.bfloat16)) - adj_three
    adj_zero = pulled[0] + apply_transposed(adj_one.astype(jnp.bfloat16)) - adj_two
    flattened = [
        member.reshape(row_count, channels) for member in (base, cheb_one, cheb_two, cheb_three)
    ]
    result = jnp.dot(flattened[0], filters[0], preferred_element_type=jnp.float32)
    for order in range(1, 4):
        result = result + jnp.dot(
            flattened[order], filters[order], preferred_element_type=jnp.float32
        )
    outputs = result.astype(jnp.bfloat16).reshape(1, row_count, channels)
    pixel_grad = adj_zero.astype(jnp.bfloat16).reshape(1, row_count, channels)
    stacked = lax.psum(jnp.stack(grad_terms), ("view", "sky"))
    scale = 1.0 / math.sqrt(lax.axis_size("view") * lax.axis_size("sky") * row_count)
    return (outputs, pixel_grad, stacked * scale)


def solution(mesh):
    return jax.shard_map(
        per_device,
        mesh=mesh,
        in_specs=(
            P("view", "sky", None),
            P("view", "sky", None),
            P(),
            P("sky", None, None, None),
            P("sky", None),
            P("sky", None),
            P("sky"),
            P("sky", None, None),
        ),
        out_specs=(P("view", "sky", None), P("view", "sky", None), P()),
        check_vma=False,
    )
```

profile of v0, /device:TPU:1, one launch (start us, length us, event | category | flops | bytes accessed | tf_op | source)
XLA Modules:
  0.0 552.6 jit_solution(11454189926382703795)
XLA Ops:
  10.6 3.0 gather_fusion.15
  13.6 3.3 fusion.16
  16.9 2.8 copy.48
  24.6 6.3 %collective-permute-start.15 = (bf16[2,256,128]{2,0,1:T(2,128)(2,1)}, bf16[2,256,128]{2,0,1:T(2,128)(2,1)}, u32[]{:S(2)}, u32[]{:S(2)}) collective-permute-start(bf16[2,256,128]{2,0,1:T(2,128)(2,1)} %get-tuple-element.16), channel_id=1, source_target_pairs={{0,2},{1,3},{2,4},{3,5},{4,6},{5,7},{6,8},{7,9},{8,10},{9,11},{10,... | collective-permute-start | bytes 393224 | tf_op jit(solution)/shard_map/ppermute | solution.py:14
  32.2 3.0 collective-permute-start.13
  38.2 4.1 collective-permute-start
  61.5 5.3 collective-permute-start.2
  71.4 4.2 collective-permute-done.3
  76.3 3.3 gather_fusion.4
  79.6 3.8 fusion.22
  83.3 2.8 copy.42
  105.3 3.1 gather_fusion.16
  108.5 3.2 fusion.14
  117.5 6.5 %collective-permute-start.19 = (bf16[2,256,128]{2,0,1:T(2,128)(2,1)}, bf16[2,256,128]{2,0,1:T(2,128)(2,1)}, u32[]{:S(2)}, u32[]{:S(2)}) collective-permute-start(bf16[2,256,128]{2,0,1:T(2,128)(2,1)} %get-tuple-element.12), channel_id=1, source_target_pairs={{0,2},{1,3},{2,4},{3,5},{4,6},{5,7},{6,8},{7,9},{8,10},{9,11},{10,... | collective-permute-start | bytes 393224 | tf_op jit(solution)/shard_map/ppermute | solution.py:14
  128.0 5.1 collective-permute-start.6
  138.1 3.5 collective-permute-start.17
  142.9 6.4 %concatenate.10 = bf16[16,256,128]{2,0,1:T(8,128)(2,1)} concatenate(bf16[8,256,128]{2,0,1:T(8,128)(2,1)} %copy-done.6, bf16[2,256,128]{2,0,1:T(2,128)(2,1)} %collective-permute-done.4, bf16[2,256,128]{2,0,1:T(2,128)(2,1)} %collective-permute-done.5, bf16[2,256,128]{2,0,1:T(2,128)(2,1)S(1)} %collective-permute-done.6, bf16[2,256,128]{2,0,1:T(2,128)(2,1)S(1)} %collective-permute-done.7), dimensions={0} | concatenate | bytes 2097152 | tf_op jit(solution)/shard_map/concatenate | solution.py:56
  151.9 3.3 gather_fusion.9
  155.1 3.8 fusion.20
  158.9 2.8 copy.43
  181.3 3.1 gather_fusion.17
  184.4 3.2 fusion.12
  194.1 6.1 %collective-permute-start.21 = (bf16[2,256,128]{2,0,1:T(2,128)(2,1)S(1)}, bf16[2,256,128]{2,0,1:T(2,128)(2,1)S(1)}, u32[]{:S(2)}, u32[]{:S(2)}) collective-permute-start(bf16[2,256,128]{2,0,1:T(2,128)(2,1)S(1)} %get-tuple-element.10), channel_id=1, source_target_pairs={{0,1},{1,2},{2,3},{3,4},{4,5},{5,6},{6,7},{7,8},{8,9},{9,10},{10,1... | collective-permute-start | bytes 393224 | tf_op jit(solution)/shard_map/ppermute | solution.py:14
  200.2 7.6 %collective-permute-start.23 = (bf16[2,256,128]{2,0,1:T(2,128)(2,1)S(1)}, bf16[2,256,128]{2,0,1:T(2,128)(2,1)S(1)}, u32[]{:S(2)}, u32[]{:S(2)}) collective-permute-start(bf16[2,256,128]{2,0,1:T(2,128)(2,1)S(1)} %get-tuple-element.8), channel_id=1, source_target_pairs={{0,2},{1,3},{2,4},{3,5},{4,6},{5,7},{6,8},{7,9},{8,10},{9,11},{10,... | collective-permute-start | bytes 393224 | tf_op jit(solution)/shard_map/ppermute | solution.py:14
  209.3 7.9 %collective-permute-start.10 = (bf16[2,256,128]{2,0,1:T(2,128)(2,1)S(1)}, bf16[2,256,128]{2,0,1:T(2,128)(2,1)}, u32[]{:S(2)}, u32[]{:S(2)}) collective-permute-start(bf16[2,256,128]{2,0,1:T(2,128)(2,1)S(1)} %copy.31), channel_id=1, source_target_pairs={{0,2},{1,3},{2,4},{3,5},{4,6},{5,7},{6,8},{7,9},{8,10},{9,11},{10,... | collective-permute-start | bytes 393224 | tf_op jit(solution)/shard_map/ppermute | solution.py:14
  221.3 3.1 collective-permute-start.8
  228.4 3.1 collective-permute-done.9
  231.5 6.5 %concatenate.11 = bf16[16,256,128]{2,0,1:T(8,128)(2,1)} concatenate(bf16[8,256,128]{2,0,1:T(8,128)(2,1)} %copy-done.13, bf16[2,256,128]{2,0,1:T(2,128)(2,1)} %collective-permute-done.8, bf16[2,256,128]{2,0,1:T(2,128)(2,1)} %collective-permute-done.9, bf16[2,256,128]{2,0,1:T(2,128)(2,1)} %collective-permute-done.10, bf16[2,256,128]{2,0,1:T(2,128)(2,1)S(1)} %collective-permute-done.11), dimensions={0} | concatenate | bytes 2097152 | tf_op jit(solution)/shard_map/concatenate | solution.py:56
  240.5 3.3 gather_fusion.14
  243.8 3.7 fusion.18
  247.5 2.7 copy.44
  256.4 287.7 %all-reduce.2.cloned.1.call-done = f32[4,128,128]{2,1,0:T(8,128)} async-done(((f32[4,128,128]{2,1,0:T(8,128)}), f32[4,128,128]{2,1,0:T(8,128)}) %all-reduce.2.cloned.1.call-update) | async-done | bytes 262160 | tf_op jit(solution)/shard_map/psum | solution.py:116
  (197 shorter events, 119.4 us)
Async XLA Ops:
  7.2 536.9 %all-reduce.2.cloned.1.call-start = ((), (), s32[]{:S(2)}) async-start(), calls=%async_computation | async-start | bytes 524288 | tf_op jit(solution)/shard_map/psum | solution.py:116
  23.5 23.1 %copy-start.21 = (bf16[4,128,128]{2,1,0:T(8,128)(2,1)S(1)}, bf16[4,128,128]{2,1,0:T(8,128)(2,1)}, u32[]{:S(2)}) copy-start(bf16[4,128,128]{2,1,0:T(8,128)(2,1)} %param.10) | copy-start | bytes 393220
  24.6 73.2 %collective-permute-start.15 = (bf16[2,256,128]{2,0,1:T(2,128)(2,1)}, bf16[2,256,128]{2,0,1:T(2,128)(2,1)}, u32[]{:S(2)}, u32[]{:S(2)}) collective-permute-start(bf16[2,256,128]{2,0,1:T(2,128)(2,1)} %get-tuple-element.16), channel_id=1, source_target_pairs={{0,2},{1,3},{2,4},{3,5},{4,6},{5,7},{6,8},{7,9},{8,10},{9,11},{10,... | collective-permute-start | bytes 393224 | tf_op jit(solution)/shard_map/ppermute | solution.py:14
  30.9 68.4 %collective-permute-start.14 = (bf16[2,256,128]{2,0,1:T(2,128)(2,1)}, bf16[2,256,128]{2,0,1:T(2,128)(2,1)}, u32[]{:S(2)}, u32[]{:S(2)}) collective-permute-start(bf16[2,256,128]{2,0,1:T(2,128)(2,1)} %get-tuple-element.17), channel_id=1, source_target_pairs={{2,0},{3,1},{4,2},{5,3},{6,4},{7,5},{8,6},{9,7},{10,8},{11,9},{12,... | collective-permute-start | bytes 393224 | tf_op jit(solution)/shard_map/ppermute | solution.py:14
  32.2 68.4 %collective-permute-start.13 = (bf16[2,256,128]{2,0,1:T(2,128)(2,1)}, bf16[2,256,128]{2,0,1:T(2,128)(2,1)}, u32[]{:S(2)}, u32[]{:S(2)}) collective-permute-start(bf16[2,256,128]{2,0,1:T(2,128)(2,1)} %get-tuple-element.18), channel_id=1, source_target_pairs={{0,1},{1,2},{2,3},{3,4},{4,5},{5,6},{6,7},{7,8},{8,9},{9,10},{10,1... | collective-permute-start | bytes 393224 | tf_op jit(solution)/shard_map/ppermute | solution.py:14
  38.2 23.4 %collective-permute-start = (bf16[2,256,128]{2,1,0:T(8,128)(2,1)}, bf16[2,256,128]{2,1,0:T(8,128)(2,1)S(1)}, u32[]{:S(2)}, u32[]{:S(2)}) collective-permute-start(bf16[2,256,128]{2,1,0:T(8,128)(2,1)} %gather_fusion), channel_id=1, source_target_pairs={{0,1},{1,2},{2,3},{3,4},{4,5},{5,6},{6,7},{7,8},{8,9},{9,10},{10,1... | collective-permute-start | bytes 393224 | tf_op jit(solution)/shard_map/ppermute | solution.py:14
  45.2 22.3 %collective-permute-start.1 = (bf16[2,256,128]{2,1,0:T(8,128)(2,1)}, bf16[2,256,128]{2,1,0:T(8,128)(2,1)S(1)}, u32[]{:S(2)}, u32[]{:S(2)}) collective-permute-start(bf16[2,256,128]{2,1,0:T(8,128)(2,1)} %gather_fusion.1), channel_id=1, source_target_pairs={{1,0},{2,1},{3,2},{4,3},{5,4},{6,5},{7,6},{8,7},{9,8},{10,9},{11,1... | collective-permute-start | bytes 393224 | tf_op jit(solution)/shard_map/ppermute | solution.py:14
  61.5 7.9 %collective-permute-start.2 = (bf16[2,256,128]{2,1,0:T(8,128)(2,1)}, bf16[2,256,128]{2,1,0:T(8,128)(2,1)S(1)}, u32[]{:S(2)}, u32[]{:S(2)}) collective-permute-start(bf16[2,256,128]{2,1,0:T(8,128)(2,1)} %gather_fusion.2), channel_id=1, source_target_pairs={{0,2},{1,3},{2,4},{3,5},{4,6},{5,7},{6,8},{7,9},{8,10},{9,11},{10,... | collective-permute-start | bytes 393224 | tf_op jit(solution)/shard_map/ppermute | solution.py:14
  67.5 8.1 %collective-permute-start.3 = (bf16[2,256,128]{2,1,0:T(8,128)(2,1)}, bf16[2,256,128]{2,1,0:T(8,128)(2,1)S(1)}, u32[]{:S(2)}, u32[]{:S(2)}) collective-permute-start(bf16[2,256,128]{2,1,0:T(8,128)(2,1)} %gather_fusion.3), channel_id=1, source_target_pairs={{2,0},{3,1},{4,2},{5,3},{6,4},{7,5},{8,6},{9,7},{10,8},{11,9},{12,... | collective-permute-start | bytes 393224 | tf_op jit(solution)/shard_map/ppermute | solution.py:14
  69.5 32.5 %collective-permute-start.12 = (bf16[2,256,128]{2,0,1:T(2,128)(2,1)}, bf16[2,256,128]{2,0,1:T(2,128)(2,1)}, u32[]{:S(2)}, u32[]{:S(2)}) collective-permute-start(bf16[2,256,128]{2,0,1:T(2,128)(2,1)} %get-tuple-element.15), channel_id=1, source_target_pairs={{1,0},{2,1},{3,2},{4,3},{5,4},{6,5},{7,6},{8,7},{9,8},{10,9},{11,1... | collective-permute-start | bytes 393224 | tf_op jit(solution)/shard_map/ppermute | solution.py:14
  116.3 19.5 %copy-start.11 = (f32[16,256,128]{2,0,1:T(8,128)}, f32[16,256,128]{2,0,1:T(8,128)S(1)}, u32[]{:S(2)}) copy-start(f32[16,256,128]{2,0,1:T(8,128)S(1)} %fusion.2) | copy-start | bytes 6291460
  116.3 18.2 %copy-start.8 = (bf16[8,256,128]{2,1,0:T(8,128)(2,1)S(1)}, bf16[8,256,128]{2,1,0:T(8,128)(2,1)}, u32[]{:S(2)}) copy-start(bf16[8,256,128]{2,1,0:T(8,128)(2,1)} %copy.14) | copy-start | bytes 1572868
  117.5 56.3 %collective-permute-start.19 = (bf16[2,256,128]{2,0,1:T(2,128)(2,1)}, bf16[2,256,128]{2,0,1:T(2,128)(2,1)}, u32[]{:S(2)}, u32[]{:S(2)}) collective-permute-start(bf16[2,256,128]{2,0,1:T(2,128)(2,1)} %get-tuple-element.12), channel_id=1, source_target_pairs={{0,2},{1,3},{2,4},{3,5},{4,6},{5,7},{6,8},{7,9},{8,10},{9,11},{10,... | collective-permute-start | bytes 393224 | tf_op jit(solution)/shard_map/ppermute | solution.py:14
  124.1 12.7 %collective-permute-start.4 = (bf16[2,256,128]{2,0,1:T(2,128)(2,1)S(1)}, bf16[2,256,128]{2,0,1:T(2,128)(2,1)}, u32[]{:S(2)}, u32[]{:S(2)}) collective-permute-start(bf16[2,256,128]{2,0,1:T(2,128)(2,1)S(1)} %copy.16), channel_id=1, source_target_pairs={{0,1},{1,2},{2,3},{3,4},{4,5},{5,6},{6,7},{7,8},{8,9},{9,10},{10,1... | collective-permute-start | bytes 393224 | tf_op jit(solution)/shard_map/ppermute | solution.py:14
  126.2 11.9 %collective-permute-start.5 = (bf16[2,256,128]{2,0,1:T(2,128)(2,1)S(1)}, bf16[2,256,128]{2,0,1:T(2,128)(2,1)}, u32[]{:S(2)}, u32[]{:S(2)}) collective-permute-start(bf16[2,256,128]{2,0,1:T(2,128)(2,1)S(1)} %copy.18), channel_id=1, source_target_pairs={{1,0},{2,1},{3,2},{4,3},{5,4},{6,5},{7,6},{8,7},{9,8},{10,9},{11,1... | collective-permute-start | bytes 393224 | tf_op jit(solution)/shard_map/ppermute | solution.py:14
  128.0 13.6 %collective-permute-start.6 = (bf16[2,256,128]{2,0,1:T(2,128)(2,1)S(1)}, bf16[2,256,128]{2,0,1:T(2,128)(2,1)S(1)}, u32[]{:S(2)}, u32[]{:S(2)}) collective-permute-start(bf16[2,256,128]{2,0,1:T(2,128)(2,1)S(1)} %copy.20), channel_id=1, source_target_pairs={{0,2},{1,3},{2,4},{3,5},{4,6},{5,7},{6,8},{7,9},{8,10},{9,11},{10,... | collective-permute-start | bytes 393224 | tf_op jit(solution)/shard_map/ppermute | solution.py:14
  133.3 9.7 %collective-permute-start.7 = (bf16[2,256,128]{2,0,1:T(2,128)(2,1)S(1)}, bf16[2,256,128]{2,0,1:T(2,128)(2,1)S(1)}, u32[]{:S(2)}, u32[]{:S(2)}) collective-permute-start(bf16[2,256,128]{2,0,1:T(2,128)(2,1)S(1)} %copy.22), channel_id=1, source_target_pairs={{2,0},{3,1},{4,2},{5,3},{6,4},{7,5},{8,6},{9,7},{10,8},{11,9},{12,... | collective-permute-start | bytes 393224 | tf_op jit(solution)/shard_map/ppermute | solution.py:14
  136.8 38.4 %collective-permute-start.18 = (bf16[2,256,128]{2,0,1:T(2,128)(2,1)}, bf16[2,256,128]{2,0,1:T(2,128)(2,1)}, u32[]{:S(2)}, u32[]{:S(2)}) collective-permute-start(bf16[2,256,128]{2,0,1:T(2,128)(2,1)} %get-tuple-element.13), channel_id=1, source_target_pairs={{2,0},{3,1},{4,2},{5,3},{6,4},{7,5},{8,6},{9,7},{10,8},{11,9},{12,... | collective-permute-start | bytes 393224 | tf_op jit(solution)/shard_map/ppermute | solution.py:14
  138.1 38.4 %collective-permute-start.17 = (bf16[2,256,128]{2,0,1:T(2,128)(2,1)}, bf16[2,256,128]{2,0,1:T(2,128)(2,1)}, u32[]{:S(2)}, u32[]{:S(2)}) collective-permute-start(bf16[2,256,128]{2,0,1:T(2,128)(2,1)} %get-tuple-element.14), channel_id=1, source_target_pairs={{0,1},{1,2},{2,3},{3,4},{4,5},{5,6},{6,7},{7,8},{8,9},{9,10},{10,1... | collective-permute-start | bytes 393224 | tf_op jit(solution)/shard_map/ppermute | solution.py:14
  141.6 36.2 %collective-permute-start.16 = (bf16[2,256,128]{2,0,1:T(2,128)(2,1)}, bf16[2,256,128]{2,0,1:T(2,128)(2,1)}, u32[]{:S(2)}, u32[]{:S(2)}) collective-permute-start(bf16[2,256,128]{2,0,1:T(2,128)(2,1)} %get-tuple-element.11), channel_id=1, source_target_pairs={{1,0},{2,1},{3,2},{4,3},{5,4},{6,5},{7,6},{8,7},{9,8},{10,9},{11,1... | collective-permute-start | bytes 393224 | tf_op jit(solution)/shard_map/ppermute | solution.py:14
  190.4 18.8 %copy-start.23 = (bf16[2,256,128]{2,1,0:T(8,128)(2,1)S(1)}, bf16[2,256,128]{2,1,0:T(8,128)(2,1)}, u32[]{:S(2)}) copy-start(bf16[2,256,128]{2,1,0:T(8,128)(2,1)} %gather_fusion.12) | copy-start | bytes 393220
  192.3 25.3 %copy-start.22 = (bf16[2,256,128]{2,1,0:T(8,128)(2,1)S(1)}, bf16[2,256,128]{2,1,0:T(8,128)(2,1)}, u32[]{:S(2)}) copy-start(bf16[2,256,128]{2,1,0:T(8,128)(2,1)} %gather_fusion.11) | copy-start | bytes 393220
  192.3 25.4 %copy-start.7 = (bf16[8,256,128]{2,1,0:T(8,128)(2,1)S(1)}, bf16[8,256,128]{2,1,0:T(8,128)(2,1)}, u32[]{:S(2)}) copy-start(bf16[8,256,128]{2,1,0:T(8,128)(2,1)} %copy.25) | copy-start | bytes 1572868
  192.3 25.4 %copy-start.20 = (f32[2048,128]{1,0:T(8,128)S(1)}, f32[2048,128]{1,0:T(8,128)}, u32[]{:S(2)}) copy-start(f32[2048,128]{1,0:T(8,128)} %convolution_add_fusion.2) | copy-start | bytes 3145732
  192.7 26.8 %collective-permute-start.22 = (bf16[2,256,128]{2,0,1:T(2,128)(2,1)S(1)}, bf16[2,256,128]{2,0,1:T(2,128)(2,1)S(1)}, u32[]{:S(2)}, u32[]{:S(2)}) collective-permute-start(bf16[2,256,128]{2,0,1:T(2,128)(2,1)S(1)} %get-tuple-element.9), channel_id=1, source_target_pairs={{2,0},{3,1},{4,2},{5,3},{6,4},{7,5},{8,6},{9,7},{10,8},{11,9},{12,... | collective-permute-start | bytes 393224 | tf_op jit(solution)/shard_map/ppermute | solution.py:14
  194.1 27.2 %collective-permute-start.21 = (bf16[2,256,128]{2,0,1:T(2,128)(2,1)S(1)}, bf16[2,256,128]{2,0,1:T(2,128)(2,1)S(1)}, u32[]{:S(2)}, u32[]{:S(2)}) collective-permute-start(bf16[2,256,128]{2,0,1:T(2,128)(2,1)S(1)} %get-tuple-element.10), channel_id=1, source_target_pairs={{0,1},{1,2},{2,3},{3,4},{4,5},{5,6},{6,7},{7,8},{8,9},{9,10},{10,1... | collective-permute-start | bytes 393224 | tf_op jit(solution)/shard_map/ppermute | solution.py:14
  200.2 24.6 %collective-permute-start.23 = (bf16[2,256,128]{2,0,1:T(2,128)(2,1)S(1)}, bf16[2,256,128]{2,0,1:T(2,128)(2,1)S(1)}, u32[]{:S(2)}, u32[]{:S(2)}) collective-permute-start(bf16[2,256,128]{2,0,1:T(2,128)(2,1)S(1)} %get-tuple-element.8), channel_id=1, source_target_pairs={{0,2},{1,3},{2,4},{3,5},{4,6},{5,7},{6,8},{7,9},{8,10},{9,11},{10,... | collective-permute-start | bytes 393224 | tf_op jit(solution)/shard_map/ppermute | solution.py:14
  207.8 18.9 %collective-permute-start.20 = (bf16[2,256,128]{2,0,1:T(2,128)(2,1)S(1)}, bf16[2,256,128]{2,0,1:T(2,128)(2,1)S(1)}, u32[]{:S(2)}, u32[]{:S(2)}) collective-permute-start(bf16[2,256,128]{2,0,1:T(2,128)(2,1)S(1)} %get-tuple-element.7), channel_id=1, source_target_pairs={{1,0},{2,1},{3,2},{4,3},{5,4},{6,5},{7,6},{8,7},{9,8},{10,9},{11,1... | collective-permute-start | bytes 393224 | tf_op jit(solution)/shard_map/ppermute | solution.py:14
  209.3 19.1 %collective-permute-start.10 = (bf16[2,256,128]{2,0,1:T(2,128)(2,1)S(1)}, bf16[2,256,128]{2,0,1:T(2,128)(2,1)}, u32[]{:S(2)}, u32[]{:S(2)}) collective-permute-start(bf16[2,256,128]{2,0,1:T(2,128)(2,1)S(1)} %copy.31), channel_id=1, source_target_pairs={{0,2},{1,3},{2,4},{3,5},{4,6},{5,7},{6,8},{7,9},{8,10},{9,11},{10,... | collective-permute-start | bytes 393224 | tf_op jit(solution)/shard_map/ppermute | solution.py:14
  219.4 9.0 %collective-permute-start.11 = (bf16[2,256,128]{2,0,1:T(2,128)(2,1)S(1)}, bf16[2,256,128]{2,0,1:T(2,128)(2,1)S(1)}, u32[]{:S(2)}, u32[]{:S(2)}) collective-permute-start(bf16[2,256,128]{2,0,1:T(2,128)(2,1)S(1)} %copy.33), channel_id=1, source_target_pairs={{2,0},{3,1},{4,2},{5,3},{6,4},{7,5},{8,6},{9,7},{10,8},{11,9},{12,... | collective-permute-start | bytes 393224 | tf_op jit(solution)/shard_map/ppermute | solution.py:14
  221.3 7.1 %collective-permute-start.8 = (bf16[2,256,128]{2,0,1:T(2,128)(2,1)S(1)}, bf16[2,256,128]{2,0,1:T(2,128)(2,1)}, u32[]{:S(2)}, u32[]{:S(2)}) collective-permute-start(bf16[2,256,128]{2,0,1:T(2,128)(2,1)S(1)} %copy.27), channel_id=1, source_target_pairs={{0,1},{1,2},{2,3},{3,4},{4,5},{5,6},{6,7},{7,8},{8,9},{9,10},{10,1... | collective-permute-start | bytes 393224 | tf_op jit(solution)/shard_map/ppermute | solution.py:14
  224.8 6.7 %collective-permute-start.9 = (bf16[2,256,128]{2,0,1:T(2,128)(2,1)S(1)}, bf16[2,256,128]{2,0,1:T(2,128)(2,1)}, u32[]{:S(2)}, u32[]{:S(2)}) collective-permute-start(bf16[2,256,128]{2,0,1:T(2,128)(2,1)S(1)} %copy.29), channel_id=1, source_target_pairs={{1,0},{2,1},{3,2},{4,3},{5,4},{6,5},{7,6},{8,7},{9,8},{10,9},{11,1... | collective-permute-start | bytes 393224 | tf_op jit(solution)/shard_map/ppermute | solution.py:14
  (32 other events, 149.7 us)
Sparse Core Ops, SparseCore 0:
  254.0 289.9 all-reduce.1
where the time goes:
time: 556 us; the launch traced here: 553 us
  waiting for transfers between devices  295 us (53%)
  local copies, waits for them, and re-layouts  95.7 us (17%)
  starting transfers between devices  77 us (14%)
  matrix products  64.3 us (12%)
  between operations  15.5 us (3%)
    psum x1, waiting for transfers between devices, per_device(): stacked = lax.psum(jnp.stack(grad_terms), ('view', 'sky'))  288 us
    ppermute x24, starting transfers between devices, passed_along(): return lax.ppermute(array, axis, pairs)  77 us
    gather x20, local copies, waits for them, and re-layouts, forward_pieces(): return [blocks[chosen[number]] for number in range(4)]  26.8 us
    dot_general x6, matrix products, tile_products(): jnp.einsum(contraction, tile_set, picked, preferred_element_type=jnp.floa...  21 us
    gather x6, local copies, waits for them, and re-layouts, tile_products(): picked = values[target] if transposed else values[source]  19.1 us
    concatenate x5, local copies, waits for them, and re-layouts, forward_finish(): extended = jnp.concatenate([blocks] + arrived, axis=0)  18.5 us
    dot_general x6, local copies, waits for them, and re-layouts, tile_products(): jnp.einsum(contraction, tile_set, picked, preferred_element_type=jnp.floa...  16.5 us
    dot_general x12, matrix products, transposed_finish(): combined = combined + jnp.einsum('bj,jqc->bqc', routing, arrived[number])  15 us
  transfers between devices with their start and end apart: 25, of which 3 were waited for; matrix products, arithmetic and copies ran while one was open for 17% of the time, Pallas kernels for 0%

commit v1 on v0

v1 whole, which is shorter than its diff:
```python
import math

import jax
import jax.numpy as jnp
from jax import lax
from jax.experimental import pallas as pl
from jax.experimental.pallas import tpu as pltpu
from jax.sharding import PartitionSpec as P

OFFSETS = (1, -1, 2, -2)
START_ORDER = (2, 3, 0, 1)
F32 = jnp.float32
BF16 = jnp.bfloat16
ANY = pl.BlockSpec(memory_space=pl.ANY)
VMEM = pl.BlockSpec(memory_space=pltpu.VMEM)
SMEM = pl.BlockSpec(memory_space=pltpu.SMEM)
NB, BLK, C, MAXT, NSEND = 8, 256, 128, 24, 2
NEXT = NB + 4 * NSEND


def mm(a, b):
    return jnp.dot(a, b, preferred_element_type=F32)


def call(kernel, name, outs, out_specs, in_specs, scratch, flops, args):
    size = sum(math.prod(o.shape) * o.dtype.itemsize for o in outs)
    size += sum(math.prod(a.shape) * a.dtype.itemsize for a in args)
    return pl.pallas_call(
        kernel,
        name=name,
        out_shape=outs,
        in_specs=in_specs,
        out_specs=out_specs,
        scratch_shapes=scratch,
        cost_estimate=pl.CostEstimate(flops=flops, bytes_accessed=size, transcendentals=0),
        compiler_params=pltpu.CompilerParams(vmem_limit_bytes=24 * 1024 * 1024),
    )(*args)


def start_tiles(tiles, tile_buf, tile_sem):
    copies = [pltpu.make_async_copy(tiles.at[t], tile_buf.at[t], tile_sem.at[t]) for t in range(MAXT)]
    for copy in copies:
        copy.start()
    return copies


PIECE = jax.ShapeDtypeStruct((NSEND, BLK, C), BF16)
PIECE_T = jax.ShapeDtypeStruct((NSEND, C, BLK), BF16)
BLOCKS = jax.ShapeDtypeStruct((NB, BLK, C), BF16)
BLOCKS_T = jax.ShapeDtypeStruct((NB, C, BLK), BF16)
OWN_T = jax.ShapeDtypeStruct((NB, C, BLK), F32)
TILE_SCRATCH = [pltpu.VMEM((MAXT, BLK, BLK), BF16), pltpu.SemaphoreType.DMA((MAXT,))]
STEP_FLOPS = 2 * MAXT * BLK * BLK * C


def pick_kernel(send, blocks, *rest):
    outs, sem = rest[:4], rest[4]
    copies = []
    for i in range(4):
        for j in range(NSEND):
            copies.append(
                pltpu.make_async_copy(blocks.at[send[0, i, j]], outs[i].at[j], sem.at[i * NSEND + j])
            )
    for copy in copies:
        copy.start()
    for copy in copies:
        copy.wait()


def pick(send, blocks):
    return call(
        pick_kernel, "pick", [PIECE] * 4, [ANY] * 4, [SMEM, ANY],
        [pltpu.SemaphoreType.DMA((4 * NSEND,))], 0, (send, blocks),
    )


def forward_kernel(first, last, *refs):
    refs = list(refs)
    take = lambda n: [refs.pop(0) for _ in range(n)]
    target, source, count, send, tiles, blocks = take(6)
    arrived = take(4)
    before = None if first else take(1)[0]
    if last:
        base, filters = take(2)
        (out,) = take(1)
    else:
        (out,) = take(1)
        pieces = take(4)
    tile_buf, tile_sem, ext, ext_sem, acc = take(5)
    tile_copies = start_tiles(tiles, tile_buf, tile_sem)
    ext_copies = [pltpu.make_async_copy(blocks, ext.at[pl.ds(0, NB)], ext_sem.at[0])]
    for i in range(4):
        ext_copies.append(
            pltpu.make_async_copy(
                arrived[i], ext.at[pl.ds(NB + i * NSEND, NSEND)], ext_sem.at[1 + i]
            )
        )
    for copy in ext_copies:
        copy.start()
    acc[...] = jnp.zeros_like(acc)
    for copy in ext_copies:
        copy.wait()
    for t in range(MAXT):
        tile_copies[t].wait()
        where = jnp.where(t < count[0], target[0, t], NB)
        acc[where] += mm(tile_buf[t], ext[source[0, t]])
    for b in range(NB):
        value = acc[b]
        if not first:
            value = 2.0 * value - before[b].astype(F32)
        value = value.astype(BF16)
        if last:
            result = mm(base[b], filters[0]) + mm(before[b], filters[1])
            result = result + mm(ext[b], filters[2]) + mm(value, filters[3])
            out[b] = result.astype(BF16)
        else:
            out[b] = value
    if not last:
        for i in range(4):
            for j in range(NSEND):
                pieces[i][j] = out[send[0, i, j]]


def forward(tables, send, tiles, blocks, arrived, before=None, base=None, filters=None):
    first, last = before is None, base is not None
    args = [*tables, send, tiles, blocks, *arrived]
    specs = [SMEM] * 4 + [ANY] * 6
    if not first:
        args.append(before)
        specs.append(VMEM)
    if last:
        args += [base, filters]
        specs += [VMEM, VMEM]
        outs, out_specs = [BLOCKS], [VMEM]
    else:
        outs, out_specs = [BLOCKS] + [PIECE] * 4, [VMEM] * 5
    scratch = TILE_SCRATCH + [
        pltpu.VMEM((NEXT, BLK, C), BF16),
        pltpu.SemaphoreType.DMA((5,)),
        pltpu.VMEM((NB + 1, BLK, C), F32),
    ]
    kernel = lambda *refs: forward_kernel(first, last, *refs)
    return call(kernel, "forward", outs, out_specs, specs, scratch, STEP_FLOPS, args)


def push_terms(target, source, count, tile_copies, tile_buf, held, acc, own, pieces):
    acc[...] = jnp.zeros_like(acc)
    for t in range(MAXT):
        tile_copies[t].wait()
        where = jnp.where(t < count[0], source[0, t], NEXT)
        acc[where] += mm(held[target[0, t]], tile_buf[t])
    for i in range(4):
        for j in range(NSEND):
            pieces[i][j] = acc[NB + i * NSEND + j].astype(BF16)
    own[...] = acc[0:NB]


def adjoint_start_kernel(target, source, count, tiles, upstream, held, own, *rest):
    pieces = rest[:4]
    tile_buf, tile_sem, acc = rest[4:]
    tile_copies = start_tiles(tiles, tile_buf, tile_sem)
    for b in range(NB):
        held[b] = upstream[b].astype(F32).T.astype(BF16)
    push_terms(target, source, count, tile_copies, tile_buf, held, acc, own, pieces)


ACC_T = pltpu.VMEM((NEXT + 1, C, BLK), F32)


def adjoint_start(tables, tiles, upstream):
    return call(
        adjoint_start_kernel, "adjoint_start", [BLOCKS_T, OWN_T] + [PIECE_T] * 4, [VMEM] * 6,
        [SMEM] * 3 + [ANY, VMEM], TILE_SCRATCH + [ACC_T], STEP_FLOPS, (*tables, tiles, upstream),
    )


def gather_terms(send, own, arrived, total):
    total[...] = own[...]
    for i in range(4):
        for j in range(NSEND):
            total[send[0, i, j]] += arrived[i][j].astype(F32)


def adjoint_kernel(first, *refs):
    refs = list(refs)
    take = lambda n: [refs.pop(0) for _ in range(n)]
    target, source, count, send, tiles, own_in = take(6)
    arrived = take(4)
    before = None if first else take(1)[0]
    held, own = take(2)
    pieces = take(4)
    tile_buf, tile_sem, acc = take(3)
    tile_copies = start_tiles(tiles, tile_buf, tile_sem)
    total = acc.at[pl.ds(0, NB)]
    gather_terms(send, own_in, arrived, total)
    for b in range(NB):
        value = total[b]
        if not first:
            value = 2.0 * value - before[b].astype(F32)
        held[b] = value.astype(BF16)
    push_terms(target, source, count, tile_copies, tile_buf, held, acc, own, pieces)


def adjoint(tables, send, tiles, own, arrived, before=None):
    first = before is None
    args = [*tables, send, tiles, own, *arrived] + ([] if first else [before])
    specs = [SMEM] * 4 + [ANY] + [VMEM] * (5 if first else 6)
    kernel = lambda *refs: adjoint_kernel(first, *refs)
    return call(
        kernel, "adjoint", [BLOCKS_T, OWN_T] + [PIECE_T] * 4, [VMEM] * 6, specs,
        TILE_SCRATCH + [ACC_T], STEP_FLOPS, args,
    )


def adjoint_end_kernel(send, own_in, a0, a1, a2, a3, u0, u1, u2, filters, out, total):
    gather_terms(send, own_in, (a0, a1, a2, a3), total)
    for b in range(NB):
        u3 = (2.0 * total[b] - u1[b].astype(F32)).astype(BF16)
        grad = mm(filters[0], u0[b]) + mm(filters[1], u1[b])
        grad = grad + mm(filters[2], u2[b]) + mm(filters[3], u3)
        out[b] = grad.T.astype(BF16)


def adjoint_end(send, own, arrived, us, filters):
    return call(
        adjoint_end_kernel, "adjoint_end", [BLOCKS], [VMEM], [SMEM] + [VMEM] * 9,
        [pltpu.VMEM((NB, C, BLK), F32)], 8 * NB * BLK * C * C, (send, own, *arrived, *us, filters),
    )[0]


def grads_kernel(base, one, two, u0, u1, out):
    g0 = jnp.zeros((C, C), F32)
    g1, g2, g3 = g0, g0, g0
    for b in range(NB):
        g0 += mm(u0[b], base[b])
        g1 += mm(u0[b], one[b])
        g2 += mm(u0[b], two[b])
        g3 += mm(u1[b], two[b])
    out[0] = g0.T
    out[1] = g1.T
    out[2] = g2.T
    out[3] = (2.0 * g3 - g1).T


def grads(base, one, two, u0, u1):
    return call(
        grads_kernel, "grads", [jax.ShapeDtypeStruct((4, C, C), F32)], [VMEM], [VMEM] * 5, [],
        8 * NB * BLK * C * C, (base, one, two, u0, u1),
    )[0]


def passed_along(array, by):
    size = lax.axis_size("sky")
    return lax.ppermute(array, "sky", [(i, i + by) for i in range(size) if 0 <= i + by < size])


def spread(pieces, sign):
    got = [None] * 4
    for i in START_ORDER:
        got[i] = passed_along(pieces[i], sign * OFFSETS[i])
    return got


def total_over_devices(local):
    axes = ("view", "sky")
    count = lax.axis_size("view") * lax.axis_size("sky")
    rows = local.shape[0] * local.shape[1] // count
    parts = lax.all_to_all(local.reshape(count, rows, C), axes, 0, 0, tiled=True)
    part = jnp.sum(parts, axis=0)
    whole = lax.all_to_all(jnp.broadcast_to(part[None], parts.shape), axes, 0, 0, tiled=True)
    return whole.reshape(local.shape)


def per_device(
    pixels, cotangent, filters, lap_tiles, tile_target, tile_source, tile_count, send_blocks
):
    base = pixels.reshape(NB, BLK, C)
    upstream = cotangent.reshape(NB, BLK, C)
    tiles = lap_tiles.reshape(MAXT, BLK, BLK)
    tables = (tile_target, tile_source, tile_count)
    send = send_blocks

    f1 = spread(pick(send, base), 1)
    u0, own, *terms = adjoint_start(tables, tiles, upstream)
    b1 = spread(terms, -1)
    one, *pieces = forward(tables, send, tiles, base, f1)
    f2 = spread(pieces, 1)
    u1, own, *terms = adjoint(tables, send, tiles, own, b1)
    b2 = spread(terms, -1)
    two, *pieces = forward(tables, send, tiles, one, f2, before=base)
    local = grads(base, one, two, u0, u1)
    summed = total_over_devices(local)
    f3 = spread(pieces, 1)
    u2, own, *terms = adjoint(tables, send, tiles, own, b2, before=u0)
    b3 = spread(terms, -1)
    (outputs,) = forward(tables, send, tiles, two, f3, before=one, base=base, filters=filters)
    pixel_grad = adjoint_end(send, own, b3, (u0, u1, u2), filters)
    scale = 1.0 / math.sqrt(lax.axis_size("view") * lax.axis_size("sky") * NB * BLK)
    return (outputs.reshape(pixels.shape), pixel_grad.reshape(pixels.shape), summed * scale)


def solution(mesh):
    return jax.shard_map(
        per_device,
        mesh=mesh,
        in_specs=(
            P("view", "sky", None),
            P("view", "sky", None),
            P(),
            P("sky", None, None, None),
            P("sky", None),
            P("sky", None),
            P("sky"),
            P("sky", None, None),
        ),
        out_specs=(P("view", "sky", None), P("view", "sky", None), P()),
        check_vma=False,
    )
```

time: 556 us -> 248 us (0.45)
  the two profiles are of different devices: /device:TPU:1 before, /device:TPU:118 now
where the time goes in v1:
time: 248 us; the launch traced here: 247 us
  starting transfers between devices  130 us (52%)
  Pallas kernels  67.1 us (27%)
  blocking collectives  22.6 us (9%)
  waiting for transfers between devices  11.7 us (5%)
  local copies, waits for them, and re-layouts  10.2 us (4%)
  other arithmetic  3.05 us (1%)
    ppermute x24, starting transfers between devices, passed_along(): lax.ppermute(array, 'sky', [(i, i + by) for i in range(size) if 0 <= i +...  117 us
    pallas_call x9, Pallas kernels, call(): pl.pallas_call(kernel, name=name, out_shape=outs, in_specs=in_specs, out_...  67.1 us
    all_to_all x1, blocking collectives, total_over_devices(): lax.all_to_all(local.reshape(count, rows, C), axes, 0, 0, tiled=True)  22.6 us
    all_to_all x1, starting transfers between devices, total_over_devices(): lax.all_to_all(jnp.broadcast_to(part[None], parts.shape), axes, 0, 0, til...  13.7 us
    ppermute x24, waiting for transfers between devices, passed_along(): lax.ppermute(array, 'sky', [(i, i + by) for i in range(size) if 0 <= i +...  11.7 us
    unnamed x61, local copies, waits for them, and re-layouts  9.42 us
  transfers between devices with their start and end apart: 25, of which 3 were waited for; matrix products, arithmetic and copies ran while one was open for 0% of the time, Pallas kernels for 22%

profile of v1, /device:TPU:118, one launch (start us, length us, event | category | flops | bytes accessed | tf_op | source)
XLA Modules:
  0.0 247.0 jit_solution(16692636778342354306)
XLA Ops:
  3.8 3.2 %collective-permute-start = (bf16[2,256,128]{2,1,0:T(8,128)(2,1)S(1)}, bf16[2,256,128]{2,1,0:T(8,128)(2,1)S(1)}, u32[]{:S(2)}, u32[]{:S(2)}) collective-permute-start(bf16[2,256,128]{2,1,0:T(8,128)(2,1)S(1)} %get-tuple-element.35), channel_id=1, source_target_pairs={{0,1},{1,2},{2,3},{3,4},{4,5},{5,6},{6,7},{7,8},{8,9},{9,10},{10,1... | collective-permute-start | bytes 393224 | tf_op jit(solution)/shard_map/ppermute | solution.py:254
  7.0 2.7 %collective-permute-start.1 = (bf16[2,256,128]{2,1,0:T(8,128)(2,1)S(1)}, bf16[2,256,128]{2,1,0:T(8,128)(2,1)S(1)}, u32[]{:S(2)}, u32[]{:S(2)}) collective-permute-start(bf16[2,256,128]{2,1,0:T(8,128)(2,1)S(1)} %get-tuple-element.36), channel_id=1, source_target_pairs={{1,0},{2,1},{3,2},{4,3},{5,4},{6,5},{7,6},{8,7},{9,8},{10,9},{11,1... | collective-permute-start | bytes 393224 | tf_op jit(solution)/shard_map/ppermute | solution.py:254
  9.6 10.2 %collective-permute-start.2 = (bf16[2,256,128]{2,1,0:T(8,128)(2,1)S(1)}, bf16[2,256,128]{2,1,0:T(8,128)(2,1)S(1)}, u32[]{:S(2)}, u32[]{:S(2)}) collective-permute-start(bf16[2,256,128]{2,1,0:T(8,128)(2,1)S(1)} %get-tuple-element.37), channel_id=1, source_target_pairs={{0,2},{1,3},{2,4},{3,5},{4,6},{5,7},{6,8},{7,9},{8,10},{9,11},{10,... | collective-permute-start | bytes 393224 | tf_op jit(solution)/shard_map/ppermute | solution.py:254
  19.8 1.9 collective-permute-start.3
  26.6 9.6 %adjoint_start.1 = (bf16[8,128,256]{2,1,0:T(8,128)(2,1)S(1)}, f32[8,128,256]{2,1,0:T(8,128)S(1)}, bf16[2,128,256]{2,1,0:T(8,128)(2,1)S(1)}, bf16[2,128,256]{2,1,...) custom-call(s32[1,24]{1,0:T(1,128)S(1)} %copy-done.18, s32[1,24]{1,0:T(1,128)S(1)} %copy-done.20, ...), custom_call_target="tpu_custom_call" | custom-call | flops 402653184 | bytes 5767364 | tf_op jit(solution)/shard_map/adjoint_start/pallas_call | solution.py:28
  36.3 1.9 collective-permute-start.12
  38.2 3.9 %collective-permute-start.13 = (bf16[2,128,256]{2,1,0:T(8,128)(2,1)S(1)}, bf16[2,128,256]{2,1,0:T(8,128)(2,1)S(1)}, u32[]{:S(2)}, u32[]{:S(2)}) collective-permute-start(bf16[2,128,256]{2,1,0:T(8,128)(2,1)S(1)} %get-tuple-element.51), channel_id=1, source_target_pairs={{0,1},{1,2},{2,3},{3,4},{4,5},{5,6},{6,7},{7,8},{8,9},{9,10},{10,1... | collective-permute-start | bytes 393224 | tf_op jit(solution)/shard_map/ppermute | solution.py:254
  42.2 1.9 collective-permute-start.14
  44.1 9.6 %collective-permute-start.15 = (bf16[2,128,256]{2,1,0:T(8,128)(2,1)S(1)}, bf16[2,128,256]{2,1,0:T(8,128)(2,1)S(1)}, u32[]{:S(2)}, u32[]{:S(2)}) collective-permute-start(bf16[2,128,256]{2,1,0:T(8,128)(2,1)S(1)} %get-tuple-element.53), channel_id=1, source_target_pairs={{0,2},{1,3},{2,4},{3,5},{4,6},{5,7},{6,8},{7,9},{8,10},{9,11},{10,... | collective-permute-start | bytes 393224 | tf_op jit(solution)/shard_map/ppermute | solution.py:254
  53.8 10.7 %forward.3 = (bf16[8,256,128]{2,1,0:T(8,128)(2,1)S(1)}, bf16[2,256,128]{2,1,0:T(8,128)(2,1)S(1)}, bf16[2,256,128]{2,1,0:T(8,128)(2,1)S(1)}, bf16[2,256,128]{2,1,0:T(8,128)(2,1)S(1)}, bf16[2,256,128]{2,1,0:T(8,128)(2,1)S(1)}) custom-call(s32[1,24]{1,0:T(1,128)S(1)} %copy-done.18, s32[1,24]{1,0:T(1,128)S(1)} %copy-done.20, s32[1]{0:T(128)S(6)} %copy.18.refs_2_.count, ...), custom_call_target="tpu_custom_call" | custom-call | flops 402653184 | bytes 5243108 | tf_op jit(solution)/shard_map/forward/pallas_call | solution.py:28
  64.5 8.9 %collective-permute-start.4 = (bf16[2,256,128]{2,1,0:T(8,128)(2,1)S(1)}, bf16[2,256,128]{2,1,0:T(8,128)(2,1)S(1)}, u32[]{:S(2)}, u32[]{:S(2)}) collective-permute-start(bf16[2,256,128]{2,1,0:T(8,128)(2,1)S(1)} %get-tuple-element.40), channel_id=1, source_target_pairs={{0,1},{1,2},{2,3},{3,4},{4,5},{5,6},{6,7},{7,8},{8,9},{9,10},{10,1... | collective-permute-start | bytes 393224 | tf_op jit(solution)/shard_map/ppermute | solution.py:254
  73.5 1.9 collective-permute-start.5
  75.4 8.2 %collective-permute-start.6 = (bf16[2,256,128]{2,1,0:T(8,128)(2,1)S(1)}, bf16[2,256,128]{2,1,0:T(8,128)(2,1)S(1)}, u32[]{:S(2)}, u32[]{:S(2)}) collective-permute-start(bf16[2,256,128]{2,1,0:T(8,128)(2,1)S(1)} %get-tuple-element.42), channel_id=1, source_target_pairs={{0,2},{1,3},{2,4},{3,5},{4,6},{5,7},{6,8},{7,9},{8,10},{9,11},{10,... | collective-permute-start | bytes 393224 | tf_op jit(solution)/shard_map/ppermute | solution.py:254
  83.6 1.9 collective-permute-start.7
  85.6 9.7 %adjoint.2 = (bf16[8,128,256]{2,1,0:T(8,128)(2,1)S(1)}, f32[8,128,256]{2,1,0:T(8,128)S(1)}, bf16[2,128,256]{2,1,0:T(8,128)(2,1)S(1)}, bf16[2,128,256]{2,1,0:T(8,...) custom-call(s32[1,24]{1,0:T(1,128)S(1)} %copy-done.18, s32[1,24]{1,0:T(1,128)S(1)} %copy-done.20, ...), custom_call_target="tpu_custom_call" | custom-call | flops 402653184 | bytes 6815972 | tf_op jit(solution)/shard_map/adjoint/pallas_call | solution.py:28
  96.4 10.8 %forward.4 = (bf16[8,256,128]{2,1,0:T(8,128)(2,1)S(1)}, bf16[2,256,128]{2,1,0:T(8,128)(2,1)S(1)}, bf16[2,256,128]{2,1,0:T(8,128)(2,1)S(1)}, bf16[2,256,128]{2,1,0:T(8,128)(2,1)S(1)}, bf16[2,256,128]{2,1,0:T(8,128)(2,1)S(1)}) custom-call(s32[1,24]{1,0:T(1,128)S(1)} %copy-done.18, s32[1,24]{1,0:T(1,128)S(1)} %copy-done.21, s32[1]{0:T(128)S(6)} %copy.18.refs_2_.count, ...), custom_call_target="tpu_custom_call" | custom-call | flops 402653184 | bytes 5767396 | tf_op jit(solution)/shard_map/forward/pallas_call | solution.py:28
  108.1 22.6 %all_to_all.10 = f32[256,2,128]{2,1,0:T(2,128)} all-to-all(f32[256,2,128]{2,1,0:T(2,128)S(1)} %bitcast.18), channel_id=1, replica_groups=mesh['view'=2,'sky'=128] {'view','sky'}, dimensions={0} | all-to-all | bytes 524288 | tf_op jit(solution)/shard_map/all_to_all | solution.py:268
  132.7 13.7 %all-to-all-start.1 = ((f32[256,2,128]{2,1,0:T(2,128)}), f32[256,2,128]{2,1,0:T(2,128)}, u32[]{:S(2)}, u32[]{:S(2)}) async-start(f32[256,2,128]{2,1,0:T(2,128)} %broadcast_in_dim.2), calls=%async_computation.1 | async-start | bytes 524288 | tf_op jit(solution)/shard_map/all_to_all | solution.py:270
  146.4 2.4 collective-permute-start.16
  148.8 3.4 %collective-permute-start.17 = (bf16[2,128,256]{2,1,0:T(8,128)(2,1)}, bf16[2,128,256]{2,1,0:T(8,128)(2,1)S(1)}, u32[]{:S(2)}, u32[]{:S(2)}) collective-permute-start(bf16[2,128,256]{2,1,0:T(8,128)(2,1)} %copy-done.28), channel_id=1, source_target_pairs={{0,1},{1,2},{2,3},{3,4},{4,5},{5,6},{6,7},{7,8},{8,9},{9,10},{10,1... | collective-permute-start | bytes 393224 | tf_op jit(solution)/shard_map/ppermute | solution.py:254
  152.2 3.5 %collective-permute-start.18 = (bf16[2,128,256]{2,1,0:T(8,128)(2,1)}, bf16[2,128,256]{2,1,0:T(8,128)(2,1)S(1)}, u32[]{:S(2)}, u32[]{:S(2)}) collective-permute-start(bf16[2,128,256]{2,1,0:T(8,128)(2,1)} %copy-done.27), channel_id=1, source_target_pairs={{2,0},{3,1},{4,2},{5,3},{6,4},{7,5},{8,6},{9,7},{10,8},{11,9},{12,... | collective-permute-start | bytes 393224 | tf_op jit(solution)/shard_map/ppermute | solution.py:254
  155.7 8.1 %collective-permute-start.19 = (bf16[2,128,256]{2,1,0:T(8,128)(2,1)}, bf16[2,128,256]{2,1,0:T(8,128)(2,1)S(1)}, u32[]{:S(2)}, u32[]{:S(2)}) collective-permute-start(bf16[2,128,256]{2,1,0:T(8,128)(2,1)} %copy-done.26), channel_id=1, source_target_pairs={{0,2},{1,3},{2,4},{3,5},{4,6},{5,7},{6,8},{7,9},{8,10},{9,11},{10,... | collective-permute-start | bytes 393224 | tf_op jit(solution)/shard_map/ppermute | solution.py:254
  165.1 2.0 collective-permute-done.19.refs_9_
  169.4 9.8 %adjoint.3 = (bf16[8,128,256]{2,1,0:T(8,128)(2,1)S(1)}, f32[8,128,256]{2,1,0:T(8,128)S(1)}, bf16[2,128,256]{2,1,0:T(8,128)(2,1)S(1)}, bf16[2,128,256]{2,1,0:T(8,...) custom-call(s32[1,24]{1,0:T(1,128)S(1)} %copy-done.19, s32[1,24]{1,0:T(1,128)S(1)} %copy-done.21, ...), custom_call_target="tpu_custom_call" | custom-call | flops 402653184 | bytes 7340260 | tf_op jit(solution)/shard_map/adjoint/pallas_call | solution.py:28
  179.3 4.8 %collective-permute-start.20 = (bf16[2,128,256]{2,1,0:T(8,128)(2,1)S(1)}, bf16[2,128,256]{2,1,0:T(8,128)(2,1)S(1)}, u32[]{:S(2)}, u32[]{:S(2)}) collective-permute-start(bf16[2,128,256]{2,1,0:T(8,128)(2,1)S(1)} %get-tuple-element.61), channel_id=1, source_target_pairs={{1,0},{2,1},{3,2},{4,3},{5,4},{6,5},{7,6},{8,7},{9,8},{10,9},{11,1... | collective-permute-start | bytes 393224 | tf_op jit(solution)/shard_map/ppermute | solution.py:254
  184.1 5.4 %collective-permute-start.21 = (bf16[2,128,256]{2,1,0:T(8,128)(2,1)S(1)}, bf16[2,128,256]{2,1,0:T(8,128)(2,1)S(1)}, u32[]{:S(2)}, u32[]{:S(2)}) collective-permute-start(bf16[2,128,256]{2,1,0:T(8,128)(2,1)S(1)} %get-tuple-element.62), channel_id=1, source_target_pairs={{0,1},{1,2},{2,3},{3,4},{4,5},{5,6},{6,7},{7,8},{8,9},{9,10},{10,1... | collective-permute-start | bytes 393224 | tf_op jit(solution)/shard_map/ppermute | solution.py:254
  191.4 9.6 %collective-permute-start.23 = (bf16[2,128,256]{2,1,0:T(8,128)(2,1)S(1)}, bf16[2,128,256]{2,1,0:T(8,128)(2,1)S(1)}, u32[]{:S(2)}, u32[]{:S(2)}) collective-permute-start(bf16[2,128,256]{2,1,0:T(8,128)(2,1)S(1)} %get-tuple-element.64), channel_id=1, source_target_pairs={{0,2},{1,3},{2,4},{3,5},{4,6},{5,7},{6,8},{7,9},{8,10},{9,11},{10,... | collective-permute-start | bytes 393224 | tf_op jit(solution)/shard_map/ppermute | solution.py:254
  201.0 9.4 %collective-permute-start.8 = (bf16[2,256,128]{2,1,0:T(8,128)(2,1)S(1)}, bf16[2,256,128]{2,1,0:T(8,128)(2,1)S(1)}, u32[]{:S(2)}, u32[]{:S(2)}) collective-permute-start(bf16[2,256,128]{2,1,0:T(8,128)(2,1)S(1)} %copy-done.25), channel_id=1, source_target_pairs={{0,1},{1,2},{2,3},{3,4},{4,5},{5,6},{6,7},{7,8},{8,9},{9,10},{10,1... | collective-permute-start | bytes 393224 | tf_op jit(solution)/shard_map/ppermute | solution.py:254
  212.3 8.2 %collective-permute-start.10 = (bf16[2,256,128]{2,1,0:T(8,128)(2,1)S(1)}, bf16[2,256,128]{2,1,0:T(8,128)(2,1)S(1)}, u32[]{:S(2)}, u32[]{:S(2)}) collective-permute-start(bf16[2,256,128]{2,1,0:T(8,128)(2,1)S(1)} %get-tuple-element.47), channel_id=1, source_target_pairs={{0,2},{1,3},{2,4},{3,5},{4,6},{5,7},{6,8},{7,9},{8,10},{9,11},{10,... | collective-permute-start | bytes 393224 | tf_op jit(solution)/shard_map/ppermute | solution.py:254
  222.5 2.3 adjoint_end.1
  224.8 8.3 %collective-permute-done.11.refs_9_ = bf16[2,256,128]{2,1,0:T(8,128)(2,1)S(1)} collective-permute-done((bf16[2,256,128]{2,1,0:T(8,128)(2,1)S(1)}, bf16[2,256,128]{2,1,0:T(8,128)(2,1)S(1)}, u32[]{:S(2)}, u32[]{:S(2)}) %collective-permute-start.11) | collective-permute-done | bytes 131104 | tf_op jit(solution)/shard_map/ppermute | solution.py:254
  233.1 12.0 %forward.5 = bf16[8,256,128]{2,1,0:T(8,128)(2,1)} custom-call(s32[1,24]{1,0:T(1,128)S(1)} %copy-done.19, s32[1,24]{1,0:T(1,128)S(1)} %copy-done.21, s32[1]{0:T(128)S(6)} %copy.18.refs_2_.count, s32[1,4,2]{2,1,0:T(4,128)S(1)} %copy.14.send.refs_3_, bf16[24,256,256]{2,1,0:T(8,128)(2,1)S(1)} %bitcast.12, bf16[8,256,128]{2,1,0:T(8,128)(2,1)S(1)} %copy-done.13, ...), custom_call_target="tpu_custom_call" | custom-call | flops 402653184 | bytes 5898468 | tf_op jit(solution)/shard_map/forward/pallas_call | solution.py:28
  (92 shorter events, 22.5 us)
Async XLA Ops:
  3.8 34.4 %collective-permute-start = (bf16[2,256,128]{2,1,0:T(8,128)(2,1)S(1)}, bf16[2,256,128]{2,1,0:T(8,128)(2,1)S(1)}, u32[]{:S(2)}, u32[]{:S(2)}) collective-permute-start(bf16[2,256,128]{2,1,0:T(8,128)(2,1)S(1)} %get-tuple-element.35), channel_id=1, source_target_pairs={{0,1},{1,2},{2,3},{3,4},{4,5},{5,6},{6,7},{7,8},{8,9},{9,10},{10,1... | collective-permute-start | bytes 393224 | tf_op jit(solution)/shard_map/ppermute | solution.py:254
  7.0 35.2 %collective-permute-start.1 = (bf16[2,256,128]{2,1,0:T(8,128)(2,1)S(1)}, bf16[2,256,128]{2,1,0:T(8,128)(2,1)S(1)}, u32[]{:S(2)}, u32[]{:S(2)}) collective-permute-start(bf16[2,256,128]{2,1,0:T(8,128)(2,1)S(1)} %get-tuple-element.36), channel_id=1, source_target_pairs={{1,0},{2,1},{3,2},{4,3},{5,4},{6,5},{7,6},{8,7},{9,8},{10,9},{11,1... | collective-permute-start | bytes 393224 | tf_op jit(solution)/shard_map/ppermute | solution.py:254
  9.6 34.5 %collective-permute-start.2 = (bf16[2,256,128]{2,1,0:T(8,128)(2,1)S(1)}, bf16[2,256,128]{2,1,0:T(8,128)(2,1)S(1)}, u32[]{:S(2)}, u32[]{:S(2)}) collective-permute-start(bf16[2,256,128]{2,1,0:T(8,128)(2,1)S(1)} %get-tuple-element.37), channel_id=1, source_target_pairs={{0,2},{1,3},{2,4},{3,5},{4,6},{5,7},{6,8},{7,9},{8,10},{9,11},{10,... | collective-permute-start | bytes 393224 | tf_op jit(solution)/shard_map/ppermute | solution.py:254
  19.8 34.0 %collective-permute-start.3 = (bf16[2,256,128]{2,1,0:T(8,128)(2,1)S(1)}, bf16[2,256,128]{2,1,0:T(8,128)(2,1)S(1)}, u32[]{:S(2)}, u32[]{:S(2)}) collective-permute-start(bf16[2,256,128]{2,1,0:T(8,128)(2,1)S(1)} %get-tuple-element.38), channel_id=1, source_target_pairs={{2,0},{3,1},{4,2},{5,3},{6,4},{7,5},{8,6},{9,7},{10,8},{11,9},{12,... | collective-permute-start | bytes 393224 | tf_op jit(solution)/shard_map/ppermute | solution.py:254
  36.3 70.9 %copy-start.7 = (bf16[8,128,256]{2,1,0:T(8,128)(2,1)}, bf16[8,128,256]{2,1,0:T(8,128)(2,1)S(1)}, u32[]{:S(2)}) copy-start(bf16[8,128,256]{2,1,0:T(8,128)(2,1)S(1)} %get-tuple-element.59.refs_10_.u0) | copy-start | bytes 1572868
  36.3 37.2 %collective-permute-start.12 = (bf16[2,128,256]{2,1,0:T(8,128)(2,1)S(1)}, bf16[2,128,256]{2,1,0:T(8,128)(2,1)S(1)}, u32[]{:S(2)}, u32[]{:S(2)}) collective-permute-start(bf16[2,128,256]{2,1,0:T(8,128)(2,1)S(1)} %get-tuple-element.50), channel_id=1, source_target_pairs={{1,0},{2,1},{3,2},{4,3},{5,4},{6,5},{7,6},{8,7},{9,8},{10,9},{11,1... | collective-permute-start | bytes 393224 | tf_op jit(solution)/shard_map/ppermute | solution.py:254
  38.2 37.2 %collective-permute-start.13 = (bf16[2,128,256]{2,1,0:T(8,128)(2,1)S(1)}, bf16[2,128,256]{2,1,0:T(8,128)(2,1)S(1)}, u32[]{:S(2)}, u32[]{:S(2)}) collective-permute-start(bf16[2,128,256]{2,1,0:T(8,128)(2,1)S(1)} %get-tuple-element.51), channel_id=1, source_target_pairs={{0,1},{1,2},{2,3},{3,4},{4,5},{5,6},{6,7},{7,8},{8,9},{9,10},{10,1... | collective-permute-start | bytes 393224 | tf_op jit(solution)/shard_map/ppermute | solution.py:254
  42.2 41.4 %collective-permute-start.14 = (bf16[2,128,256]{2,1,0:T(8,128)(2,1)S(1)}, bf16[2,128,256]{2,1,0:T(8,128)(2,1)S(1)}, u32[]{:S(2)}, u32[]{:S(2)}) collective-permute-start(bf16[2,128,256]{2,1,0:T(8,128)(2,1)S(1)} %get-tuple-element.52), channel_id=1, source_target_pairs={{2,0},{3,1},{4,2},{5,3},{6,4},{7,5},{8,6},{9,7},{10,8},{11,9},{12,... | collective-permute-start | bytes 393224 | tf_op jit(solution)/shard_map/ppermute | solution.py:254
  44.1 41.4 %collective-permute-start.15 = (bf16[2,128,256]{2,1,0:T(8,128)(2,1)S(1)}, bf16[2,128,256]{2,1,0:T(8,128)(2,1)S(1)}, u32[]{:S(2)}, u32[]{:S(2)}) collective-permute-start(bf16[2,128,256]{2,1,0:T(8,128)(2,1)S(1)} %get-tuple-element.53), channel_id=1, source_target_pairs={{0,2},{1,3},{2,4},{3,5},{4,6},{5,7},{6,8},{7,9},{8,10},{9,11},{10,... | collective-permute-start | bytes 393224 | tf_op jit(solution)/shard_map/ppermute | solution.py:254
  64.5 31.8 %collective-permute-start.4 = (bf16[2,256,128]{2,1,0:T(8,128)(2,1)S(1)}, bf16[2,256,128]{2,1,0:T(8,128)(2,1)S(1)}, u32[]{:S(2)}, u32[]{:S(2)}) collective-permute-start(bf16[2,256,128]{2,1,0:T(8,128)(2,1)S(1)} %get-tuple-element.40), channel_id=1, source_target_pairs={{0,1},{1,2},{2,3},{3,4},{4,5},{5,6},{6,7},{7,8},{8,9},{9,10},{10,1... | collective-permute-start | bytes 393224 | tf_op jit(solution)/shard_map/ppermute | solution.py:254
  73.5 22.9 %collective-permute-start.5 = (bf16[2,256,128]{2,1,0:T(8,128)(2,1)S(1)}, bf16[2,256,128]{2,1,0:T(8,128)(2,1)S(1)}, u32[]{:S(2)}, u32[]{:S(2)}) collective-permute-start(bf16[2,256,128]{2,1,0:T(8,128)(2,1)S(1)} %get-tuple-element.41), channel_id=1, source_target_pairs={{1,0},{2,1},{3,2},{4,3},{5,4},{6,5},{7,6},{8,7},{9,8},{10,9},{11,1... | collective-permute-start | bytes 393224 | tf_op jit(solution)/shard_map/ppermute | solution.py:254
  75.4 20.9 %collective-permute-start.6 = (bf16[2,256,128]{2,1,0:T(8,128)(2,1)S(1)}, bf16[2,256,128]{2,1,0:T(8,128)(2,1)S(1)}, u32[]{:S(2)}, u32[]{:S(2)}) collective-permute-start(bf16[2,256,128]{2,1,0:T(8,128)(2,1)S(1)} %get-tuple-element.42), channel_id=1, source_target_pairs={{0,2},{1,3},{2,4},{3,5},{4,6},{5,7},{6,8},{7,9},{8,10},{9,11},{10,... | collective-permute-start | bytes 393224 | tf_op jit(solution)/shard_map/ppermute | solution.py:254
  83.6 12.7 %collective-permute-start.7 = (bf16[2,256,128]{2,1,0:T(8,128)(2,1)S(1)}, bf16[2,256,128]{2,1,0:T(8,128)(2,1)S(1)}, u32[]{:S(2)}, u32[]{:S(2)}) collective-permute-start(bf16[2,256,128]{2,1,0:T(8,128)(2,1)S(1)} %get-tuple-element.43), channel_id=1, source_target_pairs={{2,0},{3,1},{4,2},{5,3},{6,4},{7,5},{8,6},{9,7},{10,8},{11,9},{12,... | collective-permute-start | bytes 393224 | tf_op jit(solution)/shard_map/ppermute | solution.py:254
  107.2 59.9 %copy-start.19 = (s32[1,24]{1,0:T(1,128)S(1)}, s32[1,24]{1,0:T(1,128)}, u32[]{:S(2)}) copy-start(s32[1,24]{1,0:T(1,128)} %refs_0_.9) | copy-start | bytes 292
  130.6 91.9 %copy-start.16 = (bf16[4,128,128]{2,1,0:T(8,128)(2,1)S(1)}, bf16[4,128,128]{2,1,0:T(8,128)(2,1)}, u32[]{:S(2)}) copy-start(bf16[4,128,128]{2,1,0:T(8,128)(2,1)} %filters.1) | copy-start | bytes 393220
  132.7 112.5 %all-to-all-start.1 = ((f32[256,2,128]{2,1,0:T(2,128)}), f32[256,2,128]{2,1,0:T(2,128)}, u32[]{:S(2)}, u32[]{:S(2)}) async-start(f32[256,2,128]{2,1,0:T(2,128)} %broadcast_in_dim.2), calls=%async_computation.1 | async-start | bytes 524288 | tf_op jit(solution)/shard_map/all_to_all | solution.py:270
  146.4 17.4 %collective-permute-start.16 = (bf16[2,128,256]{2,1,0:T(8,128)(2,1)}, bf16[2,128,256]{2,1,0:T(8,128)(2,1)S(1)}, u32[]{:S(2)}, u32[]{:S(2)}) collective-permute-start(bf16[2,128,256]{2,1,0:T(8,128)(2,1)} %copy-done.29), channel_id=1, source_target_pairs={{1,0},{2,1},{3,2},{4,3},{5,4},{6,5},{7,6},{8,7},{9,8},{10,9},{11,1... | collective-permute-start | bytes 393224 | tf_op jit(solution)/shard_map/ppermute | solution.py:254
  148.8 15.0 %collective-permute-start.17 = (bf16[2,128,256]{2,1,0:T(8,128)(2,1)}, bf16[2,128,256]{2,1,0:T(8,128)(2,1)S(1)}, u32[]{:S(2)}, u32[]{:S(2)}) collective-permute-start(bf16[2,128,256]{2,1,0:T(8,128)(2,1)} %copy-done.28), channel_id=1, source_target_pairs={{0,1},{1,2},{2,3},{3,4},{4,5},{5,6},{6,7},{7,8},{8,9},{9,10},{10,1... | collective-permute-start | bytes 393224 | tf_op jit(solution)/shard_map/ppermute | solution.py:254
  152.2 12.9 %collective-permute-start.18 = (bf16[2,128,256]{2,1,0:T(8,128)(2,1)}, bf16[2,128,256]{2,1,0:T(8,128)(2,1)S(1)}, u32[]{:S(2)}, u32[]{:S(2)}) collective-permute-start(bf16[2,128,256]{2,1,0:T(8,128)(2,1)} %copy-done.27), channel_id=1, source_target_pairs={{2,0},{3,1},{4,2},{5,3},{6,4},{7,5},{8,6},{9,7},{10,8},{11,9},{12,... | collective-permute-start | bytes 393224 | tf_op jit(solution)/shard_map/ppermute | solution.py:254
  155.7 11.4 %collective-permute-start.19 = (bf16[2,128,256]{2,1,0:T(8,128)(2,1)}, bf16[2,128,256]{2,1,0:T(8,128)(2,1)S(1)}, u32[]{:S(2)}, u32[]{:S(2)}) collective-permute-start(bf16[2,128,256]{2,1,0:T(8,128)(2,1)} %copy-done.26), channel_id=1, source_target_pairs={{0,2},{1,3},{2,4},{3,5},{4,6},{5,7},{6,8},{7,9},{8,10},{9,11},{10,... | collective-permute-start | bytes 393224 | tf_op jit(solution)/shard_map/ppermute | solution.py:254
  169.4 53.1 %copy-start.11 = (bf16[8,128,256]{2,1,0:T(8,128)(2,1)S(1)}, bf16[8,128,256]{2,1,0:T(8,128)(2,1)}, u32[]{:S(2)}) copy-start(bf16[8,128,256]{2,1,0:T(8,128)(2,1)} %copy-done.10) | copy-start | bytes 1572868
  179.2 53.9 %copy-start.4 = (bf16[1,2048,128]{2,1,0:T(8,128)(2,1)S(1)}, bf16[1,2048,128]{2,1,0:T(8,128)(2,1)}, u32[]{:S(2)}) copy-start(bf16[1,2048,128]{2,1,0:T(8,128)(2,1)} %param.8) | copy-start | bytes 1572868
  179.3 53.9 %copy-start.6 = (bf16[8,256,128]{2,1,0:T(8,128)(2,1)S(1)}, bf16[8,256,128]{2,1,0:T(8,128)(2,1)}, u32[]{:S(2)}) copy-start(bf16[8,256,128]{2,1,0:T(8,128)(2,1)} %copy-done.5) | copy-start | bytes 1572868
  179.3 53.9 %copy-start.13 = (bf16[8,256,128]{2,1,0:T(8,128)(2,1)S(1)}, bf16[8,256,128]{2,1,0:T(8,128)(2,1)}, u32[]{:S(2)}) copy-start(bf16[8,256,128]{2,1,0:T(8,128)(2,1)} %copy-done.12) | copy-start | bytes 1572868
  179.3 31.1 %collective-permute-start.20 = (bf16[2,128,256]{2,1,0:T(8,128)(2,1)S(1)}, bf16[2,128,256]{2,1,0:T(8,128)(2,1)S(1)}, u32[]{:S(2)}, u32[]{:S(2)}) collective-permute-start(bf16[2,128,256]{2,1,0:T(8,128)(2,1)S(1)} %get-tuple-element.61), channel_id=1, source_target_pairs={{1,0},{2,1},{3,2},{4,3},{5,4},{6,5},{7,6},{8,7},{9,8},{10,9},{11,1... | collective-permute-start | bytes 393224 | tf_op jit(solution)/shard_map/ppermute | solution.py:254
  184.1 28.3 %collective-permute-start.21 = (bf16[2,128,256]{2,1,0:T(8,128)(2,1)S(1)}, bf16[2,128,256]{2,1,0:T(8,128)(2,1)S(1)}, u32[]{:S(2)}, u32[]{:S(2)}) collective-permute-start(bf16[2,128,256]{2,1,0:T(8,128)(2,1)S(1)} %get-tuple-element.62), channel_id=1, source_target_pairs={{0,1},{1,2},{2,3},{3,4},{4,5},{5,6},{6,7},{7,8},{8,9},{9,10},{10,1... | collective-permute-start | bytes 393224 | tf_op jit(solution)/shard_map/ppermute | solution.py:254
  189.4 31.1 %collective-permute-start.22 = (bf16[2,128,256]{2,1,0:T(8,128)(2,1)S(1)}, bf16[2,128,256]{2,1,0:T(8,128)(2,1)S(1)}, u32[]{:S(2)}, u32[]{:S(2)}) collective-permute-start(bf16[2,128,256]{2,1,0:T(8,128)(2,1)S(1)} %get-tuple-element.63), channel_id=1, source_target_pairs={{2,0},{3,1},{4,2},{5,3},{6,4},{7,5},{8,6},{9,7},{10,8},{11,9},{12,... | collective-permute-start | bytes 393224 | tf_op jit(solution)/shard_map/ppermute | solution.py:254
  191.4 31.1 %collective-permute-start.23 = (bf16[2,128,256]{2,1,0:T(8,128)(2,1)S(1)}, bf16[2,128,256]{2,1,0:T(8,128)(2,1)S(1)}, u32[]{:S(2)}, u32[]{:S(2)}) collective-permute-start(bf16[2,128,256]{2,1,0:T(8,128)(2,1)S(1)} %get-tuple-element.64), channel_id=1, source_target_pairs={{0,2},{1,3},{2,4},{3,5},{4,6},{5,7},{6,8},{7,9},{8,10},{9,11},{10,... | collective-permute-start | bytes 393224 | tf_op jit(solution)/shard_map/ppermute | solution.py:254
  201.0 23.8 %collective-permute-start.8 = (bf16[2,256,128]{2,1,0:T(8,128)(2,1)S(1)}, bf16[2,256,128]{2,1,0:T(8,128)(2,1)S(1)}, u32[]{:S(2)}, u32[]{:S(2)}) collective-permute-start(bf16[2,256,128]{2,1,0:T(8,128)(2,1)S(1)} %copy-done.25), channel_id=1, source_target_pairs={{0,1},{1,2},{2,3},{3,4},{4,5},{5,6},{6,7},{7,8},{8,9},{9,10},{10,1... | collective-permute-start | bytes 393224 | tf_op jit(solution)/shard_map/ppermute | solution.py:254
  210.4 14.4 %collective-permute-start.9 = (bf16[2,256,128]{2,1,0:T(8,128)(2,1)S(1)}, bf16[2,256,128]{2,1,0:T(8,128)(2,1)S(1)}, u32[]{:S(2)}, u32[]{:S(2)}) collective-permute-start(bf16[2,256,128]{2,1,0:T(8,128)(2,1)S(1)} %copy-done.23), channel_id=1, source_target_pairs={{1,0},{2,1},{3,2},{4,3},{5,4},{6,5},{7,6},{8,7},{9,8},{10,9},{11,1... | collective-permute-start | bytes 393224 | tf_op jit(solution)/shard_map/ppermute | solution.py:254
  212.3 12.5 %collective-permute-start.10 = (bf16[2,256,128]{2,1,0:T(8,128)(2,1)S(1)}, bf16[2,256,128]{2,1,0:T(8,128)(2,1)S(1)}, u32[]{:S(2)}, u32[]{:S(2)}) collective-permute-start(bf16[2,256,128]{2,1,0:T(8,128)(2,1)S(1)} %get-tuple-element.47), channel_id=1, source_target_pairs={{0,2},{1,3},{2,4},{3,5},{4,6},{5,7},{6,8},{7,9},{8,10},{9,11},{10,... | collective-permute-start | bytes 393224 | tf_op jit(solution)/shard_map/ppermute | solution.py:254
  220.5 12.6 %collective-permute-start.11 = (bf16[2,256,128]{2,1,0:T(8,128)(2,1)S(1)}, bf16[2,256,128]{2,1,0:T(8,128)(2,1)S(1)}, u32[]{:S(2)}, u32[]{:S(2)}) collective-permute-start(bf16[2,256,128]{2,1,0:T(8,128)(2,1)S(1)} %get-tuple-element.48), channel_id=1, source_target_pairs={{2,0},{3,1},{4,2},{5,3},{6,4},{7,5},{8,6},{9,7},{10,8},{11,9},{12,... | collective-permute-start | bytes 393224 | tf_op jit(solution)/shard_map/ppermute | solution.py:254
  (23 other events, 348.6 us)

commit v2 on v1

--- a/solution.py
+++ b/solution.py
@@ -8,14 +8,37 @@
 from jax.sharding import PartitionSpec as P
 
 OFFSETS = (1, -1, 2, -2)
-START_ORDER = (2, 3, 0, 1)
 F32 = jnp.float32
 BF16 = jnp.bfloat16
-ANY = pl.BlockSpec(memory_space=pl.ANY)
 VMEM = pl.BlockSpec(memory_space=pltpu.VMEM)
 SMEM = pl.BlockSpec(memory_space=pltpu.SMEM)
 NB, BLK, C, MAXT, NSEND = 8, 256, 128, 24, 2
 NEXT = NB + 4 * NSEND
+
+
+ROUNDS = ("A", "C", "B", "D")
+
+
+def partner_of(device, kind):
+    if kind == "A":
+        return device + 2 if device % 4 < 2 else device - 2
+    if kind == "B":
+        return device - 2 if device % 4 < 2 else device + 2
+    if kind == "C":
+        return device + 1 if device % 2 == 0 else device - 1
+    return device - 1 if device % 2 == 0 else device + 1
+
+
+def positions():
+    me = lax.axis_index("sky")
+    high = lax.rem(me, 4) // 2
+    odd = lax.rem(me, 2)
+    where = {"A": 2 + high, "B": 3 - high, "C": odd, "D": 1 - odd}
+    return [where[kind] for kind in ROUNDS]
+
+
+def opposite(position):
+    return position + 1 - 2 * lax.rem(position, 2)
 
 
 def mm(a, b):
@@ -37,41 +60,26 @@
     )(*args)
 
 
-def start_tiles(tiles, tile_buf, tile_sem):
-    copies = [pltpu.make_async_copy(tiles.at[t], tile_buf.at[t], tile_sem.at[t]) for t in range(MAXT)]
-    for copy in copies:
-        copy.start()
-    return copies
-
-
 PIECE = jax.ShapeDtypeStruct((NSEND, BLK, C), BF16)
 PIECE_T = jax.ShapeDtypeStruct((NSEND, C, BLK), BF16)
 BLOCKS = jax.ShapeDtypeStruct((NB, BLK, C), BF16)
 BLOCKS_T = jax.ShapeDtypeStruct((NB, C, BLK), BF16)
 OWN_T = jax.ShapeDtypeStruct((NB, C, BLK), F32)
-TILE_SCRATCH = [pltpu.VMEM((MAXT, BLK, BLK), BF16), pltpu.SemaphoreType.DMA((MAXT,))]
 STEP_FLOPS = 2 * MAXT * BLK * BLK * C
 
 
-def pick_kernel(send, blocks, *rest):
-    outs, sem = rest[:4], rest[4]
-    copies = []
-    for i in range(4):
+def put_pieces(send, blocks, outs):
+    for out, position in zip(outs, positions()):
         for j in range(NSEND):
-            copies.append(
-                pltpu.make_async_copy(blocks.at[send[0, i, j]], outs[i].at[j], sem.at[i * NSEND + j])
-            )
-    for copy in copies:
-        copy.start()
-    for copy in copies:
-        copy.wait()
+            out[j] = blocks[send[0, position, j]]
+
+
+def pick_kernel(send, blocks, *outs):
+    put_pieces(send, blocks, outs)
 
 
 def pick(send, blocks):
-    return call(
-        pick_kernel, "pick", [PIECE] * 4, [ANY] * 4, [SMEM, ANY],
-        [pltpu.SemaphoreType.DMA((4 * NSEND,))], 0, (send, blocks),
-    )
+    return call(pick_kernel, "pick", [PIECE] * 4, [VMEM] * 4, [SMEM, VMEM], [], 0, (send, blocks))
 
 
 def forward_kernel(first, last, *refs):
@@ -86,24 +94,15 @@
     else:
         (out,) = take(1)
         pieces = take(4)
-    tile_buf, tile_sem, ext, ext_sem, acc = take(5)
-    tile_copies = start_tiles(tiles, tile_buf, tile_sem)
-    ext_copies = [pltpu.make_async_copy(blocks, ext.at[pl.ds(0, NB)], ext_sem.at[0])]
-    for i in range(4):
-        ext_copies.append(
-            pltpu.make_async_copy(
-                arrived[i], ext.at[pl.ds(NB + i * NSEND, NSEND)], ext_sem.at[1 + i]
-            )
-        )
-    for copy in ext_copies:
-        copy.start()
+    ext, acc = take(2)
+    ext[0:NB] = blocks[...]
+    for piece, position in zip(arrived, positions()):
+        for j in range(NSEND):
+            ext[NB + opposite(position) * NSEND + j] = piece[j]
     acc[...] = jnp.zeros_like(acc)
-    for copy in ext_copies:
-        copy.wait()
     for t in range(MAXT):
-        tile_copies[t].wait()
         where = jnp.where(t < count[0], target[0, t], NB)
-        acc[where] += mm(tile_buf[t], ext[source[0, t]])
+        acc[where] += mm(tiles[t], ext[source[0, t]])
     for b in range(NB):
         value = acc[b]
         if not first:
@@ -111,20 +110,18 @@
         value = value.astype(BF16)
         if last:
             result = mm(base[b], filters[0]) + mm(before[b], filters[1])
-            result = result + mm(ext[b], filters[2]) + mm(value, filters[3])
+            result = result + mm(blocks[b], filters[2]) + mm(value, filters[3])
             out[b] = result.astype(BF16)
         else:
             out[b] = value
     if not last:
-        for i in range(4):
-            for j in range(NSEND):
-                pieces[i][j] = out[send[0, i, j]]
+        put_pieces(send, out, pieces)
 
 
 def forward(tables, send, tiles, blocks, arrived, before=None, base=None, filters=None):
     first, last = before is None, base is not None
     args = [*tables, send, tiles, blocks, *arrived]
-    specs = [SMEM] * 4 + [ANY] * 6
+    specs = [SMEM] * 4 + [VMEM] * 6
     if not first:
         args.append(before)
         specs.append(VMEM)
@@ -134,34 +131,28 @@
         outs, out_specs = [BLOCKS], [VMEM]
     else:
         outs, out_specs = [BLOCKS] + [PIECE] * 4, [VMEM] * 5
-    scratch = TILE_SCRATCH + [
-        pltpu.VMEM((NEXT, BLK, C), BF16),
-        pltpu.SemaphoreType.DMA((5,)),
-        pltpu.VMEM((NB + 1, BLK, C), F32),
-    ]
+    scratch = [pltpu.VMEM((NEXT, BLK, C), BF16), pltpu.VMEM((NB + 1, BLK, C), F32)]
     kernel = lambda *refs: forward_kernel(first, last, *refs)
     return call(kernel, "forward", outs, out_specs, specs, scratch, STEP_FLOPS, args)
 
 
-def push_terms(target, source, count, tile_copies, tile_buf, held, acc, own, pieces):
+def push_terms(target, source, count, tiles, held, acc, own, pieces):
     acc[...] = jnp.zeros_like(acc)
     for t in range(MAXT):
-        tile_copies[t].wait()
         where = jnp.where(t < count[0], source[0, t], NEXT)
-        acc[where] += mm(held[target[0, t]], tile_buf[t])
-    for i in range(4):
+        acc[where] += mm(held[target[0, t]], tiles[t])
+    for piece, position in zip(pieces, positions()):
         for j in range(NSEND):
-            pieces[i][j] = acc[NB + i * NSEND + j].astype(BF16)
+            piece[j] = acc[NB + opposite(position) * NSEND + j].astype(BF16)
     own[...] = acc[0:NB]
 
 
 def adjoint_start_kernel(target, source, count, tiles, upstream, held, own, *rest):
     pieces = rest[:4]
-    tile_buf, tile_sem, acc = rest[4:]
-    tile_copies = start_tiles(tiles, tile_buf, tile_sem)
+    (acc,) = rest[4:]
     for b in range(NB):
         held[b] = upstream[b].astype(F32).T.astype(BF16)
-    push_terms(target, source, count, tile_copies, tile_buf, held, acc, own, pieces)
+    push_terms(target, source, count, tiles, held, acc, own, pieces)
 
 
 ACC_T = pltpu.VMEM((NEXT + 1, C, BLK), F32)
@@ -170,15 +161,15 @@
 def adjoint_start(tables, tiles, upstream):
     return call(
         adjoint_start_kernel, "adjoint_start", [BLOCKS_T, OWN_T] + [PIECE_T] * 4, [VMEM] * 6,
-        [SMEM] * 3 + [ANY, VMEM], TILE_SCRATCH + [ACC_T], STEP_FLOPS, (*tables, tiles, upstream),
+        [SMEM] * 3 + [VMEM, VMEM], [ACC_T], STEP_FLOPS, (*tables, tiles, upstream),
     )
 
 
 def gather_terms(send, own, arrived, total):
     total[...] = own[...]
-    for i in range(4):
+    for piece, position in zip(arrived, positions()):
         for j in range(NSEND):
-            total[send[0, i, j]] += arrived[i][j].astype(F32)
+            total[send[0, position, j]] += piece[j].astype(F32)
 
 
 def adjoint_kernel(first, *refs):
@@ -189,8 +180,7 @@
     before = None if first else take(1)[0]
     held, own = take(2)
     pieces = take(4)
-    tile_buf, tile_sem, acc = take(3)
-    tile_copies = start_tiles(tiles, tile_buf, tile_sem)
+    (acc,) = take(1)
     total = acc.at[pl.ds(0, NB)]
     gather_terms(send, own_in, arrived, total)
     for b in range(NB):
@@ -198,17 +188,17 @@
         if not first:
             value = 2.0 * value - before[b].astype(F32)
         held[b] = value.astype(BF16)
-    push_terms(target, source, count, tile_copies, tile_buf, held, acc, own, pieces)
+    push_terms(target, source, count, tiles, held, acc, own, pieces)
 
 
 def adjoint(tables, send, tiles, own, arrived, before=None):
     first = before is None
     args = [*tables, send, tiles, own, *arrived] + ([] if first else [before])
-    specs = [SMEM] * 4 + [ANY] + [VMEM] * (5 if first else 6)
+    specs = [SMEM] * 4 + [VMEM] * (6 if first else 7)
     kernel = lambda *refs: adjoint_kernel(first, *refs)
     return call(
         kernel, "adjoint", [BLOCKS_T, OWN_T] + [PIECE_T] * 4, [VMEM] * 6, specs,
-        TILE_SCRATCH + [ACC_T], STEP_FLOPS, args,
+        [ACC_T], STEP_FLOPS, args,
     )
 
 
@@ -249,15 +239,13 @@
     )[0]
 
 
-def passed_along(array, by):
+def spread(pieces):
     size = lax.axis_size("sky")
-    return lax.ppermute(array, "sky", [(i, i + by) for i in range(size) if 0 <= i + by < size])
-
-
-def spread(pieces, sign):
-    got = [None] * 4
-    for i in START_ORDER:
-        got[i] = passed_along(pieces[i], sign * OFFSETS[i])
+    got = []
+    for piece, kind in zip(pieces, ROUNDS):
+        pairs = [(i, partner_of(i, kind)) for i in range(size)]
+        pairs = [(i, j) for i, j in pairs if 0 <= j < size]
+        got.append(lax.ppermute(piece, "sky", pairs))
     return got
 
 
@@ -280,19 +268,19 @@
     tables = (tile_target, tile_source, tile_count)
     send = send_blocks
 
-    f1 = spread(pick(send, base), 1)
+    f1 = spread(pick(send, base))
     u0, own, *terms = adjoint_start(tables, tiles, upstream)
-    b1 = spread(terms, -1)
+    b1 = spread(terms)
     one, *pieces = forward(tables, send, tiles, base, f1)
-    f2 = spread(pieces, 1)
+    f2 = spread(pieces)
     u1, own, *terms = adjoint(tables, send, tiles, own, b1)
-    b2 = spread(terms, -1)
+    b2 = spread(terms)
     two, *pieces = forward(tables, send, tiles, one, f2, before=base)
     local = grads(base, one, two, u0, u1)
     summed = total_over_devices(local)
-    f3 = spread(pieces, 1)
+    f3 = spread(pieces)
     u2, own, *terms = adjoint(tables, send, tiles, own, b2, before=u0)
-    b3 = spread(terms, -1)
+    b3 = spread(terms)
     (outputs,) = forward(tables, send, tiles, two, f3, before=one, base=base, filters=filters)
     pixel_grad = adjoint_end(send, own, b3, (u0, u1, u2), filters)
     scale = 1.0 / math.sqrt(lax.axis_size("view") * lax.axis_size("sky") * NB * BLK)

time: 248 us -> 162 us (0.65)
  the two profiles are of different devices: /device:TPU:118 before, /device:TPU:128 now
where the time goes in v2:
time: 162 us; the launch traced here: 161 us
  starting transfers between devices  95.7 us (59%)
  blocking collectives  21.2 us (13%)
  Pallas kernels  15.2 us (9%)
  waiting for transfers between devices  14.1 us (9%)
  local copies, waits for them, and re-layouts  10.2 us (6%)
  other arithmetic  3.05 us (2%)
  between operations  1.9 us (1%)
    ppermute x24, starting transfers between devices, spread(): got.append(lax.ppermute(piece, 'sky', pairs))  83.5 us
    all_to_all x1, blocking collectives, total_over_devices(): lax.all_to_all(local.reshape(count, rows, C), axes, 0, 0, tiled=True)  21.2 us
    pallas_call x9, Pallas kernels, call(): pl.pallas_call(kernel, name=name, out_shape=outs, in_specs=in_specs, out_...  15.2 us
    ppermute x24, waiting for transfers between devices, spread(): got.append(lax.ppermute(piece, 'sky', pairs))  14.1 us
    all_to_all x1, starting transfers between devices, total_over_devices(): lax.all_to_all(jnp.broadcast_to(part[None], parts.shape), axes, 0, 0, til...  12.2 us
    unnamed x61, local copies, waits for them, and re-layouts  9.42 us
  transfers between devices with their start and end apart: 25, of which 4 were waited for; matrix products, arithmetic and copies ran while one was open for 0% of the time, Pallas kernels for 7%

profile of v2, /device:TPU:128, one launch (start us, length us, event | category | flops | bytes accessed | tf_op | source)
XLA Modules:
  0.0 161.4 jit_solution(6937284500449202800)
XLA Ops:
  1.4 1.0 copy-done.2
  3.1 3.3 %collective-permute-start = (bf16[2,256,128]{2,1,0:T(8,128)(2,1)S(1)}, bf16[2,256,128]{2,1,0:T(8,128)(2,1)S(1)}, u32[]{:S(2)}, u32[]{:S(2)}) collective-permute-start(bf16[2,256,128]{2,1,0:T(8,128)(2,1)S(1)} %get-tuple-element.35), channel_id=1, source_target_pairs={{0,2},{1,3},{2,0},{3,1},{4,6},{5,7},{6,4},{7,5},{8,10},{9,11},{10,... | collective-permute-start | bytes 393224 | tf_op jit(solution)/shard_map/ppermute | solution.py:248
  7.0 5.5 %collective-permute-start.2 = (bf16[2,256,128]{2,1,0:T(8,128)(2,1)S(1)}, bf16[2,256,128]{2,1,0:T(8,128)(2,1)S(1)}, u32[]{:S(2)}, u32[]{:S(2)}) collective-permute-start(bf16[2,256,128]{2,1,0:T(8,128)(2,1)S(1)} %get-tuple-element.37), channel_id=1, source_target_pairs={{2,4},{3,5},{4,2},{5,3},{6,8},{7,9},{8,6},{9,7},{10,12},{11,13},{1... | collective-permute-start | bytes 393224 | tf_op jit(solution)/shard_map/ppermute | solution.py:248
  12.5 6.6 %collective-permute-start.3 = (bf16[2,256,128]{2,1,0:T(8,128)(2,1)S(1)}, bf16[2,256,128]{2,1,0:T(8,128)(2,1)S(1)}, u32[]{:S(2)}, u32[]{:S(2)}) collective-permute-start(bf16[2,256,128]{2,1,0:T(8,128)(2,1)S(1)} %get-tuple-element.38), channel_id=1, source_target_pairs={{1,2},{2,1},{3,4},{4,3},{5,6},{6,5},{7,8},{8,7},{9,10},{10,9},{11,... | collective-permute-start | bytes 393224 | tf_op jit(solution)/shard_map/ppermute | solution.py:248
  19.7 1.9 %copy-done = bf16[1,24,256,256]{3,2,1,0:T(8,128)(2,1)S(1)} copy-done((bf16[1,24,256,256]{3,2,1,0:T(8,128)(2,1)S(1)}, bf16[1,24,256,256]{3,2,1,0:T(8,128)(2,1)}, u32[]{:S(2)}) %copy-start) | copy-done | bytes 3145752
  24.0 1.5 adjoint_start.1
  25.8 6.1 %collective-permute-start.14 = (bf16[2,128,256]{2,1,0:T(8,128)(2,1)S(1)}, bf16[2,128,256]{2,1,0:T(8,128)(2,1)S(1)}, u32[]{:S(2)}, u32[]{:S(2)}) collective-permute-start(bf16[2,128,256]{2,1,0:T(8,128)(2,1)S(1)} %get-tuple-element.52), channel_id=1, source_target_pairs={{2,4},{3,5},{4,2},{5,3},{6,8},{7,9},{8,6},{9,7},{10,12},{11,13},{1... | collective-permute-start | bytes 393224 | tf_op jit(solution)/shard_map/ppermute | solution.py:248
  31.9 6.6 %collective-permute-start.15 = (bf16[2,128,256]{2,1,0:T(8,128)(2,1)S(1)}, bf16[2,128,256]{2,1,0:T(8,128)(2,1)S(1)}, u32[]{:S(2)}, u32[]{:S(2)}) collective-permute-start(bf16[2,128,256]{2,1,0:T(8,128)(2,1)S(1)} %get-tuple-element.53), channel_id=1, source_target_pairs={{1,2},{2,1},{3,4},{4,3},{5,6},{6,5},{7,8},{8,7},{9,10},{10,9},{11,... | collective-permute-start | bytes 393224 | tf_op jit(solution)/shard_map/ppermute | solution.py:248
  38.5 1.7 %forward.3 = (bf16[8,256,128]{2,1,0:T(8,128)(2,1)S(1)}, bf16[2,256,128]{2,1,0:T(8,128)(2,1)S(1)}, bf16[2,256,128]{2,1,0:T(8,128)(2,1)S(1)}, bf16[2,256,128]{2,1,0:T(8,128)(2,1)S(1)}, bf16[2,256,128]{2,1,0:T(8,128)(2,1)S(1)}) custom-call(s32[1,24]{1,0:T(1,128)S(1)} %copy-done.18, s32[1,24]{1,0:T(1,128)S(1)} %copy-done.20, s32[1]{0:T(128)S(6)} %copy.18.refs_2_.count, ...), custom_call_target="tpu_custom_call" | custom-call | flops 402653184 | bytes 5243108 | tf_op jit(solution)/shard_map/forward/pallas_call | solution.py:51
  40.5 6.1 %collective-permute-start.6 = (bf16[2,256,128]{2,1,0:T(8,128)(2,1)S(1)}, bf16[2,256,128]{2,1,0:T(8,128)(2,1)S(1)}, u32[]{:S(2)}, u32[]{:S(2)}) collective-permute-start(bf16[2,256,128]{2,1,0:T(8,128)(2,1)S(1)} %get-tuple-element.42), channel_id=1, source_target_pairs={{2,4},{3,5},{4,2},{5,3},{6,8},{7,9},{8,6},{9,7},{10,12},{11,13},{1... | collective-permute-start | bytes 393224 | tf_op jit(solution)/shard_map/ppermute | solution.py:248
  46.7 6.6 %collective-permute-start.7 = (bf16[2,256,128]{2,1,0:T(8,128)(2,1)S(1)}, bf16[2,256,128]{2,1,0:T(8,128)(2,1)S(1)}, u32[]{:S(2)}, u32[]{:S(2)}) collective-permute-start(bf16[2,256,128]{2,1,0:T(8,128)(2,1)S(1)} %get-tuple-element.43), channel_id=1, source_target_pairs={{1,2},{2,1},{3,4},{4,3},{5,6},{6,5},{7,8},{8,7},{9,10},{10,9},{11,... | collective-permute-start | bytes 393224 | tf_op jit(solution)/shard_map/ppermute | solution.py:248
  53.3 1.7 %adjoint.2 = (bf16[8,128,256]{2,1,0:T(8,128)(2,1)S(1)}, f32[8,128,256]{2,1,0:T(8,128)S(1)}, bf16[2,128,256]{2,1,0:T(8,128)(2,1)S(1)}, bf16[2,128,256]{2,1,0:T(8,...) custom-call(s32[1,24]{1,0:T(1,128)S(1)} %copy-done.18, s32[1,24]{1,0:T(1,128)S(1)} %copy-done.20, ...), custom_call_target="tpu_custom_call" | custom-call | flops 402653184 | bytes 6815972 | tf_op jit(solution)/shard_map/adjoint/pallas_call | solution.py:51
  56.0 2.9 %collective-permute-done.7.refs_9_ = bf16[2,256,128]{2,1,0:T(8,128)(2,1)S(1)} collective-permute-done((bf16[2,256,128]{2,1,0:T(8,128)(2,1)S(1)}, bf16[2,256,128]{2,1,0:T(8,128)(2,1)S(1)}, u32[]{:S(2)}, u32[]{:S(2)}) %collective-permute-start.7) | collective-permute-done | bytes 131104 | tf_op jit(solution)/shard_map/ppermute | solution.py:248
  59.0 1.8 %forward.4 = (bf16[8,256,128]{2,1,0:T(8,128)(2,1)S(1)}, bf16[2,256,128]{2,1,0:T(8,128)(2,1)S(1)}, bf16[2,256,128]{2,1,0:T(8,128)(2,1)S(1)}, bf16[2,256,128]{2,1,0:T(8,128)(2,1)S(1)}, bf16[2,256,128]{2,1,0:T(8,128)(2,1)S(1)}) custom-call(s32[1,24]{1,0:T(1,128)S(1)} %copy-done.18, s32[1,24]{1,0:T(1,128)S(1)} %copy-done.21, s32[1]{0:T(128)S(6)} %copy.18.refs_2_.count, ...), custom_call_target="tpu_custom_call" | custom-call | flops 402653184 | bytes 5767396 | tf_op jit(solution)/shard_map/forward/pallas_call | solution.py:51
  61.7 21.2 %all_to_all.10 = f32[256,2,128]{2,1,0:T(2,128)} all-to-all(f32[256,2,128]{2,1,0:T(2,128)S(1)} %bitcast.18), channel_id=1, replica_groups=mesh['view'=2,'sky'=128] {'view','sky'}, dimensions={0} | all-to-all | bytes 524288 | tf_op jit(solution)/shard_map/all_to_all | solution.py:256
  82.9 1.3 reduce_sum.9
  84.9 12.2 %all-to-all-start.1 = ((f32[256,2,128]{2,1,0:T(2,128)}), f32[256,2,128]{2,1,0:T(2,128)}, u32[]{:S(2)}, u32[]{:S(2)}) async-start(f32[256,2,128]{2,1,0:T(2,128)} %broadcast_in_dim.2), calls=%async_computation.1 | async-start | bytes 524288 | tf_op jit(solution)/shard_map/all_to_all | solution.py:258
  97.2 3.2 %collective-permute-start.16 = (bf16[2,128,256]{2,1,0:T(8,128)(2,1)}, bf16[2,128,256]{2,1,0:T(8,128)(2,1)S(1)}, u32[]{:S(2)}, u32[]{:S(2)}) collective-permute-start(bf16[2,128,256]{2,1,0:T(8,128)(2,1)} %copy-done.29), channel_id=1, source_target_pairs={{0,2},{1,3},{2,0},{3,1},{4,6},{5,7},{6,4},{7,5},{8,10},{9,11},{10,... | collective-permute-start | bytes 393224 | tf_op jit(solution)/shard_map/ppermute | solution.py:248
  101.0 5.7 %collective-permute-start.18 = (bf16[2,128,256]{2,1,0:T(8,128)(2,1)}, bf16[2,128,256]{2,1,0:T(8,128)(2,1)S(1)}, u32[]{:S(2)}, u32[]{:S(2)}) collective-permute-start(bf16[2,128,256]{2,1,0:T(8,128)(2,1)} %copy-done.27), channel_id=1, source_target_pairs={{2,4},{3,5},{4,2},{5,3},{6,8},{7,9},{8,6},{9,7},{10,12},{11,13},{1... | collective-permute-start | bytes 393224 | tf_op jit(solution)/shard_map/ppermute | solution.py:248
  106.7 6.4 %collective-permute-start.19 = (bf16[2,128,256]{2,1,0:T(8,128)(2,1)}, bf16[2,128,256]{2,1,0:T(8,128)(2,1)S(1)}, u32[]{:S(2)}, u32[]{:S(2)}) collective-permute-start(bf16[2,128,256]{2,1,0:T(8,128)(2,1)} %copy-done.26), channel_id=1, source_target_pairs={{1,2},{2,1},{3,4},{4,3},{5,6},{6,5},{7,8},{8,7},{9,10},{10,9},{11,... | collective-permute-start | bytes 393224 | tf_op jit(solution)/shard_map/ppermute | solution.py:248
  113.8 5.4 %collective-permute-done.19.refs_9_ = bf16[2,128,256]{2,1,0:T(8,128)(2,1)S(1)} collective-permute-done((bf16[2,128,256]{2,1,0:T(8,128)(2,1)}, bf16[2,128,256]{2,1,0:T(8,128)(2,1)S(1)}, u32[]{:S(2)}, u32[]{:S(2)}) %collective-permute-start.19) | collective-permute-done | bytes 131104 | tf_op jit(solution)/shard_map/ppermute | solution.py:248
  119.2 1.0 copy-done.8
  120.3 1.2 copy-done.15
  121.5 1.8 %adjoint.3 = (bf16[8,128,256]{2,1,0:T(8,128)(2,1)S(1)}, f32[8,128,256]{2,1,0:T(8,128)S(1)}, bf16[2,128,256]{2,1,0:T(8,128)(2,1)S(1)}, bf16[2,128,256]{2,1,0:T(8,...) custom-call(s32[1,24]{1,0:T(1,128)S(1)} %copy-done.19, s32[1,24]{1,0:T(1,128)S(1)} %copy-done.21, ...), custom_call_target="tpu_custom_call" | custom-call | flops 402653184 | bytes 7340260 | tf_op jit(solution)/shard_map/adjoint/pallas_call | solution.py:51
  123.5 7.8 %collective-permute-start.22 = (bf16[2,128,256]{2,1,0:T(8,128)(2,1)S(1)}, bf16[2,128,256]{2,1,0:T(8,128)(2,1)S(1)}, u32[]{:S(2)}, u32[]{:S(2)}) collective-permute-start(bf16[2,128,256]{2,1,0:T(8,128)(2,1)S(1)} %get-tuple-element.63), channel_id=1, source_target_pairs={{2,4},{3,5},{4,2},{5,3},{6,8},{7,9},{8,6},{9,7},{10,12},{11,13},{1... | collective-permute-start | bytes 393224 | tf_op jit(solution)/shard_map/ppermute | solution.py:248
  131.3 4.9 %collective-permute-start.23 = (bf16[2,128,256]{2,1,0:T(8,128)(2,1)S(1)}, bf16[2,128,256]{2,1,0:T(8,128)(2,1)S(1)}, u32[]{:S(2)}, u32[]{:S(2)}) collective-permute-start(bf16[2,128,256]{2,1,0:T(8,128)(2,1)S(1)} %get-tuple-element.64), channel_id=1, source_target_pairs={{1,2},{2,1},{3,4},{4,3},{5,6},{6,5},{7,8},{8,7},{9,10},{10,9},{11,... | collective-permute-start | bytes 393224 | tf_op jit(solution)/shard_map/ppermute | solution.py:248
  136.5 7.8 %collective-permute-start.10 = (bf16[2,256,128]{2,1,0:T(8,128)(2,1)S(1)}, bf16[2,256,128]{2,1,0:T(8,128)(2,1)S(1)}, u32[]{:S(2)}, u32[]{:S(2)}) collective-permute-start(bf16[2,256,128]{2,1,0:T(8,128)(2,1)S(1)} %get-tuple-element.47), channel_id=1, source_target_pairs={{2,4},{3,5},{4,2},{5,3},{6,8},{7,9},{8,6},{9,7},{10,12},{11,13},{1... | collective-permute-start | bytes 393224 | tf_op jit(solution)/shard_map/ppermute | solution.py:248
  144.3 4.9 %collective-permute-start.11 = (bf16[2,256,128]{2,1,0:T(8,128)(2,1)S(1)}, bf16[2,256,128]{2,1,0:T(8,128)(2,1)S(1)}, u32[]{:S(2)}, u32[]{:S(2)}) collective-permute-start(bf16[2,256,128]{2,1,0:T(8,128)(2,1)S(1)} %get-tuple-element.48), channel_id=1, source_target_pairs={{1,2},{2,1},{3,4},{4,3},{5,6},{6,5},{7,8},{8,7},{9,10},{10,9},{11,... | collective-permute-start | bytes 393224 | tf_op jit(solution)/shard_map/ppermute | solution.py:248
  149.3 2.3 %adjoint_end.1 = bf16[8,256,128]{2,1,0:T(8,128)(2,1)} custom-call(s32[1,4,2]{2,1,0:T(4,128)S(1)} %copy.14.send.refs_3_, f32[8,128,256]{2,1,0:T(8,128)S(1)} %get-tuple-element.60.own_in, bf16[2,128,256]{2,1,0:T(8,128)(2,1)S(1)} %collective-permute-done.20.a0, bf16[2,128,256]{2,1,0:T(8,128)(2,1)S(1)} %collective-permute-done.21.a1, ...), custom_call_target="tpu_custom_call" | custom-call | flops 268435456 | bytes 3801120 | tf_op jit(solution)/shard_map/adjoint_end/pallas_call | solution.py:51
  151.5 5.0 %collective-permute-done.11.refs_9_ = bf16[2,256,128]{2,1,0:T(8,128)(2,1)S(1)} collective-permute-done((bf16[2,256,128]{2,1,0:T(8,128)(2,1)S(1)}, bf16[2,256,128]{2,1,0:T(8,128)(2,1)S(1)}, u32[]{:S(2)}, u32[]{:S(2)}) %collective-permute-start.11) | collective-permute-done | bytes 131104 | tf_op jit(solution)/shard_map/ppermute | solution.py:248
  156.6 3.0 %forward.5 = bf16[8,256,128]{2,1,0:T(8,128)(2,1)} custom-call(s32[1,24]{1,0:T(1,128)S(1)} %copy-done.19, s32[1,24]{1,0:T(1,128)S(1)} %copy-done.21, s32[1]{0:T(128)S(6)} %copy.18.refs_2_.count, s32[1,4,2]{2,1,0:T(4,128)S(1)} %copy.14.send.refs_3_, bf16[24,256,256]{2,1,0:T(8,128)(2,1)S(1)} %bitcast.12, bf16[8,256,128]{2,1,0:T(8,128)(2,1)S(1)} %copy-done.13, ...), custom_call_target="tpu_custom_call" | custom-call | flops 402653184 | bytes 5898468 | tf_op jit(solution)/shard_map/forward/pallas_call | solution.py:51
  159.6 1.8 %broadcast_multiply_fusion = f32[256,2,128]{2,1,0:T(2,128)} fusion(f32[256,2,128]{2,1,0:T(2,128)} %all-to-all-done.1), kind=kLoop, calls=%fused_computation | loop fusion | flops 65536 | bytes 524288 | tf_op jit(solution)/shard_map/mul | solution.py:287
  (92 shorter events, 9.2 us)
Async XLA Ops:
  2.4 36.1 %copy-start.3 = (bf16[1,2048,128]{2,1,0:T(8,128)(2,1)S(1)}, bf16[1,2048,128]{2,1,0:T(8,128)(2,1)}, u32[]{:S(2)}) copy-start(bf16[1,2048,128]{2,1,0:T(8,128)(2,1)} %param.8) | copy-start | bytes 1572868
  3.1 22.6 %collective-permute-start = (bf16[2,256,128]{2,1,0:T(8,128)(2,1)S(1)}, bf16[2,256,128]{2,1,0:T(8,128)(2,1)S(1)}, u32[]{:S(2)}, u32[]{:S(2)}) collective-permute-start(bf16[2,256,128]{2,1,0:T(8,128)(2,1)S(1)} %get-tuple-element.35), channel_id=1, source_target_pairs={{0,2},{1,3},{2,0},{3,1},{4,6},{5,7},{6,4},{7,5},{8,10},{9,11},{10,... | collective-permute-start | bytes 393224 | tf_op jit(solution)/shard_map/ppermute | solution.py:248
  6.3 19.4 %collective-permute-start.1 = (bf16[2,256,128]{2,1,0:T(8,128)(2,1)S(1)}, bf16[2,256,128]{2,1,0:T(8,128)(2,1)S(1)}, u32[]{:S(2)}, u32[]{:S(2)}) collective-permute-start(bf16[2,256,128]{2,1,0:T(8,128)(2,1)S(1)} %get-tuple-element.36), channel_id=1, source_target_pairs={{0,1},{1,0},{2,3},{3,2},{4,5},{5,4},{6,7},{7,6},{8,9},{9,8},{10,11... | collective-permute-start | bytes 393224 | tf_op jit(solution)/shard_map/ppermute | solution.py:248
  7.0 24.9 %collective-permute-start.2 = (bf16[2,256,128]{2,1,0:T(8,128)(2,1)S(1)}, bf16[2,256,128]{2,1,0:T(8,128)(2,1)S(1)}, u32[]{:S(2)}, u32[]{:S(2)}) collective-permute-start(bf16[2,256,128]{2,1,0:T(8,128)(2,1)S(1)} %get-tuple-element.37), channel_id=1, source_target_pairs={{2,4},{3,5},{4,2},{5,3},{6,8},{7,9},{8,6},{9,7},{10,12},{11,13},{1... | collective-permute-start | bytes 393224 | tf_op jit(solution)/shard_map/ppermute | solution.py:248
  12.5 26.0 %collective-permute-start.3 = (bf16[2,256,128]{2,1,0:T(8,128)(2,1)S(1)}, bf16[2,256,128]{2,1,0:T(8,128)(2,1)S(1)}, u32[]{:S(2)}, u32[]{:S(2)}) collective-permute-start(bf16[2,256,128]{2,1,0:T(8,128)(2,1)S(1)} %get-tuple-element.38), channel_id=1, source_target_pairs={{1,2},{2,1},{3,4},{4,3},{5,6},{6,5},{7,8},{8,7},{9,10},{10,9},{11,... | collective-permute-start | bytes 393224 | tf_op jit(solution)/shard_map/ppermute | solution.py:248
  25.5 35.3 %copy-start.7 = (bf16[8,128,256]{2,1,0:T(8,128)(2,1)}, bf16[8,128,256]{2,1,0:T(8,128)(2,1)S(1)}, u32[]{:S(2)}) copy-start(bf16[8,128,256]{2,1,0:T(8,128)(2,1)S(1)} %get-tuple-element.59.refs_10_.u0) | copy-start | bytes 1572868
  25.5 14.8 %collective-permute-start.12 = (bf16[2,128,256]{2,1,0:T(8,128)(2,1)S(1)}, bf16[2,128,256]{2,1,0:T(8,128)(2,1)S(1)}, u32[]{:S(2)}, u32[]{:S(2)}) collective-permute-start(bf16[2,128,256]{2,1,0:T(8,128)(2,1)S(1)} %get-tuple-element.50), channel_id=1, source_target_pairs={{0,2},{1,3},{2,0},{3,1},{4,6},{5,7},{6,4},{7,5},{8,10},{9,11},{10,... | collective-permute-start | bytes 393224 | tf_op jit(solution)/shard_map/ppermute | solution.py:248
  25.7 14.8 %collective-permute-start.13 = (bf16[2,128,256]{2,1,0:T(8,128)(2,1)S(1)}, bf16[2,128,256]{2,1,0:T(8,128)(2,1)S(1)}, u32[]{:S(2)}, u32[]{:S(2)}) collective-permute-start(bf16[2,128,256]{2,1,0:T(8,128)(2,1)S(1)} %get-tuple-element.51), channel_id=1, source_target_pairs={{0,1},{1,0},{2,3},{3,2},{4,5},{5,4},{6,7},{7,6},{8,9},{9,8},{10,11... | collective-permute-start | bytes 393224 | tf_op jit(solution)/shard_map/ppermute | solution.py:248
  25.8 20.9 %collective-permute-start.14 = (bf16[2,128,256]{2,1,0:T(8,128)(2,1)S(1)}, bf16[2,128,256]{2,1,0:T(8,128)(2,1)S(1)}, u32[]{:S(2)}, u32[]{:S(2)}) collective-permute-start(bf16[2,128,256]{2,1,0:T(8,128)(2,1)S(1)} %get-tuple-element.52), channel_id=1, source_target_pairs={{2,4},{3,5},{4,2},{5,3},{6,8},{7,9},{8,6},{9,7},{10,12},{11,13},{1... | collective-permute-start | bytes 393224 | tf_op jit(solution)/shard_map/ppermute | solution.py:248
  31.9 21.3 %collective-permute-start.15 = (bf16[2,128,256]{2,1,0:T(8,128)(2,1)S(1)}, bf16[2,128,256]{2,1,0:T(8,128)(2,1)S(1)}, u32[]{:S(2)}, u32[]{:S(2)}) collective-permute-start(bf16[2,128,256]{2,1,0:T(8,128)(2,1)S(1)} %get-tuple-element.53), channel_id=1, source_target_pairs={{1,2},{2,1},{3,4},{4,3},{5,6},{6,5},{7,8},{8,7},{9,10},{10,9},{11,... | collective-permute-start | bytes 393224 | tf_op jit(solution)/shard_map/ppermute | solution.py:248
  40.3 15.7 %collective-permute-start.4 = (bf16[2,256,128]{2,1,0:T(8,128)(2,1)S(1)}, bf16[2,256,128]{2,1,0:T(8,128)(2,1)S(1)}, u32[]{:S(2)}, u32[]{:S(2)}) collective-permute-start(bf16[2,256,128]{2,1,0:T(8,128)(2,1)S(1)} %get-tuple-element.40), channel_id=1, source_target_pairs={{0,2},{1,3},{2,0},{3,1},{4,6},{5,7},{6,4},{7,5},{8,10},{9,11},{10,... | collective-permute-start | bytes 393224 | tf_op jit(solution)/shard_map/ppermute | solution.py:248
  40.4 15.6 %collective-permute-start.5 = (bf16[2,256,128]{2,1,0:T(8,128)(2,1)S(1)}, bf16[2,256,128]{2,1,0:T(8,128)(2,1)S(1)}, u32[]{:S(2)}, u32[]{:S(2)}) collective-permute-start(bf16[2,256,128]{2,1,0:T(8,128)(2,1)S(1)} %get-tuple-element.41), channel_id=1, source_target_pairs={{0,1},{1,0},{2,3},{3,2},{4,5},{5,4},{6,7},{7,6},{8,9},{9,8},{10,11... | collective-permute-start | bytes 393224 | tf_op jit(solution)/shard_map/ppermute | solution.py:248
  40.5 15.5 %collective-permute-start.6 = (bf16[2,256,128]{2,1,0:T(8,128)(2,1)S(1)}, bf16[2,256,128]{2,1,0:T(8,128)(2,1)S(1)}, u32[]{:S(2)}, u32[]{:S(2)}) collective-permute-start(bf16[2,256,128]{2,1,0:T(8,128)(2,1)S(1)} %get-tuple-element.42), channel_id=1, source_target_pairs={{2,4},{3,5},{4,2},{5,3},{6,8},{7,9},{8,6},{9,7},{10,12},{11,13},{1... | collective-permute-start | bytes 393224 | tf_op jit(solution)/shard_map/ppermute | solution.py:248
  46.7 12.3 %collective-permute-start.7 = (bf16[2,256,128]{2,1,0:T(8,128)(2,1)S(1)}, bf16[2,256,128]{2,1,0:T(8,128)(2,1)S(1)}, u32[]{:S(2)}, u32[]{:S(2)}) collective-permute-start(bf16[2,256,128]{2,1,0:T(8,128)(2,1)S(1)} %get-tuple-element.43), channel_id=1, source_target_pairs={{1,2},{2,1},{3,4},{4,3},{5,6},{6,5},{7,8},{8,7},{9,10},{10,9},{11,... | collective-permute-start | bytes 393224 | tf_op jit(solution)/shard_map/ppermute | solution.py:248
  60.8 58.4 %copy-start.19 = (s32[1,24]{1,0:T(1,128)S(1)}, s32[1,24]{1,0:T(1,128)}, u32[]{:S(2)}) copy-start(s32[1,24]{1,0:T(1,128)} %refs_0_.9) | copy-start | bytes 292
  82.9 66.3 %copy-start.16 = (bf16[4,128,128]{2,1,0:T(8,128)(2,1)S(1)}, bf16[4,128,128]{2,1,0:T(8,128)(2,1)}, u32[]{:S(2)}) copy-start(bf16[4,128,128]{2,1,0:T(8,128)(2,1)} %filters.1) | copy-start | bytes 393220
  84.9 74.7 %all-to-all-start.1 = ((f32[256,2,128]{2,1,0:T(2,128)}), f32[256,2,128]{2,1,0:T(2,128)}, u32[]{:S(2)}, u32[]{:S(2)}) async-start(f32[256,2,128]{2,1,0:T(2,128)} %broadcast_in_dim.2), calls=%async_computation.1 | async-start | bytes 524288 | tf_op jit(solution)/shard_map/all_to_all | solution.py:258
  97.2 15.9 %collective-permute-start.16 = (bf16[2,128,256]{2,1,0:T(8,128)(2,1)}, bf16[2,128,256]{2,1,0:T(8,128)(2,1)S(1)}, u32[]{:S(2)}, u32[]{:S(2)}) collective-permute-start(bf16[2,128,256]{2,1,0:T(8,128)(2,1)} %copy-done.29), channel_id=1, source_target_pairs={{0,2},{1,3},{2,0},{3,1},{4,6},{5,7},{6,4},{7,5},{8,10},{9,11},{10,... | collective-permute-start | bytes 393224 | tf_op jit(solution)/shard_map/ppermute | solution.py:248
  100.4 12.8 %collective-permute-start.17 = (bf16[2,128,256]{2,1,0:T(8,128)(2,1)}, bf16[2,128,256]{2,1,0:T(8,128)(2,1)S(1)}, u32[]{:S(2)}, u32[]{:S(2)}) collective-permute-start(bf16[2,128,256]{2,1,0:T(8,128)(2,1)} %copy-done.28), channel_id=1, source_target_pairs={{0,1},{1,0},{2,3},{3,2},{4,5},{5,4},{6,7},{7,6},{8,9},{9,8},{10,11... | collective-permute-start | bytes 393224 | tf_op jit(solution)/shard_map/ppermute | solution.py:248
  101.0 12.8 %collective-permute-start.18 = (bf16[2,128,256]{2,1,0:T(8,128)(2,1)}, bf16[2,128,256]{2,1,0:T(8,128)(2,1)S(1)}, u32[]{:S(2)}, u32[]{:S(2)}) collective-permute-start(bf16[2,128,256]{2,1,0:T(8,128)(2,1)} %copy-done.27), channel_id=1, source_target_pairs={{2,4},{3,5},{4,2},{5,3},{6,8},{7,9},{8,6},{9,7},{10,12},{11,13},{1... | collective-permute-start | bytes 393224 | tf_op jit(solution)/shard_map/ppermute | solution.py:248
  106.7 12.5 %collective-permute-start.19 = (bf16[2,128,256]{2,1,0:T(8,128)(2,1)}, bf16[2,128,256]{2,1,0:T(8,128)(2,1)S(1)}, u32[]{:S(2)}, u32[]{:S(2)}) collective-permute-start(bf16[2,128,256]{2,1,0:T(8,128)(2,1)} %copy-done.26), channel_id=1, source_target_pairs={{1,2},{2,1},{3,4},{4,3},{5,6},{6,5},{7,8},{8,7},{9,10},{10,9},{11,... | collective-permute-start | bytes 393224 | tf_op jit(solution)/shard_map/ppermute | solution.py:248
  123.3 33.3 %copy-start.4 = (bf16[1,2048,128]{2,1,0:T(8,128)(2,1)S(1)}, bf16[1,2048,128]{2,1,0:T(8,128)(2,1)}, u32[]{:S(2)}) copy-start(bf16[1,2048,128]{2,1,0:T(8,128)(2,1)} %param.8) | copy-start | bytes 1572868
  123.3 33.3 %copy-start.6 = (bf16[8,256,128]{2,1,0:T(8,128)(2,1)S(1)}, bf16[8,256,128]{2,1,0:T(8,128)(2,1)}, u32[]{:S(2)}) copy-start(bf16[8,256,128]{2,1,0:T(8,128)(2,1)} %copy-done.5) | copy-start | bytes 1572868
  123.3 33.3 %copy-start.13 = (bf16[8,256,128]{2,1,0:T(8,128)(2,1)S(1)}, bf16[8,256,128]{2,1,0:T(8,128)(2,1)}, u32[]{:S(2)}) copy-start(bf16[8,256,128]{2,1,0:T(8,128)(2,1)} %copy-done.12) | copy-start | bytes 1572868
  123.3 13.0 %collective-permute-start.20 = (bf16[2,128,256]{2,1,0:T(8,128)(2,1)S(1)}, bf16[2,128,256]{2,1,0:T(8,128)(2,1)S(1)}, u32[]{:S(2)}, u32[]{:S(2)}) collective-permute-start(bf16[2,128,256]{2,1,0:T(8,128)(2,1)S(1)} %get-tuple-element.61), channel_id=1, source_target_pairs={{0,2},{1,3},{2,0},{3,1},{4,6},{5,7},{6,4},{7,5},{8,10},{9,11},{10,... | collective-permute-start | bytes 393224 | tf_op jit(solution)/shard_map/ppermute | solution.py:248
  123.4 13.1 %collective-permute-start.21 = (bf16[2,128,256]{2,1,0:T(8,128)(2,1)S(1)}, bf16[2,128,256]{2,1,0:T(8,128)(2,1)S(1)}, u32[]{:S(2)}, u32[]{:S(2)}) collective-permute-start(bf16[2,128,256]{2,1,0:T(8,128)(2,1)S(1)} %get-tuple-element.62), channel_id=1, source_target_pairs={{0,1},{1,0},{2,3},{3,2},{4,5},{5,4},{6,7},{7,6},{8,9},{9,8},{10,11... | collective-permute-start | bytes 393224 | tf_op jit(solution)/shard_map/ppermute | solution.py:248
  123.5 20.8 %collective-permute-start.22 = (bf16[2,128,256]{2,1,0:T(8,128)(2,1)S(1)}, bf16[2,128,256]{2,1,0:T(8,128)(2,1)S(1)}, u32[]{:S(2)}, u32[]{:S(2)}) collective-permute-start(bf16[2,128,256]{2,1,0:T(8,128)(2,1)S(1)} %get-tuple-element.63), channel_id=1, source_target_pairs={{2,4},{3,5},{4,2},{5,3},{6,8},{7,9},{8,6},{9,7},{10,12},{11,13},{1... | collective-permute-start | bytes 393224 | tf_op jit(solution)/shard_map/ppermute | solution.py:248
  131.3 17.9 %collective-permute-start.23 = (bf16[2,128,256]{2,1,0:T(8,128)(2,1)S(1)}, bf16[2,128,256]{2,1,0:T(8,128)(2,1)S(1)}, u32[]{:S(2)}, u32[]{:S(2)}) collective-permute-start(bf16[2,128,256]{2,1,0:T(8,128)(2,1)S(1)} %get-tuple-element.64), channel_id=1, source_target_pairs={{1,2},{2,1},{3,4},{4,3},{5,6},{6,5},{7,8},{8,7},{9,10},{10,9},{11,... | collective-permute-start | bytes 393224 | tf_op jit(solution)/shard_map/ppermute | solution.py:248
  136.2 15.3 %collective-permute-start.8 = (bf16[2,256,128]{2,1,0:T(8,128)(2,1)S(1)}, bf16[2,256,128]{2,1,0:T(8,128)(2,1)S(1)}, u32[]{:S(2)}, u32[]{:S(2)}) collective-permute-start(bf16[2,256,128]{2,1,0:T(8,128)(2,1)S(1)} %copy-done.25), channel_id=1, source_target_pairs={{0,2},{1,3},{2,0},{3,1},{4,6},{5,7},{6,4},{7,5},{8,10},{9,11},{10,... | collective-permute-start | bytes 393224 | tf_op jit(solution)/shard_map/ppermute | solution.py:248
  136.4 15.2 %collective-permute-start.9 = (bf16[2,256,128]{2,1,0:T(8,128)(2,1)S(1)}, bf16[2,256,128]{2,1,0:T(8,128)(2,1)S(1)}, u32[]{:S(2)}, u32[]{:S(2)}) collective-permute-start(bf16[2,256,128]{2,1,0:T(8,128)(2,1)S(1)} %copy-done.23), channel_id=1, source_target_pairs={{0,1},{1,0},{2,3},{3,2},{4,5},{5,4},{6,7},{7,6},{8,9},{9,8},{10,11... | collective-permute-start | bytes 393224 | tf_op jit(solution)/shard_map/ppermute | solution.py:248
  136.5 15.1 %collective-permute-start.10 = (bf16[2,256,128]{2,1,0:T(8,128)(2,1)S(1)}, bf16[2,256,128]{2,1,0:T(8,128)(2,1)S(1)}, u32[]{:S(2)}, u32[]{:S(2)}) collective-permute-start(bf16[2,256,128]{2,1,0:T(8,128)(2,1)S(1)} %get-tuple-element.47), channel_id=1, source_target_pairs={{2,4},{3,5},{4,2},{5,3},{6,8},{7,9},{8,6},{9,7},{10,12},{11,13},{1... | collective-permute-start | bytes 393224 | tf_op jit(solution)/shard_map/ppermute | solution.py:248
  144.3 12.3 %collective-permute-start.11 = (bf16[2,256,128]{2,1,0:T(8,128)(2,1)S(1)}, bf16[2,256,128]{2,1,0:T(8,128)(2,1)S(1)}, u32[]{:S(2)}, u32[]{:S(2)}) collective-permute-start(bf16[2,256,128]{2,1,0:T(8,128)(2,1)S(1)} %get-tuple-element.48), channel_id=1, source_target_pairs={{1,2},{2,1},{3,4},{4,3},{5,6},{6,5},{7,8},{8,7},{9,10},{10,9},{11,... | collective-permute-start | bytes 393224 | tf_op jit(solution)/shard_map/ppermute | solution.py:248
  (23 other events, 178.4 us)

commit v3 on v0

v3 whole, which is shorter than its diff:
```python
import math

import jax
import jax.numpy as jnp
from jax import lax
from jax.experimental import pallas as pl
from jax.experimental.pallas import tpu as pltpu
from jax.sharding import PartitionSpec as P

OFFSETS = (1, -1, 2, -2)
F32 = jnp.float32
BF16 = jnp.bfloat16
VMEM = pl.BlockSpec(memory_space=pltpu.VMEM)
SMEM = pl.BlockSpec(memory_space=pltpu.SMEM)
HBM = pl.BlockSpec(memory_space=pltpu.HBM)
NB, BLK, C, MAXT, NSEND = 8, 256, 128, 24, 2
NEXT = NB + 4 * NSEND


ROUNDS = ("A", "C", "B", "D")


def partner_of(device, kind):
    if kind == "A":
        return device + 2 if device % 4 < 2 else device - 2
    if kind == "B":
        return device - 2 if device % 4 < 2 else device + 2
    if kind == "C":
        return device + 1 if device % 2 == 0 else device - 1
    return device - 1 if device % 2 == 0 else device + 1


def positions():
    me = lax.axis_index("sky")
    high = lax.rem(me, 4) // 2
    odd = lax.rem(me, 2)
    where = {"A": 2 + high, "B": 3 - high, "C": odd, "D": 1 - odd}
    return [where[kind] for kind in ROUNDS]


def opposite(position):
    return position + 1 - 2 * lax.rem(position, 2)


def mm(a, b):
    return jnp.dot(a, b, preferred_element_type=F32)


def call(kernel, name, outs, out_specs, in_specs, scratch, flops, args):
    size = sum(math.prod(o.shape) * o.dtype.itemsize for o in outs)
    size += sum(math.prod(a.shape) * a.dtype.itemsize for a in args)
    pin = pltpu.with_memory_space_constraint
    args = [pin(a, pltpu.HBM) if spec is HBM else a for a, spec in zip(args, in_specs)]
    outs = [pltpu.HBM(o.shape, o.dtype) if spec is HBM else o for o, spec in zip(outs, out_specs)]
    return pl.pallas_call(
        kernel,
        name=name,
        out_shape=outs,
        in_specs=in_specs,
        out_specs=out_specs,
        scratch_shapes=scratch,
        cost_estimate=pl.CostEstimate(flops=flops, bytes_accessed=size, transcendentals=0),
        compiler_params=pltpu.CompilerParams(vmem_limit_bytes=24 * 1024 * 1024),
    )(*args)


BLOCKS = jax.ShapeDtypeStruct((NB, BLK, C), BF16)
BLOCKS_T = jax.ShapeDtypeStruct((NB, C, BLK), BF16)
OWN_T = jax.ShapeDtypeStruct((NB, C, BLK), F32)
LETTER = jax.ShapeDtypeStruct((2 * NSEND, BLK, C), BF16)
GRADS = jax.ShapeDtypeStruct((4 * C, C), BF16)
ACC = pltpu.VMEM((NB + 1, BLK, C), F32)
ACC_T = pltpu.VMEM((NEXT + 1, C, BLK), F32)
EXT = pltpu.VMEM((NEXT, BLK, C), BF16)
STEP_FLOPS = 2 * MAXT * BLK * BLK * C


def put_blocks(send, blocks, letters):
    for letter, position in zip(letters, positions()):
        for j in range(NSEND):
            letter[j] = blocks[send[0, position, j]]


def put_terms(acc, letters):
    for letter, position in zip(letters, positions()):
        for j in range(NSEND):
            term = acc[NB + opposite(position) * NSEND + j].astype(BF16)
            letter[NSEND + j, 0:C] = term[:, 0:C]
            letter[NSEND + j, C:BLK] = term[:, C:BLK]


def apply_forward(target, source, count, tiles, blocks, letters, ext, acc):
    ext[0:NB] = blocks[...]
    for letter, position in zip(letters, positions()):
        for j in range(NSEND):
            ext[NB + opposite(position) * NSEND + j] = letter[j]
    acc[...] = jnp.zeros_like(acc)
    for t in range(MAXT):
        where = jnp.where(t < count[0], target[0, t], NB)
        acc[where] += mm(tiles[t], ext[source[0, t]])


def apply_transposed(target, source, count, tiles, held, acc, which=range(MAXT)):
    for t in which:
        where = jnp.where(t < count[0], source[0, t], NEXT)
        acc[where] += mm(held[target[0, t]], tiles[t])


def gather_terms(send, own, letters, total):
    total[...] = own[...]
    for letter, position in zip(letters, positions()):
        for j in range(NSEND):
            block = send[0, position, j]
            total[block, :, 0:C] += letter[NSEND + j, 0:C].astype(F32)
            total[block, :, C:BLK] += letter[NSEND + j, C:BLK].astype(F32)


TILE_GROUPS = 4


def start_kernel(count, target_in, source_in, send_in, tiles_in, base, upstream_in, u0, own, *rest):
    letters = rest[:4]
    target, source, send, tiles, upstream, acc, table_sem, map_sem, tile_sem, letter_sem = rest[4:]
    copy = pltpu.make_async_copy
    tables = [
        copy(send_in, send, table_sem.at[0]),
        copy(target_in, target, table_sem.at[1]),
        copy(source_in, source, table_sem.at[2]),
    ]
    for one in tables:
        one.start()
    map_copy = copy(upstream_in, upstream, map_sem)
    map_copy.start()
    size = MAXT // TILE_GROUPS
    tile_copies = []
    for g in range(TILE_GROUPS):
        part = pl.ds(g * size, size)
        tile_copies.append(copy(tiles_in.at[part], tiles.at[part], tile_sem.at[g]))
        tile_copies[g].start()
    acc[...] = jnp.zeros_like(acc)
    for one in tables:
        one.wait()
    block_copies = []
    for k, position in enumerate(positions()):
        for j in range(NSEND):
            block_copies.append(
                copy(base.at[send[0, position, j]], letters[k].at[j], letter_sem.at[k * NSEND + j])
            )
    for one in block_copies:
        one.start()
    map_copy.wait()
    for b in range(NB):
        u0[b] = upstream[b].astype(F32).T.astype(BF16)
    for g in range(TILE_GROUPS):
        tile_copies[g].wait()
        group = range(g * size, (g + 1) * size)
        apply_transposed(target, source, count, tiles, u0, acc, group)
    for one in block_copies:
        one.wait()
    put_terms(acc, letters)
    own[...] = acc[0:NB]


def start(tables, tiles, base, upstream):
    target, source, count, send = tables
    dma = pltpu.SemaphoreType.DMA
    scratch = [
        pltpu.SMEM(target.shape, jnp.int32),
        pltpu.SMEM(source.shape, jnp.int32),
        pltpu.SMEM(send.shape, jnp.int32),
        pltpu.VMEM(tiles.shape, BF16),
        pltpu.VMEM(upstream.shape, BF16),
        ACC_T,
        dma((3,)),
        dma,
        dma((TILE_GROUPS,)),
        dma((4 * NSEND,)),
    ]
    return call(
        start_kernel, "start", [BLOCKS_T, OWN_T] + [LETTER] * 4, [VMEM] * 6,
        [SMEM] + [HBM] * 6, scratch, STEP_FLOPS, (count, target, source, send, tiles, base, upstream),
    )


def advance(first, scale, ins, arrived, cheb_out, u_out, letters, grads, scratch, sent):
    target, source, count, send, tiles, cheb, own_in = ins[:7]
    ext, acc, acc_t = scratch
    apply_forward(target, source, count, tiles, cheb, arrived, ext, acc)
    if not first:
        u0, cheb_before, u_before = ins[7:]
    for b in range(NB):
        value = acc[b]
        if not first:
            value = 2.0 * value - cheb_before[b].astype(F32)
        cheb_out[b] = value.astype(BF16)
    put_blocks(send, cheb_out, letters)
    sent("forward")
    if not first:
        g0 = jnp.zeros((C, C), F32)
        g1, g2, g3 = g0, g0, g0
        for b in range(NB):
            g0 += mm(u0[b], cheb_before[b])
            g1 += mm(u0[b], cheb[b])
            g2 += mm(u0[b], cheb_out[b])
            g3 += mm(u_before[b], cheb_out[b])
        for k, grad in enumerate((g0, g1, g2, 2.0 * g3 - g1)):
            grads[k * C : (k + 1) * C] = (scale * grad.T).astype(BF16)
        sent("grads")
    gather_terms(send, own_in, arrived, acc_t.at[pl.ds(0, NB)])
    for b in range(NB):
        value = acc_t[b]
        if not first:
            value = 2.0 * value - u0[b].astype(F32)
        u_out[b] = value.astype(BF16)
    sent("adjoint")
    acc_t[...] = jnp.zeros_like(acc_t)
    apply_transposed(target, source, count, tiles, u_out, acc_t)
    put_terms(acc_t, letters)


def first_step_kernel(*refs):
    ins, arrived, outs = refs[:7], refs[7:11], refs[11:18]
    scratch = refs[18:]
    cheb_out, u_out, own = outs[:3]
    advance(True, None, ins, arrived, cheb_out, u_out, outs[3:], None, scratch, lambda what: None)
    own[...] = scratch[2][0:NB]


def first_step(tables, tiles, cheb, own, arrived):
    args = [*tables, tiles, cheb, own, *arrived]
    outs = [BLOCKS, BLOCKS_T, OWN_T] + [LETTER] * 4
    return call(
        first_step_kernel, "first_step", outs, [VMEM] * len(outs),
        [SMEM] * 4 + [VMEM] * (len(args) - 4), [EXT, ACC, ACC_T], 2 * STEP_FLOPS, args,
    )


def second_step_kernel(scale, *refs):
    ins, arrived, outs = refs[:10], refs[10:14], refs[14:22]
    scratch, (cheb_out, u_out, letters, grads, sem) = refs[22:25], refs[25:]
    letters = [letters.at[k] for k in range(4)]
    copies = []

    def send_off(here, there):
        copies.append(pltpu.make_async_copy(here, there, sem.at[len(copies)]))
        copies[-1].start()

    def sent(what):
        if what == "forward":
            send_off(cheb_out, outs[0])
        elif what == "grads":
            send_off(grads, outs[7])
        else:
            send_off(u_out, outs[1])

    advance(False, scale, ins, arrived, cheb_out, u_out, letters, grads, scratch, sent)
    for k in range(4):
        send_off(letters[k], outs[3 + k])
    send_off(scratch[2].at[pl.ds(0, NB)], outs[2])
    for copy in copies:
        copy.wait()


def second_step(tables, tiles, cheb, own, arrived, scale, u0, cheb_before, u_before):
    args = [*tables, tiles, cheb, own, u0, cheb_before, u_before, *arrived]
    outs = [BLOCKS, BLOCKS_T, OWN_T] + [LETTER] * 4 + [GRADS]
    scratch = [EXT, ACC, ACC_T]
    scratch += [pltpu.VMEM(o.shape, o.dtype) for o in (BLOCKS, BLOCKS_T)]
    scratch += [pltpu.VMEM((4, *LETTER.shape), BF16), pltpu.VMEM(GRADS.shape, BF16)]
    scratch += [pltpu.SemaphoreType.DMA((8,))]
    return call(
        lambda *refs: second_step_kernel(scale, *refs), "second_step", outs, [HBM] * len(outs),
        [SMEM] * 4 + [VMEM] * (len(args) - 4), scratch, 2 * STEP_FLOPS, args,
    )


def end_kernel(target, source, count, send, tiles, filters, *refs):
    sources, (out, grad_out), stages = refs[:11], refs[11:13], refs[13:24]
    sem, ext, acc, total = refs[24:]
    copies = [pltpu.make_async_copy(a, b, sem.at[k]) for k, (a, b) in enumerate(zip(sources, stages))]
    for copy in copies:
        copy.start()
    arrived, own, c2, u1, u2, u0, c1, c0 = stages[:4], *stages[4:]
    for copy in copies[:9]:
        copy.wait()
    gather_terms(send, own, arrived, total)
    for b in range(NB):
        u3 = (2.0 * total[b] - u1[b].astype(F32)).astype(BF16)
        grad = mm(filters[0], u0[b]) + mm(filters[1], u1[b])
        grad = grad + mm(filters[2], u2[b]) + mm(filters[3], u3)
        grad_out[b] = grad.T.astype(BF16)
    apply_forward(target, source, count, tiles, c2, arrived, ext, acc)
    for copy in copies[9:]:
        copy.wait()
    for b in range(NB):
        c3 = (2.0 * acc[b] - c1[b].astype(F32)).astype(BF16)
        result = mm(c0[b], filters[0]) + mm(c1[b], filters[1])
        result = result + mm(c2[b], filters[2]) + mm(c3, filters[3])
        out[b] = result.astype(BF16)


END_FLOPS = 30 * STEP_FLOPS


def end(tables, tiles, filters, chebs, us, own, arrived):
    (c0, c1, c2), (u0, u1, u2) = chebs, us
    sources = (*arrived, own, c2, u1, u2, u0, c1, c0)
    args = (*tables, tiles, filters, *sources)
    scratch = [pltpu.VMEM(a.shape, a.dtype) for a in sources]
    scratch += [pltpu.SemaphoreType.DMA((len(sources),))]
    scratch += [EXT, ACC, pltpu.VMEM((NB, C, BLK), F32)]
    return call(
        end_kernel, "end", [BLOCKS, BLOCKS], [VMEM] * 2,
        [SMEM] * 4 + [VMEM] * 2 + [HBM] * len(sources), scratch, END_FLOPS, args,
    )


def trade(letters):
    size = lax.axis_size("sky")
    got = []
    for letter, kind in zip(letters, ROUNDS):
        pairs = [(i, partner_of(i, kind)) for i in range(size)]
        pairs = [(i, j) for i, j in pairs if 0 <= j < size]
        got.append(lax.ppermute(letter, "sky", pairs))
    return got


def fold_kernel(parts, out):
    groups = parts.shape[0] // 16
    total = parts[0:16].astype(F32)
    for g in range(1, groups):
        total = total + parts[16 * g : 16 * (g + 1)].astype(F32)
    for shift in (8, 4, 2):
        total = total + pltpu.roll(total, shift, axis=0)
    for g in range(groups):
        out[16 * g : 16 * (g + 1)] = total.astype(BF16)


def total_over_devices(local):
    axes = ("view", "sky")
    count = lax.axis_size("view") * lax.axis_size("sky")
    assert local.shape[0] == 2 * count
    parts = lax.all_to_all(local.reshape(count, 2, C), axes, 0, 0, tiled=True)
    whole = call(
        fold_kernel, "fold", [GRADS], [VMEM], [VMEM], [], END_FLOPS, (parts.reshape(local.shape),)
    )[0]
    whole = lax.all_to_all(whole.reshape(count, 2, C), axes, 0, 0, tiled=True)
    return whole.reshape(4, C, C).astype(F32)


def per_device(
    pixels, cotangent, filters, lap_tiles, tile_target, tile_source, tile_count, send_blocks
):
    c0 = pixels.reshape(NB, BLK, C)
    upstream = cotangent.reshape(NB, BLK, C)
    tiles = lap_tiles.reshape(MAXT, BLK, BLK)
    tables = (tile_target, tile_source, tile_count, send_blocks)
    scale = 1.0 / math.sqrt(lax.axis_size("view") * lax.axis_size("sky") * NB * BLK)

    u0, own, *letters = start(tables, tiles, c0, upstream)
    arrived = trade(letters)
    c1, u1, own, *letters = first_step(tables, tiles, c0, own, arrived)
    arrived = trade(letters)
    c2, u2, own, *letters, local = second_step(tables, tiles, c1, own, arrived, scale, u0, c0, u1)
    filter_grad = total_over_devices(local)
    arrived = trade(letters)
    outputs, pixel_grad = end(tables, tiles, filters, (c0, c1, c2), (u0, u1, u2), own, arrived)
    return (outputs.reshape(pixels.shape), pixel_grad.reshape(pixels.shape), filter_grad)


def solution(mesh):
    return jax.shard_map(
        per_device,
        mesh=mesh,
        in_specs=(
            P("view", "sky", None),
            P("view", "sky", None),
            P(),
            P("sky", None, None, None),
            P("sky", None),
            P("sky", None),
            P("sky"),
            P("sky", None, None),
        ),
        out_specs=(P("view", "sky", None), P("view", "sky", None), P()),
        check_vma=False,
    )
```

time: 556 us -> 114 us (0.21)
  waiting for transfers between devices: 295 us -> 44.7 us
  local copies, waits for them, and re-layouts: 95.7 us -> 1.54 us
  matrix products: 64.3 us -> 0 us
  starting transfers between devices: 77 us -> 47.3 us
  Pallas kernels: 0 us -> 17.7 us
  between operations: 15.5 us -> 1.66 us
    psum x1 -> x0, waiting for transfers between devices: 288 us -> none  [per_device(): stacked = lax.psum(jnp.stack(grad_terms), ('view', 'sky'))]
    dot_general x36 -> x0, matrix products: 64.3 us -> none  [the longest x6 21 us: tile_products(): jnp.einsum(contraction, tile_set, picked, preferred_element_type=jnp.floa...]
    ppermute x24 -> x12, starting transfers between devices: 77 us -> 16.9 us  [trade(): got.append(lax.ppermute(letter, 'sky', pairs))]
    gather x26 -> x0, local copies, waits for them, and re-layouts: 45.9 us -> none  [the longest x20 26.8 us: forward_pieces(): return [blocks[chosen[number]] for number in range(4)]]
    all_to_all x0 -> x2, starting transfers between devices: none -> 30.5 us  [the longest x1 17.4 us: total_over_devices(): parts = lax.all_to_all(local.reshape(count, 2, C), axes, 0, 0, tiled=True)]
    ppermute x24 -> x12, waiting for transfers between devices: 7.37 us -> 30.7 us  [trade(): got.append(lax.ppermute(letter, 'sky', pairs))]
    concatenate x5 -> x0, local copies, waits for them, and re-layouts: 18.5 us -> none  [forward_finish(): extended = jnp.concatenate([blocks] + arrived, axis=0)]
    pallas_call x0 -> x5, Pallas kernels: none -> 17.7 us  [call(): pl.pallas_call(kernel, name=name, out_shape=outs, in_specs=in_specs, out_...]
  transfers between devices with their start and end apart: 25 -> 14, of which waited for: 3 -> 6; matrix products, arithmetic and copies ran while one was open for 17% -> 0% of each run, Pallas kernels for 0% -> 6%
where the time goes in v3:
time: 114 us
  starting transfers between devices  47.3 us (41%)
  waiting for transfers between devices  44.7 us (39%)
  Pallas kernels  17.7 us (16%)
  between operations  1.66 us (1%)
  local copies, waits for them, and re-layouts  1.54 us (1%)
    ppermute x12, waiting for transfers between devices, trade(): got.append(lax.ppermute(letter, 'sky', pairs))  30.7 us
    pallas_call x5, Pallas kernels, call(): pl.pallas_call(kernel, name=name, out_shape=outs, in_specs=in_specs, out_...  17.7 us
    all_to_all x1, starting transfers between devices, total_over_devices(): parts = lax.all_to_all(local.reshape(count, 2, C), axes, 0, 0, tiled=True)  17.4 us
    ppermute x12, starting transfers between devices, trade(): got.append(lax.ppermute(letter, 'sky', pairs))  16.9 us
    all_to_all x1, starting transfers between devices, total_over_devices(): whole = lax.all_to_all(whole.reshape(count, 2, C), axes, 0, 0, tiled=True)  13.1 us
    all_to_all x1, waiting for transfers between devices, total_over_devices(): parts = lax.all_to_all(local.reshape(count, 2, C), axes, 0, 0, tiled=True)  7.06 us
    all_to_all x1, waiting for transfers between devices, total_over_devices(): whole = lax.all_to_all(whole.reshape(count, 2, C), axes, 0, 0, tiled=True)  6.97 us
  transfers between devices with their start and end apart: 14, of which 6 were waited for; matrix products, arithmetic and copies ran while one was open for 0% of the time, Pallas kernels for 6%

profile of v3, /device:TPU:1, one launch (start us, length us, event | category | flops | bytes accessed | tf_op | source)
XLA Modules:
  0.0 113.7 jit_solution(17738266722438727218)
XLA Ops:
  0.6 0.0 copy-start.7
  0.6 0.0 copy-start.6
  0.7 0.0 copy-start
  1.5 1.5 %copy.14.send_in.refs_3_.send = s32[1,4,2]{2,1,0:T(4,128)} copy(s32[1,4,2]{1,2,0:T(2,128)} %param.15) | data formatting | bytes 64 | tf_op args[7]
  3.0 3.4 %start.1 = (bf16[8,128,256]{2,1,0:T(8,128)(2,1)S(1)}, f32[8,128,256]{2,1,0:T(8,128)S(1)}, bf16[4,256,128]{2,1,0:T(8,128)(2,1)S(1)}, bf16[4,256,128]{2,1,0:T(8,12...) custom-call(s32[1]{0:T(128)S(6)} %copy.15.count.refs_2_, s32[1,24]{1,0:T(1,128)} %target.1, ...), custom_call_target="tpu_custom_call" | custom-call | flops 402653184 | bytes 6815972 | tf_op jit(solution)/shard_map/start/pallas_call | solution.py:55
  6.4 3.8 %collective-permute-start = (bf16[4,256,128]{2,1,0:T(8,128)(2,1)S(1)}, bf16[4,256,128]{2,1,0:T(8,128)(2,1)S(1)}, u32[]{:S(2)}, u32[]{:S(2)}) collective-permute-start(bf16[4,256,128]{2,1,0:T(8,128)(2,1)S(1)} %get-tuple-element.27), channel_id=1, source_target_pairs={{0,2},{1,3},{2,0},{3,1},{4,6},{5,7},{6,4},{7,5},{8,10},{9,11},{10,... | collective-permute-start | bytes 786440 | tf_op jit(solution)/shard_map/ppermute | solution.py:324
  10.3 0.4 collective-permute-start.1
  10.7 0.7 collective-permute-start.2
  11.3 0.7 collective-permute-start.3
  12.0 3.2 %collective-permute-done.refs_7_ = bf16[4,256,128]{2,1,0:T(8,128)(2,1)S(1)} collective-permute-done((bf16[4,256,128]{2,1,0:T(8,128)(2,1)S(1)}, bf16[4,256,128]{2,1,0:T(8,128)(2,1)S(1)}, u32[]{:S(2)}, u32[]{:S(2)}) %collective-permute-start) | collective-permute-done | bytes 262176 | tf_op jit(solution)/shard_map/ppermute | solution.py:324
  15.2 12.4 %collective-permute-done.1.refs_8_ = bf16[4,256,128]{2,1,0:T(8,128)(2,1)S(1)} collective-permute-done((bf16[4,256,128]{2,1,0:T(8,128)(2,1)S(1)}, bf16[4,256,128]{2,1,0:T(8,128)(2,1)S(1)}, u32[]{:S(2)}, u32[]{:S(2)}) %collective-permute-start.1) | collective-permute-done | bytes 262176 | tf_op jit(solution)/shard_map/ppermute | solution.py:324
  27.6 0.0 collective-permute-done.2.refs_9_
  27.6 0.0 collective-permute-done.3.refs_10_
  27.7 2.6 %first_step.1 = (bf16[8,256,128]{2,1,0:T(8,128)(2,1)S(1)}, bf16[8,128,256]{2,1,0:T(8,128)(2,1)S(1)}, f32[8,128,256]{2,1,0:T(8,128)S(1)}, bf16[4,256,128]{2,1,0:T...) custom-call(s32[1,24]{1,0:T(1,128)S(1)} %copy-done.6, ...), custom_call_target="tpu_custom_call" | custom-call | flops 805306368 | bytes 8913124 | tf_op jit(solution)/shard_map/first_step/pallas_call | solution.py:55
  30.3 3.9 %collective-permute-start.4 = (bf16[4,256,128]{2,1,0:T(8,128)(2,1)S(1)}, bf16[4,256,128]{2,1,0:T(8,128)(2,1)S(1)}, u32[]{:S(2)}, u32[]{:S(2)}) collective-permute-start(bf16[4,256,128]{2,1,0:T(8,128)(2,1)S(1)} %get-tuple-element.35), channel_id=1, source_target_pairs={{0,2},{1,3},{2,0},{3,1},{4,6},{5,7},{6,4},{7,5},{8,10},{9,11},{10,... | collective-permute-start | bytes 786440 | tf_op jit(solution)/shard_map/ppermute | solution.py:324
  34.2 0.0 collective-permute-start.5
  34.2 0.7 collective-permute-start.6
  34.9 0.7 collective-permute-start.7
  35.6 9.3 %collective-permute-done.4.refs_10_ = bf16[4,256,128]{2,1,0:T(8,128)(2,1)S(1)} collective-permute-done((bf16[4,256,128]{2,1,0:T(8,128)(2,1)S(1)}, bf16[4,256,128]{2,1,0:T(8,128)(2,1)S(1)}, u32[]{:S(2)}, u32[]{:S(2)}) %collective-permute-start.4) | collective-permute-done | bytes 262176 | tf_op jit(solution)/shard_map/ppermute | solution.py:324
  44.9 5.8 %collective-permute-done.5.refs_11_ = bf16[4,256,128]{2,1,0:T(8,128)(2,1)S(1)} collective-permute-done((bf16[4,256,128]{2,1,0:T(8,128)(2,1)S(1)}, bf16[4,256,128]{2,1,0:T(8,128)(2,1)S(1)}, u32[]{:S(2)}, u32[]{:S(2)}) %collective-permute-start.5) | collective-permute-done | bytes 262176 | tf_op jit(solution)/shard_map/ppermute | solution.py:324
  50.7 4.8 %second_step.1 = (bf16[8,256,128]{2,1,0:T(8,128)(2,1)}, bf16[8,128,256]{2,1,0:T(8,128)(2,1)}, f32[8,128,256]{2,1,0:T(8,128)}, bf16[4,256,128]{2,1,0:T(8,128)(2,1...) custom-call(s32[1,24]{1,0:T(1,128)S(1)} %copy-done.6, ...), custom_call_target="tpu_custom_call" | custom-call | flops 805306368 | bytes 10617060 | tf_op jit(solution)/shard_map/second_step/pallas_call | solution.py:55
  55.6 17.4 %all-to-all-start = ((bf16[256,2,128]{2,1,0:T(2,128)(2,1)}), bf16[256,2,128]{2,1,0:T(2,128)(2,1)S(1)}, u32[]{:S(2)}, u32[]{:S(2)}) async-start(bf16[256,2,128]{2,1,0:T(2,128)(2,1)} %bitcast.23), calls=%async_computation | async-start | bytes 262144 | tf_op jit(solution)/shard_map/all_to_all | solution.py:343
  73.0 3.0 %collective-permute-start.8 = (bf16[4,256,128]{2,1,0:T(8,128)(2,1)}, bf16[4,256,128]{2,1,0:T(8,128)(2,1)}, u32[]{:S(2)}, u32[]{:S(2)}) collective-permute-start(bf16[4,256,128]{2,1,0:T(8,128)(2,1)} %get-tuple-element.39), channel_id=1, source_target_pairs={{0,2},{1,3},{2,0},{3,1},{4,6},{5,7},{6,4},{7,5},{8,10},{9,11},{10,... | collective-permute-start | bytes 786440 | tf_op jit(solution)/shard_map/ppermute | solution.py:324
  76.0 0.3 collective-permute-start.9
  76.3 1.4 %collective-permute-start.10 = (bf16[4,256,128]{2,1,0:T(8,128)(2,1)}, bf16[4,256,128]{2,1,0:T(8,128)(2,1)}, u32[]{:S(2)}, u32[]{:S(2)}) collective-permute-start(bf16[4,256,128]{2,1,0:T(8,128)(2,1)} %get-tuple-element.41), channel_id=1, source_target_pairs={{2,4},{3,5},{4,2},{5,3},{6,8},{7,9},{8,6},{9,7},{10,12},{11,13},{1... | collective-permute-start | bytes 786440 | tf_op jit(solution)/shard_map/ppermute | solution.py:324
  77.6 1.4 %collective-permute-start.11 = (bf16[4,256,128]{2,1,0:T(8,128)(2,1)}, bf16[4,256,128]{2,1,0:T(8,128)(2,1)}, u32[]{:S(2)}, u32[]{:S(2)}) collective-permute-start(bf16[4,256,128]{2,1,0:T(8,128)(2,1)} %get-tuple-element.42), channel_id=1, source_target_pairs={{1,2},{2,1},{3,4},{4,3},{5,6},{6,5},{7,8},{8,7},{9,10},{10,9},{11,... | collective-permute-start | bytes 786440 | tf_op jit(solution)/shard_map/ppermute | solution.py:324
  79.0 7.1 %all-to-all-done = bf16[256,2,128]{2,1,0:T(2,128)(2,1)S(1)} async-done(((bf16[256,2,128]{2,1,0:T(2,128)(2,1)}), bf16[256,2,128]{2,1,0:T(2,128)(2,1)S(1)}, u32[]{:S(2)}, u32[]{:S(2)}) %all-to-all-start) | async-done | bytes 131104 | tf_op jit(solution)/shard_map/all_to_all | solution.py:343
  86.1 0.7 fold.1
  86.8 13.1 %all-to-all-start.1 = ((bf16[256,2,128]{2,1,0:T(2,128)(2,1)}), bf16[256,2,128]{2,1,0:T(2,128)(2,1)S(1)}, u32[]{:S(2)}, u32[]{:S(2)}) async-start(bf16[256,2,128]{2,1,0:T(2,128)(2,1)} %bitcast.7), calls=%async_computation.1 | async-start | bytes 262144 | tf_op jit(solution)/shard_map/all_to_all | solution.py:347
  99.9 6.1 %end.1 = (bf16[8,256,128]{2,1,0:T(8,128)(2,1)}, bf16[8,256,128]{2,1,0:T(8,128)(2,1)}) custom-call(s32[1,24]{1,0:T(1,128)S(1)} %copy-done.6, s32[1,24]{1,0:T(1,128)S(1)} %copy-done.7, s32[1]{0:T(128)S(6)} %copy.15.count.refs_2_, s32[1,4,2]{2,1,0:T(4,128)S(1)} %copy-done.5, bf16[24,256,256]{2,1,0:T(8,128)(2,1)S(1)} %bitcast.15, ...), custom_call_target="tpu_custom_call" | custom-call | flops 12079595520 | bytes 9568484 | tf_op jit(solution)/shard_map/end/pallas_call | solution.py:55
  106.0 7.0 %all-to-all-done.1 = bf16[256,2,128]{2,1,0:T(2,128)(2,1)S(1)} async-done(((bf16[256,2,128]{2,1,0:T(2,128)(2,1)}), bf16[256,2,128]{2,1,0:T(2,128)(2,1)S(1)}, u32[]{:S(2)}, u32[]{:S(2)}) %all-to-all-start.1) | async-done | bytes 131104 | tf_op jit(solution)/shard_map/all_to_all | solution.py:347
  113.0 0.7 bitcast_convert_fusion
  (21 shorter events, 0.0 us)
Async XLA Ops:
  0.6 27.0 %copy-start.7 = (s32[1,24]{1,0:T(1,128)S(1)}, s32[1,24]{1,0:T(1,128)}, u32[]{:S(2)}) copy-start(s32[1,24]{1,0:T(1,128)} %source.1) | copy-start | bytes 292
  0.6 27.0 %copy-start.6 = (s32[1,24]{1,0:T(1,128)S(1)}, s32[1,24]{1,0:T(1,128)}, u32[]{:S(2)}) copy-start(s32[1,24]{1,0:T(1,128)} %target.1) | copy-start | bytes 292
  0.7 27.0 %copy-start = (bf16[1,24,256,256]{3,2,1,0:T(8,128)(2,1)S(1)}, bf16[1,24,256,256]{3,2,1,0:T(8,128)(2,1)}, u32[]{:S(2)}) copy-start(bf16[1,24,256,256]{3,2,1,0:T(8,128)(2,1)} %param.11) | copy-start | bytes 9437188
  3.0 24.7 %copy-start.1 = (bf16[1,2048,128]{2,1,0:T(8,128)(2,1)S(1)}, bf16[1,2048,128]{2,1,0:T(8,128)(2,1)}, u32[]{:S(2)}) copy-start(bf16[1,2048,128]{2,1,0:T(8,128)(2,1)} %param.8) | copy-start | bytes 1572868
  3.0 24.7 %copy-start.5 = (s32[1,4,2]{2,1,0:T(4,128)S(1)}, s32[1,4,2]{2,1,0:T(4,128)}, u32[]{:S(2)}) copy-start(s32[1,4,2]{2,1,0:T(4,128)} %copy.14.send_in.refs_3_.send) | copy-start | bytes 100
  6.4 49.1 %copy-start.2 = (bf16[8,128,256]{2,1,0:T(8,128)(2,1)}, bf16[8,128,256]{2,1,0:T(8,128)(2,1)S(1)}, u32[]{:S(2)}) copy-start(bf16[8,128,256]{2,1,0:T(8,128)(2,1)S(1)} %get-tuple-element.33.refs_7_.refs_8_) | copy-start | bytes 1572868
  6.4 8.8 %collective-permute-start = (bf16[4,256,128]{2,1,0:T(8,128)(2,1)S(1)}, bf16[4,256,128]{2,1,0:T(8,128)(2,1)S(1)}, u32[]{:S(2)}, u32[]{:S(2)}) collective-permute-start(bf16[4,256,128]{2,1,0:T(8,128)(2,1)S(1)} %get-tuple-element.27), channel_id=1, source_target_pairs={{0,2},{1,3},{2,0},{3,1},{4,6},{5,7},{6,4},{7,5},{8,10},{9,11},{10,... | collective-permute-start | bytes 786440 | tf_op jit(solution)/shard_map/ppermute | solution.py:324
  10.3 17.3 %collective-permute-start.1 = (bf16[4,256,128]{2,1,0:T(8,128)(2,1)S(1)}, bf16[4,256,128]{2,1,0:T(8,128)(2,1)S(1)}, u32[]{:S(2)}, u32[]{:S(2)}) collective-permute-start(bf16[4,256,128]{2,1,0:T(8,128)(2,1)S(1)} %get-tuple-element.28), channel_id=1, source_target_pairs={{0,1},{1,0},{2,3},{3,2},{4,5},{5,4},{6,7},{7,6},{8,9},{9,8},{10,11... | collective-permute-start | bytes 786440 | tf_op jit(solution)/shard_map/ppermute | solution.py:324
  10.7 16.9 %collective-permute-start.2 = (bf16[4,256,128]{2,1,0:T(8,128)(2,1)S(1)}, bf16[4,256,128]{2,1,0:T(8,128)(2,1)S(1)}, u32[]{:S(2)}, u32[]{:S(2)}) collective-permute-start(bf16[4,256,128]{2,1,0:T(8,128)(2,1)S(1)} %get-tuple-element.29), channel_id=1, source_target_pairs={{2,4},{3,5},{4,2},{5,3},{6,8},{7,9},{8,6},{9,7},{10,12},{11,13},{1... | collective-permute-start | bytes 786440 | tf_op jit(solution)/shard_map/ppermute | solution.py:324
  11.3 16.3 %collective-permute-start.3 = (bf16[4,256,128]{2,1,0:T(8,128)(2,1)S(1)}, bf16[4,256,128]{2,1,0:T(8,128)(2,1)S(1)}, u32[]{:S(2)}, u32[]{:S(2)}) collective-permute-start(bf16[4,256,128]{2,1,0:T(8,128)(2,1)S(1)} %get-tuple-element.30), channel_id=1, source_target_pairs={{1,2},{2,1},{3,4},{4,3},{5,6},{6,5},{7,8},{8,7},{9,10},{10,9},{11,... | collective-permute-start | bytes 786440 | tf_op jit(solution)/shard_map/ppermute | solution.py:324
  30.3 25.2 %copy-start.3 = (bf16[8,256,128]{2,1,0:T(8,128)(2,1)}, bf16[8,256,128]{2,1,0:T(8,128)(2,1)S(1)}, u32[]{:S(2)}) copy-start(bf16[8,256,128]{2,1,0:T(8,128)(2,1)S(1)} %get-tuple-element.31.refs_5_.refs_9_) | copy-start | bytes 1572868
  30.3 25.2 %copy-start.4 = (bf16[8,128,256]{2,1,0:T(8,128)(2,1)}, bf16[8,128,256]{2,1,0:T(8,128)(2,1)S(1)}, u32[]{:S(2)}) copy-start(bf16[8,128,256]{2,1,0:T(8,128)(2,1)S(1)} %get-tuple-element.34.refs_9_.refs_6_) | copy-start | bytes 1572868
  30.3 14.6 %collective-permute-start.4 = (bf16[4,256,128]{2,1,0:T(8,128)(2,1)S(1)}, bf16[4,256,128]{2,1,0:T(8,128)(2,1)S(1)}, u32[]{:S(2)}, u32[]{:S(2)}) collective-permute-start(bf16[4,256,128]{2,1,0:T(8,128)(2,1)S(1)} %get-tuple-element.35), channel_id=1, source_target_pairs={{0,2},{1,3},{2,0},{3,1},{4,6},{5,7},{6,4},{7,5},{8,10},{9,11},{10,... | collective-permute-start | bytes 786440 | tf_op jit(solution)/shard_map/ppermute | solution.py:324
  34.2 16.5 %collective-permute-start.5 = (bf16[4,256,128]{2,1,0:T(8,128)(2,1)S(1)}, bf16[4,256,128]{2,1,0:T(8,128)(2,1)S(1)}, u32[]{:S(2)}, u32[]{:S(2)}) collective-permute-start(bf16[4,256,128]{2,1,0:T(8,128)(2,1)S(1)} %get-tuple-element.36), channel_id=1, source_target_pairs={{0,1},{1,0},{2,3},{3,2},{4,5},{5,4},{6,7},{7,6},{8,9},{9,8},{10,11... | collective-permute-start | bytes 786440 | tf_op jit(solution)/shard_map/ppermute | solution.py:324
  34.2 16.5 %collective-permute-start.6 = (bf16[4,256,128]{2,1,0:T(8,128)(2,1)S(1)}, bf16[4,256,128]{2,1,0:T(8,128)(2,1)S(1)}, u32[]{:S(2)}, u32[]{:S(2)}) collective-permute-start(bf16[4,256,128]{2,1,0:T(8,128)(2,1)S(1)} %get-tuple-element.37), channel_id=1, source_target_pairs={{2,4},{3,5},{4,2},{5,3},{6,8},{7,9},{8,6},{9,7},{10,12},{11,13},{1... | collective-permute-start | bytes 786440 | tf_op jit(solution)/shard_map/ppermute | solution.py:324
  34.9 15.8 %collective-permute-start.7 = (bf16[4,256,128]{2,1,0:T(8,128)(2,1)S(1)}, bf16[4,256,128]{2,1,0:T(8,128)(2,1)S(1)}, u32[]{:S(2)}, u32[]{:S(2)}) collective-permute-start(bf16[4,256,128]{2,1,0:T(8,128)(2,1)S(1)} %get-tuple-element.38), channel_id=1, source_target_pairs={{1,2},{2,1},{3,4},{4,3},{5,6},{6,5},{7,8},{8,7},{9,10},{10,9},{11,... | collective-permute-start | bytes 786440 | tf_op jit(solution)/shard_map/ppermute | solution.py:324
  55.6 30.5 %all-to-all-start = ((bf16[256,2,128]{2,1,0:T(2,128)(2,1)}), bf16[256,2,128]{2,1,0:T(2,128)(2,1)S(1)}, u32[]{:S(2)}, u32[]{:S(2)}) async-start(bf16[256,2,128]{2,1,0:T(2,128)(2,1)} %bitcast.23), calls=%async_computation | async-start | bytes 262144 | tf_op jit(solution)/shard_map/all_to_all | solution.py:343
  73.0 26.9 %collective-permute-start.8 = (bf16[4,256,128]{2,1,0:T(8,128)(2,1)}, bf16[4,256,128]{2,1,0:T(8,128)(2,1)}, u32[]{:S(2)}, u32[]{:S(2)}) collective-permute-start(bf16[4,256,128]{2,1,0:T(8,128)(2,1)} %get-tuple-element.39), channel_id=1, source_target_pairs={{0,2},{1,3},{2,0},{3,1},{4,6},{5,7},{6,4},{7,5},{8,10},{9,11},{10,... | collective-permute-start | bytes 786440 | tf_op jit(solution)/shard_map/ppermute | solution.py:324
  76.0 23.9 %collective-permute-start.9 = (bf16[4,256,128]{2,1,0:T(8,128)(2,1)}, bf16[4,256,128]{2,1,0:T(8,128)(2,1)}, u32[]{:S(2)}, u32[]{:S(2)}) collective-permute-start(bf16[4,256,128]{2,1,0:T(8,128)(2,1)} %get-tuple-element.40), channel_id=1, source_target_pairs={{0,1},{1,0},{2,3},{3,2},{4,5},{5,4},{6,7},{7,6},{8,9},{9,8},{10,11... | collective-permute-start | bytes 786440 | tf_op jit(solution)/shard_map/ppermute | solution.py:324
  76.3 23.6 %collective-permute-start.10 = (bf16[4,256,128]{2,1,0:T(8,128)(2,1)}, bf16[4,256,128]{2,1,0:T(8,128)(2,1)}, u32[]{:S(2)}, u32[]{:S(2)}) collective-permute-start(bf16[4,256,128]{2,1,0:T(8,128)(2,1)} %get-tuple-element.41), channel_id=1, source_target_pairs={{2,4},{3,5},{4,2},{5,3},{6,8},{7,9},{8,6},{9,7},{10,12},{11,13},{1... | collective-permute-start | bytes 786440 | tf_op jit(solution)/shard_map/ppermute | solution.py:324
  77.6 22.2 %collective-permute-start.11 = (bf16[4,256,128]{2,1,0:T(8,128)(2,1)}, bf16[4,256,128]{2,1,0:T(8,128)(2,1)}, u32[]{:S(2)}, u32[]{:S(2)}) collective-permute-start(bf16[4,256,128]{2,1,0:T(8,128)(2,1)} %get-tuple-element.42), channel_id=1, source_target_pairs={{1,2},{2,1},{3,4},{4,3},{5,6},{6,5},{7,8},{8,7},{9,10},{10,9},{11,... | collective-permute-start | bytes 786440 | tf_op jit(solution)/shard_map/ppermute | solution.py:324
  86.1 13.8 %copy-start.8 = (bf16[4,128,128]{2,1,0:T(8,128)(2,1)S(1)}, bf16[4,128,128]{2,1,0:T(8,128)(2,1)}, u32[]{:S(2)}) copy-start(bf16[4,128,128]{2,1,0:T(8,128)(2,1)} %filters.1) | copy-start | bytes 393220
  86.8 26.2 %all-to-all-start.1 = ((bf16[256,2,128]{2,1,0:T(2,128)(2,1)}), bf16[256,2,128]{2,1,0:T(2,128)(2,1)S(1)}, u32[]{:S(2)}, u32[]{:S(2)}) async-start(bf16[256,2,128]{2,1,0:T(2,128)(2,1)} %bitcast.7), calls=%async_computation.1 | async-start | bytes 262144 | tf_op jit(solution)/shard_map/all_to_all | solution.py:347

commit v4 on v3

--- a/solution.py
+++ b/solution.py
@@ -5,6 +5,7 @@
 from jax import lax
 from jax.experimental import pallas as pl
 from jax.experimental.pallas import tpu as pltpu
+from jax.sharding import Mesh
 from jax.sharding import PartitionSpec as P
 
 OFFSETS = (1, -1, 2, -2)
@@ -15,9 +16,11 @@
 HBM = pl.BlockSpec(memory_space=pltpu.HBM)
 NB, BLK, C, MAXT, NSEND = 8, 256, 128, 24, 2
 NEXT = NB + 4 * NSEND
-
-
-ROUNDS = ("A", "C", "B", "D")
+PLANE = 16
+SKY = ("z", "plane")
+
+
+ROUNDS = ("A", "C", "D", "B")
 
 
 def partner_of(device, kind):
@@ -31,7 +34,7 @@
 
 
 def positions():
-    me = lax.axis_index("sky")
+    me = lax.axis_index(SKY)
     high = lax.rem(me, 4) // 2
     odd = lax.rem(me, 2)
     where = {"A": 2 + high, "B": 3 - high, "C": odd, "D": 1 - odd}
@@ -67,6 +70,7 @@
 BLOCKS = jax.ShapeDtypeStruct((NB, BLK, C), BF16)
 BLOCKS_T = jax.ShapeDtypeStruct((NB, C, BLK), BF16)
 OWN_T = jax.ShapeDtypeStruct((NB, C, BLK), F32)
+MAPS, TERMS = pl.ds(0, NSEND), pl.ds(NSEND, NSEND)
 LETTER = jax.ShapeDtypeStruct((2 * NSEND, BLK, C), BF16)
 GRADS = jax.ShapeDtypeStruct((4 * C, C), BF16)
 ACC = pltpu.VMEM((NB + 1, BLK, C), F32)
@@ -75,10 +79,17 @@
 STEP_FLOPS = 2 * MAXT * BLK * BLK * C
 
 
+def turned(block):
+    rows = lax.broadcasted_iota(jnp.int32, (C, C), 0)
+    unit = (rows == lax.broadcasted_iota(jnp.int32, (C, C), 1)).astype(BF16)
+    product = lax.dot_general(unit, block, (((1,), (1,)), ((), ())), preferred_element_type=F32)
+    return product.astype(BF16)
+
+
 def put_blocks(send, blocks, letters):
     for letter, position in zip(letters, positions()):
         for j in range(NSEND):
-            letter[j] = blocks[send[0, position, j]]
+            letter[j] = blocks[send[0, j, position]]
 
 
 def put_terms(acc, letters):
@@ -110,7 +121,7 @@
     total[...] = own[...]
     for letter, position in zip(letters, positions()):
         for j in range(NSEND):
-            block = send[0, position, j]
+            block = send[0, j, position]
             total[block, :, 0:C] += letter[NSEND + j, 0:C].astype(F32)
             total[block, :, C:BLK] += letter[NSEND + j, C:BLK].astype(F32)
 
@@ -144,13 +155,13 @@
     for k, position in enumerate(positions()):
         for j in range(NSEND):
             block_copies.append(
-                copy(base.at[send[0, position, j]], letters[k].at[j], letter_sem.at[k * NSEND + j])
+                copy(base.at[send[0, j, position]], letters[k].at[j], letter_sem.at[k * NSEND + j])
             )
     for one in block_copies:
         one.start()
     map_copy.wait()
     for b in range(NB):
-        u0[b] = upstream[b].astype(F32).T.astype(BF16)
+        u0[b] = turned(upstream[b])
     for g in range(TILE_GROUPS):
         tile_copies[g].wait()
         group = range(g * size, (g + 1) * size)
@@ -185,16 +196,34 @@
 def advance(first, scale, ins, arrived, cheb_out, u_out, letters, grads, scratch, sent):
     target, source, count, send, tiles, cheb, own_in = ins[:7]
     ext, acc, acc_t = scratch
-    apply_forward(target, source, count, tiles, cheb, arrived, ext, acc)
     if not first:
         u0, cheb_before, u_before = ins[7:]
-    for b in range(NB):
-        value = acc[b]
-        if not first:
-            value = 2.0 * value - cheb_before[b].astype(F32)
-        cheb_out[b] = value.astype(BF16)
-    put_blocks(send, cheb_out, letters)
-    sent("forward")
+
+    def adjoint_part():
+        gather_terms(send, own_in, arrived, acc_t.at[pl.ds(0, NB)])
+        for b in range(NB):
+            value = acc_t[b]
+            if not first:
+                value = 2.0 * value - u0[b].astype(F32)
+            u_out[b] = value.astype(BF16)
+        sent("adjoint")
+        acc_t[...] = jnp.zeros_like(acc_t)
+        apply_transposed(target, source, count, tiles, u_out, acc_t)
+        put_terms(acc_t, letters)
+        sent("terms")
+
+    def forward_part():
+        apply_forward(target, source, count, tiles, cheb, arrived, ext, acc)
+        for b in range(NB):
+            value = acc[b]
+            if not first:
+                value = 2.0 * value - cheb_before[b].astype(F32)
+            cheb_out[b] = value.astype(BF16)
+        put_blocks(send, cheb_out, letters)
+        sent("forward")
+
+    for part in (forward_part, adjoint_part) if first else (adjoint_part, forward_part):
+        part()
     if not first:
         g0 = jnp.zeros((C, C), F32)
         g1, g2, g3 = g0, g0, g0
@@ -206,16 +235,6 @@
         for k, grad in enumerate((g0, g1, g2, 2.0 * g3 - g1)):
             grads[k * C : (k + 1) * C] = (scale * grad.T).astype(BF16)
         sent("grads")
-    gather_terms(send, own_in, arrived, acc_t.at[pl.ds(0, NB)])
-    for b in range(NB):
-        value = acc_t[b]
-        if not first:
-            value = 2.0 * value - u0[b].astype(F32)
-        u_out[b] = value.astype(BF16)
-    sent("adjoint")
-    acc_t[...] = jnp.zeros_like(acc_t)
-    apply_transposed(target, source, count, tiles, u_out, acc_t)
-    put_terms(acc_t, letters)
 
 
 def first_step_kernel(*refs):
@@ -246,17 +265,20 @@
         copies[-1].start()
 
     def sent(what):
-        if what == "forward":
+        if what == "adjoint":
+            send_off(u_out, outs[1])
+        elif what == "terms":
+            send_off(scratch[2].at[pl.ds(0, NB)], outs[2])
+            for k in range(4):
+                send_off(letters[k].at[TERMS], outs[3 + k].at[TERMS])
+        elif what == "forward":
             send_off(cheb_out, outs[0])
-        elif what == "grads":
+            for k in range(4):
+                send_off(letters[k].at[MAPS], outs[3 + k].at[MAPS])
+        else:
             send_off(grads, outs[7])
-        else:
-            send_off(u_out, outs[1])
 
     advance(False, scale, ins, arrived, cheb_out, u_out, letters, grads, scratch, sent)
-    for k in range(4):
-        send_off(letters[k], outs[3 + k])
-    send_off(scratch[2].at[pl.ds(0, NB)], outs[2])
     for copy in copies:
         copy.wait()
 
@@ -267,7 +289,7 @@
     scratch = [EXT, ACC, ACC_T]
     scratch += [pltpu.VMEM(o.shape, o.dtype) for o in (BLOCKS, BLOCKS_T)]
     scratch += [pltpu.VMEM((4, *LETTER.shape), BF16), pltpu.VMEM(GRADS.shape, BF16)]
-    scratch += [pltpu.SemaphoreType.DMA((8,))]
+    scratch += [pltpu.SemaphoreType.DMA((12,))]
     return call(
         lambda *refs: second_step_kernel(scale, *refs), "second_step", outs, [HBM] * len(outs),
         [SMEM] * 4 + [VMEM] * (len(args) - 4), scratch, 2 * STEP_FLOPS, args,
@@ -275,28 +297,44 @@
 
 
 def end_kernel(target, source, count, send, tiles, filters, *refs):
-    sources, (out, grad_out), stages = refs[:11], refs[11:13], refs[13:24]
-    sem, ext, acc, total = refs[24:]
+    sources, outs, stages = refs[:11], refs[11:13], refs[13:24]
+    sem, ext, acc, total, ready, out_sem = refs[24:]
     copies = [pltpu.make_async_copy(a, b, sem.at[k]) for k, (a, b) in enumerate(zip(sources, stages))]
     for copy in copies:
         copy.start()
-    arrived, own, c2, u1, u2, u0, c1, c0 = stages[:4], *stages[4:]
-    for copy in copies[:9]:
+    arrived, c2, c1, c0, own, u1, u2, u0 = stages[:4], *stages[4:]
+    written = []
+
+    def write(which, b):
+        half = NB // 2
+        if (b + 1) % half == 0:
+            part = pl.ds(b + 1 - half, half)
+            k = len(written)
+            written.append(
+                pltpu.make_async_copy(ready.at[which, part], outs[which].at[part], out_sem.at[k])
+            )
+            written[k].start()
+
+    for copy in copies[:5]:
         copy.wait()
+    apply_forward(target, source, count, tiles, c2, arrived, ext, acc)
+    for copy in copies[5:]:
+        copy.wait()
+    for b in range(NB):
+        c3 = (2.0 * acc[b] - c1[b].astype(F32)).astype(BF16)
+        result = mm(c0[b], filters[0]) + mm(c1[b], filters[1])
+        result = result + mm(c2[b], filters[2]) + mm(c3, filters[3])
+        ready[0, b] = result.astype(BF16)
+        write(0, b)
     gather_terms(send, own, arrived, total)
     for b in range(NB):
         u3 = (2.0 * total[b] - u1[b].astype(F32)).astype(BF16)
         grad = mm(filters[0], u0[b]) + mm(filters[1], u1[b])
         grad = grad + mm(filters[2], u2[b]) + mm(filters[3], u3)
-        grad_out[b] = grad.T.astype(BF16)
-    apply_forward(target, source, count, tiles, c2, arrived, ext, acc)
-    for copy in copies[9:]:
+        ready[1, b] = grad.T.astype(BF16)
+        write(1, b)
+    for copy in written:
         copy.wait()
-    for b in range(NB):
-        c3 = (2.0 * acc[b] - c1[b].astype(F32)).astype(BF16)
-        result = mm(c0[b], filters[0]) + mm(c1[b], filters[1])
-        result = result + mm(c2[b], filters[2]) + mm(c3, filters[3])
-        out[b] = result.astype(BF16)
 
 
 END_FLOPS = 30 * STEP_FLOPS
@@ -304,47 +342,48 @@
 
 def end(tables, tiles, filters, chebs, us, own, arrived):
     (c0, c1, c2), (u0, u1, u2) = chebs, us
-    sources = (*arrived, own, c2, u1, u2, u0, c1, c0)
+    sources = (*arrived, c2, c1, c0, own, u1, u2, u0)
     args = (*tables, tiles, filters, *sources)
     scratch = [pltpu.VMEM(a.shape, a.dtype) for a in sources]
     scratch += [pltpu.SemaphoreType.DMA((len(sources),))]
     scratch += [EXT, ACC, pltpu.VMEM((NB, C, BLK), F32)]
+    scratch += [pltpu.VMEM((2, *BLOCKS.shape), BF16), pltpu.SemaphoreType.DMA((4,))]
     return call(
-        end_kernel, "end", [BLOCKS, BLOCKS], [VMEM] * 2,
+        end_kernel, "end", [BLOCKS, BLOCKS], [HBM] * 2,
         [SMEM] * 4 + [VMEM] * 2 + [HBM] * len(sources), scratch, END_FLOPS, args,
     )
 
 
 def trade(letters):
-    size = lax.axis_size("sky")
+    size = lax.axis_size(SKY)
     got = []
     for letter, kind in zip(letters, ROUNDS):
         pairs = [(i, partner_of(i, kind)) for i in range(size)]
         pairs = [(i, j) for i, j in pairs if 0 <= j < size]
-        got.append(lax.ppermute(letter, "sky", pairs))
+        got.append(lax.ppermute(letter, SKY, pairs))
     return got
 
 
 def fold_kernel(parts, out):
-    groups = parts.shape[0] // 16
-    total = parts[0:16].astype(F32)
-    for g in range(1, groups):
-        total = total + parts[16 * g : 16 * (g + 1)].astype(F32)
-    for shift in (8, 4, 2):
-        total = total + pltpu.roll(total, shift, axis=0)
-    for g in range(groups):
-        out[16 * g : 16 * (g + 1)] = total.astype(BF16)
+    members, rows = parts.shape[0], parts.shape[1]
+    total = parts[0].astype(F32)
+    for k in range(1, members):
+        total = total + parts[k].astype(F32)
+    total = total.astype(BF16)
+    for k in range(members):
+        out[k] = total
 
 
 def total_over_devices(local):
-    axes = ("view", "sky")
-    count = lax.axis_size("view") * lax.axis_size("sky")
-    assert local.shape[0] == 2 * count
-    parts = lax.all_to_all(local.reshape(count, 2, C), axes, 0, 0, tiled=True)
-    whole = call(
-        fold_kernel, "fold", [GRADS], [VMEM], [VMEM], [], END_FLOPS, (parts.reshape(local.shape),)
-    )[0]
-    whole = lax.all_to_all(whole.reshape(count, 2, C), axes, 0, 0, tiled=True)
+    others = lax.axis_size("view") * lax.axis_size("z")
+    rows = local.shape[0] // PLANE
+    assert others == PLANE and rows % 16 == 0
+    parts = local.reshape(PLANE, rows, C)
+    for axes, flops in ((("plane",), END_FLOPS), (("view", "z"), 0)):
+        parts = lax.all_to_all(parts, axes, 0, 0, tiled=True)
+        shape = jax.ShapeDtypeStruct(parts.shape, BF16)
+        parts = call(fold_kernel, "fold", [shape], [VMEM], [VMEM], [], flops, (parts,))[0]
+    whole = lax.all_to_all(parts, ("plane",), 0, 0, tiled=True)
     return whole.reshape(4, C, C).astype(F32)
 
 
@@ -354,8 +393,8 @@
     c0 = pixels.reshape(NB, BLK, C)
     upstream = cotangent.reshape(NB, BLK, C)
     tiles = lap_tiles.reshape(MAXT, BLK, BLK)
-    tables = (tile_target, tile_source, tile_count, send_blocks)
-    scale = 1.0 / math.sqrt(lax.axis_size("view") * lax.axis_size("sky") * NB * BLK)
+    tables = (tile_target, tile_source, tile_count, send_blocks.swapaxes(1, 2))
+    scale = 1.0 / math.sqrt(lax.axis_size("view") * lax.axis_size(SKY) * NB * BLK)
 
     u0, own, *letters = start(tables, tiles, c0, upstream)
     arrived = trade(letters)
@@ -369,19 +408,21 @@
 
 
 def solution(mesh):
+    views, skies = mesh.devices.shape
+    fine = Mesh(mesh.devices.reshape(views, skies // PLANE, PLANE), ("view", *SKY))
     return jax.shard_map(
         per_device,
-        mesh=mesh,
+        mesh=fine,
         in_specs=(
-            P("view", "sky", None),
-            P("view", "sky", None),
+            P("view", SKY, None),
+            P("view", SKY, None),
             P(),
-            P("sky", None, None, None),
-            P("sky", None),
-            P("sky", None),
-            P("sky"),
-            P("sky", None, None),
+            P(SKY, None, None, None),
+            P(SKY, None),
+            P(SKY, None),
+            P(SKY),
+            P(SKY, None, None),
         ),
-        out_specs=(P("view", "sky", None), P("view", "sky", None), P()),
+        out_specs=(P("view", SKY, None), P("view", SKY, None), P()),
         check_vma=False,
     )

time: 114 us -> 107 us (0.939)
  blocking collectives: 0 us -> 26.4 us
  waiting for transfers between devices: 44.7 us -> 22.7 us
  starting transfers between devices: 47.3 us -> 37.2 us
  local copies, waits for them, and re-layouts: 1.54 us -> 0.04 us
    all_to_all x0 -> x1, blocking collectives: none -> 26.4 us  [total_over_devices(): parts = lax.all_to_all(parts, axes, 0, 0, tiled=True)]
    all_to_all x2, waiting for transfers between devices: 14 us -> 2.02 us  [the longest x1 1.29 us: total_over_devices(): whole = lax.all_to_all(parts, ('plane',), 0, 0, tiled=True)]
    all_to_all x2, starting transfers between devices: 30.5 us -> 19.6 us  [the longest x1 15.7 us: total_over_devices(): parts = lax.all_to_all(parts, axes, 0, 0, tiled=True)]
    ppermute x12, waiting for transfers between devices: 30.7 us -> 20.7 us  [trade(): got.append(lax.ppermute(letter, SKY, pairs))]
    unnamed x19 -> x18, local copies, waits for them, and re-layouts: 1.54 us -> 0.04 us
    pallas_call x5 -> x6, Pallas kernels: 17.7 us -> 16.9 us  [call(): pl.pallas_call(kernel, name=name, out_shape=outs, in_specs=in_specs, out_...]
where the time goes in v4:
time: 107 us; the launch traced here: 106 us
  starting transfers between devices  37.2 us (35%)
  blocking collectives  26.4 us (25%)
  waiting for transfers between devices  22.7 us (21%)
  Pallas kernels  16.9 us (16%)
  between operations  1.68 us (2%)
    all_to_all x1, blocking collectives, total_over_devices(): parts = lax.all_to_all(parts, axes, 0, 0, tiled=True)  26.4 us
    ppermute x12, waiting for transfers between devices, trade(): got.append(lax.ppermute(letter, SKY, pairs))  20.7 us
    ppermute x12, starting transfers between devices, trade(): got.append(lax.ppermute(letter, SKY, pairs))  17.6 us
    pallas_call x6, Pallas kernels, call(): pl.pallas_call(kernel, name=name, out_shape=outs, in_specs=in_specs, out_...  16.9 us
    all_to_all x1, starting transfers between devices, total_over_devices(): parts = lax.all_to_all(parts, axes, 0, 0, tiled=True)  15.7 us
    all_to_all x1, starting transfers between devices, total_over_devices(): whole = lax.all_to_all(parts, ('plane',), 0, 0, tiled=True)  3.82 us
  transfers between devices with their start and end apart: 14, of which 6 were waited for; matrix products, arithmetic and copies ran while one was open for 0% of the time, Pallas kernels for 6%

profile of v4, /device:TPU:1, one launch (start us, length us, event | category | flops | bytes accessed | tf_op | source)
XLA Modules:
  0.0 105.6 jit_solution(12169770256691730260)
XLA Ops:
  0.7 0.0 copy-start.1
  1.5 3.8 %start.1 = (bf16[8,128,256]{2,1,0:T(8,128)(2,1)S(1)}, f32[8,128,256]{2,1,0:T(8,128)S(1)}, bf16[4,256,128]{2,1,0:T(8,128)(2,1)S(1)}, bf16[4,256,128]{2,1,0:T(8,12...) custom-call(s32[1]{0:T(128)S(6)} %copy.11.count.refs_2_, s32[1,24]{1,0:T(1,128)} %target.1, ...), custom_call_target="tpu_custom_call" | custom-call | flops 402653184 | bytes 6815972 | tf_op jit(solution)/shard_map/start/pallas_call | solution.py:58
  5.3 3.8 %collective-permute-start = (bf16[4,256,128]{2,1,0:T(8,128)(2,1)S(1)}, bf16[4,256,128]{2,1,0:T(8,128)(2,1)S(1)}, u32[]{:S(2)}, u32[]{:S(2)}) collective-permute-start(bf16[4,256,128]{2,1,0:T(8,128)(2,1)S(1)} %get-tuple-element.27), channel_id=1, source_target_pairs={{0,2},{1,3},{2,0},{3,1},{4,6},{5,7},{6,4},{7,5},{8,10},{9,11},{10,... | collective-permute-start | bytes 786440 | tf_op jit(solution)/shard_map/ppermute | solution.py:363
  9.1 0.4 collective-permute-start.1
  9.5 0.7 collective-permute-start.2
  10.2 0.7 collective-permute-start.3
  10.9 3.3 %collective-permute-done.refs_7_ = bf16[4,256,128]{2,1,0:T(8,128)(2,1)S(1)} collective-permute-done((bf16[4,256,128]{2,1,0:T(8,128)(2,1)S(1)}, bf16[4,256,128]{2,1,0:T(8,128)(2,1)S(1)}, u32[]{:S(2)}, u32[]{:S(2)}) %collective-permute-start) | collective-permute-done | bytes 262176 | tf_op jit(solution)/shard_map/ppermute | solution.py:363
  14.1 9.5 %collective-permute-done.1.refs_8_ = bf16[4,256,128]{2,1,0:T(8,128)(2,1)S(1)} collective-permute-done((bf16[4,256,128]{2,1,0:T(8,128)(2,1)S(1)}, bf16[4,256,128]{2,1,0:T(8,128)(2,1)S(1)}, u32[]{:S(2)}, u32[]{:S(2)}) %collective-permute-start.1) | collective-permute-done | bytes 262176 | tf_op jit(solution)/shard_map/ppermute | solution.py:363
  23.7 0.0 collective-permute-done.2.refs_9_
  23.7 0.0 collective-permute-done.3.refs_10_
  23.7 2.6 %first_step.1 = (bf16[8,256,128]{2,1,0:T(8,128)(2,1)S(1)}, bf16[8,128,256]{2,1,0:T(8,128)(2,1)S(1)}, f32[8,128,256]{2,1,0:T(8,128)S(1)}, bf16[4,256,128]{2,1,0:T...) custom-call(s32[1,24]{1,0:T(1,128)S(1)} %copy-done.6, ...), custom_call_target="tpu_custom_call" | custom-call | flops 805306368 | bytes 8913124 | tf_op jit(solution)/shard_map/first_step/pallas_call | solution.py:58
  26.4 4.6 %collective-permute-start.4 = (bf16[4,256,128]{2,1,0:T(8,128)(2,1)S(1)}, bf16[4,256,128]{2,1,0:T(8,128)(2,1)S(1)}, u32[]{:S(2)}, u32[]{:S(2)}) collective-permute-start(bf16[4,256,128]{2,1,0:T(8,128)(2,1)S(1)} %get-tuple-element.35), channel_id=1, source_target_pairs={{0,2},{1,3},{2,0},{3,1},{4,6},{5,7},{6,4},{7,5},{8,10},{9,11},{10,... | collective-permute-start | bytes 786440 | tf_op jit(solution)/shard_map/ppermute | solution.py:363
  31.0 0.1 collective-permute-start.5
  31.1 0.7 collective-permute-start.6
  31.7 0.7 collective-permute-start.7
  32.4 2.3 %collective-permute-done.4.refs_10_ = bf16[4,256,128]{2,1,0:T(8,128)(2,1)S(1)} collective-permute-done((bf16[4,256,128]{2,1,0:T(8,128)(2,1)S(1)}, bf16[4,256,128]{2,1,0:T(8,128)(2,1)S(1)}, u32[]{:S(2)}, u32[]{:S(2)}) %collective-permute-start.4) | collective-permute-done | bytes 262176 | tf_op jit(solution)/shard_map/ppermute | solution.py:363
  34.7 5.6 %collective-permute-done.5.refs_11_ = bf16[4,256,128]{2,1,0:T(8,128)(2,1)S(1)} collective-permute-done((bf16[4,256,128]{2,1,0:T(8,128)(2,1)S(1)}, bf16[4,256,128]{2,1,0:T(8,128)(2,1)S(1)}, u32[]{:S(2)}, u32[]{:S(2)}) %collective-permute-start.5) | collective-permute-done | bytes 262176 | tf_op jit(solution)/shard_map/ppermute | solution.py:363
  40.3 0.0 collective-permute-done.7.refs_13_
  40.3 4.4 %second_step.1 = (bf16[8,256,128]{2,1,0:T(8,128)(2,1)}, bf16[8,128,256]{2,1,0:T(8,128)(2,1)}, f32[8,128,256]{2,1,0:T(8,128)}, bf16[4,256,128]{2,1,0:T(8,128)(2,1...) custom-call(s32[1,24]{1,0:T(1,128)S(1)} %copy-done.6, ...), custom_call_target="tpu_custom_call" | custom-call | flops 805306368 | bytes 10617060 | tf_op jit(solution)/shard_map/second_step/pallas_call | solution.py:58
  44.8 15.7 %all-to-all-start = ((bf16[16,32,128]{2,1,0:T(8,128)(2,1)}), bf16[16,32,128]{2,1,0:T(8,128)(2,1)S(1)}, u32[]{:S(2)}, u32[]{:S(2)}) async-start(bf16[16,32,128]{2,1,0:T(8,128)(2,1)} %bitcast.25), calls=%async_computation | async-start | bytes 262144 | tf_op jit(solution)/shard_map/all_to_all | solution.py:383
  60.5 2.9 %collective-permute-start.8 = (bf16[4,256,128]{2,1,0:T(8,128)(2,1)}, bf16[4,256,128]{2,1,0:T(8,128)(2,1)}, u32[]{:S(2)}, u32[]{:S(2)}) collective-permute-start(bf16[4,256,128]{2,1,0:T(8,128)(2,1)} %get-tuple-element.39), channel_id=1, source_target_pairs={{0,2},{1,3},{2,0},{3,1},{4,6},{5,7},{6,4},{7,5},{8,10},{9,11},{10,... | collective-permute-start | bytes 786440 | tf_op jit(solution)/shard_map/ppermute | solution.py:363
  63.4 0.3 collective-permute-start.9
  63.7 1.4 %collective-permute-start.10 = (bf16[4,256,128]{2,1,0:T(8,128)(2,1)}, bf16[4,256,128]{2,1,0:T(8,128)(2,1)}, u32[]{:S(2)}, u32[]{:S(2)}) collective-permute-start(bf16[4,256,128]{2,1,0:T(8,128)(2,1)} %get-tuple-element.41), channel_id=1, source_target_pairs={{1,2},{2,1},{3,4},{4,3},{5,6},{6,5},{7,8},{8,7},{9,10},{10,9},{11,... | collective-permute-start | bytes 786440 | tf_op jit(solution)/shard_map/ppermute | solution.py:363
  65.0 1.5 %collective-permute-start.11 = (bf16[4,256,128]{2,1,0:T(8,128)(2,1)}, bf16[4,256,128]{2,1,0:T(8,128)(2,1)}, u32[]{:S(2)}, u32[]{:S(2)}) collective-permute-start(bf16[4,256,128]{2,1,0:T(8,128)(2,1)} %get-tuple-element.42), channel_id=1, source_target_pairs={{2,4},{3,5},{4,2},{5,3},{6,8},{7,9},{8,6},{9,7},{10,12},{11,13},{1... | collective-permute-start | bytes 786440 | tf_op jit(solution)/shard_map/ppermute | solution.py:363
  66.6 0.7 all-to-all-done.parts
  67.3 26.4 %all_to_all.15.parts = bf16[16,32,128]{2,1,0:T(8,128)(2,1)S(1)} all-to-all(bf16[16,32,128]{2,1,0:T(8,128)(2,1)S(1)} %fold.2), channel_id=1, replica_groups=mesh['view'=2,'z'=8,'plane'=16] {'view','z'}, dimensions={0} | all-to-all | bytes 262144 | tf_op jit(solution)/shard_map/all_to_all | solution.py:383
  93.7 0.7 fold.3
  94.4 3.8 %all-to-all-start.2 = ((bf16[16,32,128]{2,1,0:T(8,128)(2,1)}), bf16[16,32,128]{2,1,0:T(8,128)(2,1)S(1)}, u32[]{:S(2)}, u32[]{:S(2)}) async-start(bf16[16,32,128]{2,1,0:T(8,128)(2,1)} %fold.3), calls=%async_computation.2 | async-start | bytes 262144 | tf_op jit(solution)/shard_map/all_to_all | solution.py:386
  98.2 0.0 collective-permute-done.10.refs_2_
  98.2 5.3 %end.1 = (bf16[8,256,128]{2,1,0:T(8,128)(2,1)}, bf16[8,256,128]{2,1,0:T(8,128)(2,1)}) custom-call(s32[1,24]{1,0:T(1,128)S(1)} %copy-done.6, s32[1,24]{1,0:T(1,128)S(1)} %copy-done.7, s32[1]{0:T(128)S(6)} %copy.11.count.refs_2_, s32[1,2,4]{2,1,0:T(2,128)S(1)} %bitcast.22, bf16[24,256,256]{2,1,0:T(8,128)(2,1)S(1)} %bitcast.14, ...), custom_call_target="tpu_custom_call" | custom-call | flops 12079595520 | bytes 9568484 | tf_op jit(solution)/shard_map/end/pallas_call | solution.py:58
  103.6 1.3 %all-to-all-done.2 = bf16[16,32,128]{2,1,0:T(8,128)(2,1)S(1)} async-done(((bf16[16,32,128]{2,1,0:T(8,128)(2,1)}), bf16[16,32,128]{2,1,0:T(8,128)(2,1)S(1)}, u32[]{:S(2)}, u32[]{:S(2)}) %all-to-all-start.2) | async-done | bytes 131104 | tf_op jit(solution)/shard_map/all_to_all | solution.py:386
  104.9 0.7 bitcast_convert_fusion
  (22 shorter events, 0.1 us)
Async XLA Ops:
  0.6 23.0 %copy-start.7 = (s32[1,24]{1,0:T(1,128)S(1)}, s32[1,24]{1,0:T(1,128)}, u32[]{:S(2)}) copy-start(s32[1,24]{1,0:T(1,128)} %source.1) | copy-start | bytes 292
  0.6 23.0 %copy-start.6 = (s32[1,24]{1,0:T(1,128)S(1)}, s32[1,24]{1,0:T(1,128)}, u32[]{:S(2)}) copy-start(s32[1,24]{1,0:T(1,128)} %target.1) | copy-start | bytes 292
  0.7 23.0 %copy-start.5 = (s32[1,4,2]{1,2,0:T(2,128)S(1)}, s32[1,4,2]{1,2,0:T(2,128)}, u32[]{:S(2)}) copy-start(s32[1,4,2]{1,2,0:T(2,128)} %param.15) | copy-start | bytes 100
  0.7 23.0 %copy-start = (bf16[1,24,256,256]{3,2,1,0:T(8,128)(2,1)S(1)}, bf16[1,24,256,256]{3,2,1,0:T(8,128)(2,1)}, u32[]{:S(2)}) copy-start(bf16[1,24,256,256]{3,2,1,0:T(8,128)(2,1)} %param.11) | copy-start | bytes 9437188
  0.7 23.0 %copy-start.1 = (bf16[1,2048,128]{2,1,0:T(8,128)(2,1)S(1)}, bf16[1,2048,128]{2,1,0:T(8,128)(2,1)}, u32[]{:S(2)}) copy-start(bf16[1,2048,128]{2,1,0:T(8,128)(2,1)} %param.8) | copy-start | bytes 1572868
  5.3 39.5 %copy-start.2 = (bf16[8,128,256]{2,1,0:T(8,128)(2,1)}, bf16[8,128,256]{2,1,0:T(8,128)(2,1)S(1)}, u32[]{:S(2)}) copy-start(bf16[8,128,256]{2,1,0:T(8,128)(2,1)S(1)} %get-tuple-element.33.refs_7_.refs_10_) | copy-start | bytes 1572868
  5.3 8.8 %collective-permute-start = (bf16[4,256,128]{2,1,0:T(8,128)(2,1)S(1)}, bf16[4,256,128]{2,1,0:T(8,128)(2,1)S(1)}, u32[]{:S(2)}, u32[]{:S(2)}) collective-permute-start(bf16[4,256,128]{2,1,0:T(8,128)(2,1)S(1)} %get-tuple-element.27), channel_id=1, source_target_pairs={{0,2},{1,3},{2,0},{3,1},{4,6},{5,7},{6,4},{7,5},{8,10},{9,11},{10,... | collective-permute-start | bytes 786440 | tf_op jit(solution)/shard_map/ppermute | solution.py:363
  9.1 14.5 %collective-permute-start.1 = (bf16[4,256,128]{2,1,0:T(8,128)(2,1)S(1)}, bf16[4,256,128]{2,1,0:T(8,128)(2,1)S(1)}, u32[]{:S(2)}, u32[]{:S(2)}) collective-permute-start(bf16[4,256,128]{2,1,0:T(8,128)(2,1)S(1)} %get-tuple-element.28), channel_id=1, source_target_pairs={{0,1},{1,0},{2,3},{3,2},{4,5},{5,4},{6,7},{7,6},{8,9},{9,8},{10,11... | collective-permute-start | bytes 786440 | tf_op jit(solution)/shard_map/ppermute | solution.py:363
  9.5 14.1 %collective-permute-start.2 = (bf16[4,256,128]{2,1,0:T(8,128)(2,1)S(1)}, bf16[4,256,128]{2,1,0:T(8,128)(2,1)S(1)}, u32[]{:S(2)}, u32[]{:S(2)}) collective-permute-start(bf16[4,256,128]{2,1,0:T(8,128)(2,1)S(1)} %get-tuple-element.29), channel_id=1, source_target_pairs={{1,2},{2,1},{3,4},{4,3},{5,6},{6,5},{7,8},{8,7},{9,10},{10,9},{11,... | collective-permute-start | bytes 786440 | tf_op jit(solution)/shard_map/ppermute | solution.py:363
  10.2 13.5 %collective-permute-start.3 = (bf16[4,256,128]{2,1,0:T(8,128)(2,1)S(1)}, bf16[4,256,128]{2,1,0:T(8,128)(2,1)S(1)}, u32[]{:S(2)}, u32[]{:S(2)}) collective-permute-start(bf16[4,256,128]{2,1,0:T(8,128)(2,1)S(1)} %get-tuple-element.30), channel_id=1, source_target_pairs={{2,4},{3,5},{4,2},{5,3},{6,8},{7,9},{8,6},{9,7},{10,12},{11,13},{1... | collective-permute-start | bytes 786440 | tf_op jit(solution)/shard_map/ppermute | solution.py:363
  26.4 18.4 %copy-start.3 = (bf16[8,256,128]{2,1,0:T(8,128)(2,1)}, bf16[8,256,128]{2,1,0:T(8,128)(2,1)S(1)}, u32[]{:S(2)}) copy-start(bf16[8,256,128]{2,1,0:T(8,128)(2,1)S(1)} %get-tuple-element.31.refs_5_) | copy-start | bytes 1572868
  26.4 18.4 %copy-start.4 = (bf16[8,128,256]{2,1,0:T(8,128)(2,1)}, bf16[8,128,256]{2,1,0:T(8,128)(2,1)S(1)}, u32[]{:S(2)}) copy-start(bf16[8,128,256]{2,1,0:T(8,128)(2,1)S(1)} %get-tuple-element.34.refs_9_.refs_8_) | copy-start | bytes 1572868
  26.4 8.3 %collective-permute-start.4 = (bf16[4,256,128]{2,1,0:T(8,128)(2,1)S(1)}, bf16[4,256,128]{2,1,0:T(8,128)(2,1)S(1)}, u32[]{:S(2)}, u32[]{:S(2)}) collective-permute-start(bf16[4,256,128]{2,1,0:T(8,128)(2,1)S(1)} %get-tuple-element.35), channel_id=1, source_target_pairs={{0,2},{1,3},{2,0},{3,1},{4,6},{5,7},{6,4},{7,5},{8,10},{9,11},{10,... | collective-permute-start | bytes 786440 | tf_op jit(solution)/shard_map/ppermute | solution.py:363
  31.0 9.4 %collective-permute-start.5 = (bf16[4,256,128]{2,1,0:T(8,128)(2,1)S(1)}, bf16[4,256,128]{2,1,0:T(8,128)(2,1)S(1)}, u32[]{:S(2)}, u32[]{:S(2)}) collective-permute-start(bf16[4,256,128]{2,1,0:T(8,128)(2,1)S(1)} %get-tuple-element.36), channel_id=1, source_target_pairs={{0,1},{1,0},{2,3},{3,2},{4,5},{5,4},{6,7},{7,6},{8,9},{9,8},{10,11... | collective-permute-start | bytes 786440 | tf_op jit(solution)/shard_map/ppermute | solution.py:363
  31.1 9.3 %collective-permute-start.6 = (bf16[4,256,128]{2,1,0:T(8,128)(2,1)S(1)}, bf16[4,256,128]{2,1,0:T(8,128)(2,1)S(1)}, u32[]{:S(2)}, u32[]{:S(2)}) collective-permute-start(bf16[4,256,128]{2,1,0:T(8,128)(2,1)S(1)} %get-tuple-element.37), channel_id=1, source_target_pairs={{1,2},{2,1},{3,4},{4,3},{5,6},{6,5},{7,8},{8,7},{9,10},{10,9},{11,... | collective-permute-start | bytes 786440 | tf_op jit(solution)/shard_map/ppermute | solution.py:363
  31.7 8.6 %collective-permute-start.7 = (bf16[4,256,128]{2,1,0:T(8,128)(2,1)S(1)}, bf16[4,256,128]{2,1,0:T(8,128)(2,1)S(1)}, u32[]{:S(2)}, u32[]{:S(2)}) collective-permute-start(bf16[4,256,128]{2,1,0:T(8,128)(2,1)S(1)} %get-tuple-element.38), channel_id=1, source_target_pairs={{2,4},{3,5},{4,2},{5,3},{6,8},{7,9},{8,6},{9,7},{10,12},{11,13},{1... | collective-permute-start | bytes 786440 | tf_op jit(solution)/shard_map/ppermute | solution.py:363
  44.8 22.5 %all-to-all-start = ((bf16[16,32,128]{2,1,0:T(8,128)(2,1)}), bf16[16,32,128]{2,1,0:T(8,128)(2,1)S(1)}, u32[]{:S(2)}, u32[]{:S(2)}) async-start(bf16[16,32,128]{2,1,0:T(8,128)(2,1)} %bitcast.25), calls=%async_computation | async-start | bytes 262144 | tf_op jit(solution)/shard_map/all_to_all | solution.py:383
  60.5 37.7 %collective-permute-start.8 = (bf16[4,256,128]{2,1,0:T(8,128)(2,1)}, bf16[4,256,128]{2,1,0:T(8,128)(2,1)}, u32[]{:S(2)}, u32[]{:S(2)}) collective-permute-start(bf16[4,256,128]{2,1,0:T(8,128)(2,1)} %get-tuple-element.39), channel_id=1, source_target_pairs={{0,2},{1,3},{2,0},{3,1},{4,6},{5,7},{6,4},{7,5},{8,10},{9,11},{10,... | collective-permute-start | bytes 786440 | tf_op jit(solution)/shard_map/ppermute | solution.py:363
  63.4 34.8 %collective-permute-start.9 = (bf16[4,256,128]{2,1,0:T(8,128)(2,1)}, bf16[4,256,128]{2,1,0:T(8,128)(2,1)}, u32[]{:S(2)}, u32[]{:S(2)}) collective-permute-start(bf16[4,256,128]{2,1,0:T(8,128)(2,1)} %get-tuple-element.40), channel_id=1, source_target_pairs={{0,1},{1,0},{2,3},{3,2},{4,5},{5,4},{6,7},{7,6},{8,9},{9,8},{10,11... | collective-permute-start | bytes 786440 | tf_op jit(solution)/shard_map/ppermute | solution.py:363
  63.7 34.5 %collective-permute-start.10 = (bf16[4,256,128]{2,1,0:T(8,128)(2,1)}, bf16[4,256,128]{2,1,0:T(8,128)(2,1)}, u32[]{:S(2)}, u32[]{:S(2)}) collective-permute-start(bf16[4,256,128]{2,1,0:T(8,128)(2,1)} %get-tuple-element.41), channel_id=1, source_target_pairs={{1,2},{2,1},{3,4},{4,3},{5,6},{6,5},{7,8},{8,7},{9,10},{10,9},{11,... | collective-permute-start | bytes 786440 | tf_op jit(solution)/shard_map/ppermute | solution.py:363
  65.0 33.2 %copy-start.8 = (bf16[4,128,128]{2,1,0:T(8,128)(2,1)S(1)}, bf16[4,128,128]{2,1,0:T(8,128)(2,1)}, u32[]{:S(2)}) copy-start(bf16[4,128,128]{2,1,0:T(8,128)(2,1)} %filters.1) | copy-start | bytes 393220
  65.0 33.2 %collective-permute-start.11 = (bf16[4,256,128]{2,1,0:T(8,128)(2,1)}, bf16[4,256,128]{2,1,0:T(8,128)(2,1)}, u32[]{:S(2)}, u32[]{:S(2)}) collective-permute-start(bf16[4,256,128]{2,1,0:T(8,128)(2,1)} %get-tuple-element.42), channel_id=1, source_target_pairs={{2,4},{3,5},{4,2},{5,3},{6,8},{7,9},{8,6},{9,7},{10,12},{11,13},{1... | collective-permute-start | bytes 786440 | tf_op jit(solution)/shard_map/ppermute | solution.py:363
  94.4 10.5 %all-to-all-start.2 = ((bf16[16,32,128]{2,1,0:T(8,128)(2,1)}), bf16[16,32,128]{2,1,0:T(8,128)(2,1)S(1)}, u32[]{:S(2)}, u32[]{:S(2)}) async-start(bf16[16,32,128]{2,1,0:T(8,128)(2,1)} %fold.3), calls=%async_computation.2 | async-start | bytes 262144 | tf_op jit(solution)/shard_map/all_to_all | solution.py:386

commit v5 on v4

--- a/solution.py
+++ b/solution.py
@@ -129,9 +129,9 @@
 TILE_GROUPS = 4
 
 
-def start_kernel(count, target_in, source_in, send_in, tiles_in, base, upstream_in, u0, own, *rest):
+def start_kernel(count, target_in, source_in, send_in, tiles_in, base, upstream_in, u0, own, tiles, *rest):
     letters = rest[:4]
-    target, source, send, tiles, upstream, acc, table_sem, map_sem, tile_sem, letter_sem = rest[4:]
+    target, source, send, upstream, acc, table_sem, map_sem, tile_sem, letter_sem = rest[4:]
     copy = pltpu.make_async_copy
     tables = [
         copy(send_in, send, table_sem.at[0]),
@@ -179,7 +179,6 @@
         pltpu.SMEM(target.shape, jnp.int32),
         pltpu.SMEM(source.shape, jnp.int32),
         pltpu.SMEM(send.shape, jnp.int32),
-        pltpu.VMEM(tiles.shape, BF16),
         pltpu.VMEM(upstream.shape, BF16),
         ACC_T,
         dma((3,)),
@@ -188,7 +187,7 @@
         dma((4 * NSEND,)),
     ]
     return call(
-        start_kernel, "start", [BLOCKS_T, OWN_T] + [LETTER] * 4, [VMEM] * 6,
+        start_kernel, "start", [BLOCKS_T, OWN_T, tiles] + [LETTER] * 4, [VMEM] * 7,
         [SMEM] + [HBM] * 6, scratch, STEP_FLOPS, (count, target, source, send, tiles, base, upstream),
     )
 
@@ -396,7 +395,7 @@
     tables = (tile_target, tile_source, tile_count, send_blocks.swapaxes(1, 2))
     scale = 1.0 / math.sqrt(lax.axis_size("view") * lax.axis_size(SKY) * NB * BLK)
 
-    u0, own, *letters = start(tables, tiles, c0, upstream)
+    u0, own, tiles, *letters = start(tables, tiles, c0, upstream)
     arrived = trade(letters)
     c1, u1, own, *letters = first_step(tables, tiles, c0, own, arrived)
     arrived = trade(letters)

time: 107 us -> 107 us (level)
  no operation moved by 1% of the time
where the time goes in v5:
time: 107 us; the launch traced here: 105 us
  starting transfers between devices  37.2 us (35%)
  blocking collectives  26.4 us (25%)
  waiting for transfers between devices  22.7 us (21%)
  Pallas kernels  16.7 us (16%)
  between operations  1.58 us (1%)
    all_to_all x1, blocking collectives, total_over_devices(): parts = lax.all_to_all(parts, axes, 0, 0, tiled=True)  26.4 us
    ppermute x12, waiting for transfers between devices, trade(): got.append(lax.ppermute(letter, SKY, pairs))  20.7 us
    ppermute x12, starting transfers between devices, trade(): got.append(lax.ppermute(letter, SKY, pairs))  17.6 us
    pallas_call x6, Pallas kernels, call(): pl.pallas_call(kernel, name=name, out_shape=outs, in_specs=in_specs, out_...  16.7 us
    all_to_all x1, starting transfers between devices, total_over_devices(): parts = lax.all_to_all(parts, axes, 0, 0, tiled=True)  15.8 us
    all_to_all x1, starting transfers between devices, total_over_devices(): whole = lax.all_to_all(parts, ('plane',), 0, 0, tiled=True)  3.82 us
  transfers between devices with their start and end apart: 14, of which 6 were waited for; matrix products, arithmetic and copies ran while one was open for 0% of the time, Pallas kernels for 6%

profile of v5, /device:TPU:1, one launch (start us, length us, event | category | flops | bytes accessed | tf_op | source)
XLA Modules:
  0.0 105.3 jit_solution(12604759621581220594)
XLA Ops:
  0.7 0.0 copy-start
  1.4 3.5 %start.1 = (bf16[8,128,256]{2,1,0:T(8,128)(2,1)S(1)}, f32[8,128,256]{2,1,0:T(8,128)S(1)}, bf16[24,256,256]{2,1,0:T(8,128)(2,1)S(1)}, bf16[4,256,128]{2,1,0:T(8,1...) custom-call(s32[1]{0:T(128)S(6)} %copy.11.count.refs_2_, ...), custom_call_target="tpu_custom_call" | custom-call | flops 402653184 | bytes 9961700 | tf_op jit(solution)/shard_map/start/pallas_call | solution.py:58
  4.9 3.8 %collective-permute-start = (bf16[4,256,128]{2,1,0:T(8,128)(2,1)S(1)}, bf16[4,256,128]{2,1,0:T(8,128)(2,1)S(1)}, u32[]{:S(2)}, u32[]{:S(2)}) collective-permute-start(bf16[4,256,128]{2,1,0:T(8,128)(2,1)S(1)} %get-tuple-element.29), channel_id=1, source_target_pairs={{0,2},{1,3},{2,0},{3,1},{4,6},{5,7},{6,4},{7,5},{8,10},{9,11},{10,... | collective-permute-start | bytes 786440 | tf_op jit(solution)/shard_map/ppermute | solution.py:362
  8.7 0.4 collective-permute-start.1
  9.1 0.7 collective-permute-start.2
  9.8 0.7 collective-permute-start.3
  10.5 3.3 %collective-permute-done.refs_7_ = bf16[4,256,128]{2,1,0:T(8,128)(2,1)S(1)} collective-permute-done((bf16[4,256,128]{2,1,0:T(8,128)(2,1)S(1)}, bf16[4,256,128]{2,1,0:T(8,128)(2,1)S(1)}, u32[]{:S(2)}, u32[]{:S(2)}) %collective-permute-start) | collective-permute-done | bytes 262176 | tf_op jit(solution)/shard_map/ppermute | solution.py:362
  13.7 9.5 %collective-permute-done.1.refs_8_ = bf16[4,256,128]{2,1,0:T(8,128)(2,1)S(1)} collective-permute-done((bf16[4,256,128]{2,1,0:T(8,128)(2,1)S(1)}, bf16[4,256,128]{2,1,0:T(8,128)(2,1)S(1)}, u32[]{:S(2)}, u32[]{:S(2)}) %collective-permute-start.1) | collective-permute-done | bytes 262176 | tf_op jit(solution)/shard_map/ppermute | solution.py:362
  23.2 0.0 collective-permute-done.2.refs_9_
  23.3 0.0 collective-permute-done.3.refs_10_
  23.3 2.7 %first_step.1 = (bf16[8,256,128]{2,1,0:T(8,128)(2,1)S(1)}, bf16[8,128,256]{2,1,0:T(8,128)(2,1)S(1)}, f32[8,128,256]{2,1,0:T(8,128)S(1)}, bf16[4,256,128]{2,1,0:T...) custom-call(s32[1,24]{1,0:T(1,128)S(1)} %copy-done.5, ...), custom_call_target="tpu_custom_call" | custom-call | flops 805306368 | bytes 8913124 | tf_op jit(solution)/shard_map/first_step/pallas_call | solution.py:58
  26.0 4.6 %collective-permute-start.4 = (bf16[4,256,128]{2,1,0:T(8,128)(2,1)S(1)}, bf16[4,256,128]{2,1,0:T(8,128)(2,1)S(1)}, u32[]{:S(2)}, u32[]{:S(2)}) collective-permute-start(bf16[4,256,128]{2,1,0:T(8,128)(2,1)S(1)} %get-tuple-element.37), channel_id=1, source_target_pairs={{0,2},{1,3},{2,0},{3,1},{4,6},{5,7},{6,4},{7,5},{8,10},{9,11},{10,... | collective-permute-start | bytes 786440 | tf_op jit(solution)/shard_map/ppermute | solution.py:362
  30.6 0.1 collective-permute-start.5
  30.7 0.7 collective-permute-start.6
  31.4 0.7 collective-permute-start.7
  32.1 2.3 %collective-permute-done.4.refs_10_ = bf16[4,256,128]{2,1,0:T(8,128)(2,1)S(1)} collective-permute-done((bf16[4,256,128]{2,1,0:T(8,128)(2,1)S(1)}, bf16[4,256,128]{2,1,0:T(8,128)(2,1)S(1)}, u32[]{:S(2)}, u32[]{:S(2)}) %collective-permute-start.4) | collective-permute-done | bytes 262176 | tf_op jit(solution)/shard_map/ppermute | solution.py:362
  34.4 5.6 %collective-permute-done.5.refs_11_ = bf16[4,256,128]{2,1,0:T(8,128)(2,1)S(1)} collective-permute-done((bf16[4,256,128]{2,1,0:T(8,128)(2,1)S(1)}, bf16[4,256,128]{2,1,0:T(8,128)(2,1)S(1)}, u32[]{:S(2)}, u32[]{:S(2)}) %collective-permute-start.5) | collective-permute-done | bytes 262176 | tf_op jit(solution)/shard_map/ppermute | solution.py:362
  40.0 0.0 collective-permute-done.6.refs_12_
  40.0 0.0 collective-permute-done.7.refs_13_
  40.0 4.4 %second_step.1 = (bf16[8,256,128]{2,1,0:T(8,128)(2,1)}, bf16[8,128,256]{2,1,0:T(8,128)(2,1)}, f32[8,128,256]{2,1,0:T(8,128)}, bf16[4,256,128]{2,1,0:T(8,128)(2,1...) custom-call(s32[1,24]{1,0:T(1,128)S(1)} %copy-done.5, ...), custom_call_target="tpu_custom_call" | custom-call | flops 805306368 | bytes 10617060 | tf_op jit(solution)/shard_map/second_step/pallas_call | solution.py:58
  44.5 15.8 %all-to-all-start = ((bf16[16,32,128]{2,1,0:T(8,128)(2,1)}), bf16[16,32,128]{2,1,0:T(8,128)(2,1)S(1)}, u32[]{:S(2)}, u32[]{:S(2)}) async-start(bf16[16,32,128]{2,1,0:T(8,128)(2,1)} %bitcast.22), calls=%async_computation | async-start | bytes 262144 | tf_op jit(solution)/shard_map/all_to_all | solution.py:382
  60.2 2.9 %collective-permute-start.8 = (bf16[4,256,128]{2,1,0:T(8,128)(2,1)}, bf16[4,256,128]{2,1,0:T(8,128)(2,1)}, u32[]{:S(2)}, u32[]{:S(2)}) collective-permute-start(bf16[4,256,128]{2,1,0:T(8,128)(2,1)} %get-tuple-element.41), channel_id=1, source_target_pairs={{0,2},{1,3},{2,0},{3,1},{4,6},{5,7},{6,4},{7,5},{8,10},{9,11},{10,... | collective-permute-start | bytes 786440 | tf_op jit(solution)/shard_map/ppermute | solution.py:362
  63.1 0.3 collective-permute-start.9
  63.4 1.4 %collective-permute-start.10 = (bf16[4,256,128]{2,1,0:T(8,128)(2,1)}, bf16[4,256,128]{2,1,0:T(8,128)(2,1)}, u32[]{:S(2)}, u32[]{:S(2)}) collective-permute-start(bf16[4,256,128]{2,1,0:T(8,128)(2,1)} %get-tuple-element.43), channel_id=1, source_target_pairs={{1,2},{2,1},{3,4},{4,3},{5,6},{6,5},{7,8},{8,7},{9,10},{10,9},{11,... | collective-permute-start | bytes 786440 | tf_op jit(solution)/shard_map/ppermute | solution.py:362
  64.7 1.5 %collective-permute-start.11 = (bf16[4,256,128]{2,1,0:T(8,128)(2,1)}, bf16[4,256,128]{2,1,0:T(8,128)(2,1)}, u32[]{:S(2)}, u32[]{:S(2)}) collective-permute-start(bf16[4,256,128]{2,1,0:T(8,128)(2,1)} %get-tuple-element.44), channel_id=1, source_target_pairs={{2,4},{3,5},{4,2},{5,3},{6,8},{7,9},{8,6},{9,7},{10,12},{11,13},{1... | collective-permute-start | bytes 786440 | tf_op jit(solution)/shard_map/ppermute | solution.py:362
  66.2 0.7 all-to-all-done.parts
  67.0 26.4 %all_to_all.15.parts = bf16[16,32,128]{2,1,0:T(8,128)(2,1)S(1)} all-to-all(bf16[16,32,128]{2,1,0:T(8,128)(2,1)S(1)} %fold.2), channel_id=1, replica_groups=mesh['view'=2,'z'=8,'plane'=16] {'view','z'}, dimensions={0} | all-to-all | bytes 262144 | tf_op jit(solution)/shard_map/all_to_all | solution.py:382
  93.4 0.7 fold.3
  94.1 3.8 %all-to-all-start.2 = ((bf16[16,32,128]{2,1,0:T(8,128)(2,1)}), bf16[16,32,128]{2,1,0:T(8,128)(2,1)S(1)}, u32[]{:S(2)}, u32[]{:S(2)}) async-start(bf16[16,32,128]{2,1,0:T(8,128)(2,1)} %fold.3), calls=%async_computation.2 | async-start | bytes 262144 | tf_op jit(solution)/shard_map/all_to_all | solution.py:385
  97.9 5.3 %end.1 = (bf16[8,256,128]{2,1,0:T(8,128)(2,1)}, bf16[8,256,128]{2,1,0:T(8,128)(2,1)}) custom-call(s32[1,24]{1,0:T(1,128)S(1)} %copy-done.5, s32[1,24]{1,0:T(1,128)S(1)} %copy-done.6, s32[1]{0:T(128)S(6)} %copy.11.count.refs_2_, s32[1,2,4]{2,1,0:T(2,128)S(1)} %bitcast.18, bf16[24,256,256]{2,1,0:T(8,128)(2,1)S(1)} %get-tuple-element.27.refs_4_.tiles, ...), custom_call_target="tpu_custom_call" | custom-call | flops 12079595520 | bytes 9568484 | tf_op jit(solution)/shard_map/end/pallas_call | solution.py:58
  103.3 1.3 %all-to-all-done.2 = bf16[16,32,128]{2,1,0:T(8,128)(2,1)S(1)} async-done(((bf16[16,32,128]{2,1,0:T(8,128)(2,1)}), bf16[16,32,128]{2,1,0:T(8,128)(2,1)S(1)}, u32[]{:S(2)}, u32[]{:S(2)}) %all-to-all-start.2) | async-done | bytes 131104 | tf_op jit(solution)/shard_map/all_to_all | solution.py:385
  104.6 0.7 bitcast_convert_fusion
  (20 shorter events, 0.1 us)
Async XLA Ops:
  0.6 22.6 %copy-start.6 = (s32[1,24]{1,0:T(1,128)S(1)}, s32[1,24]{1,0:T(1,128)}, u32[]{:S(2)}) copy-start(s32[1,24]{1,0:T(1,128)} %source.1) | copy-start | bytes 292
  0.6 22.6 %copy-start.5 = (s32[1,24]{1,0:T(1,128)S(1)}, s32[1,24]{1,0:T(1,128)}, u32[]{:S(2)}) copy-start(s32[1,24]{1,0:T(1,128)} %target.1) | copy-start | bytes 292
  0.7 22.6 %copy-start.4 = (s32[1,4,2]{1,2,0:T(2,128)S(1)}, s32[1,4,2]{1,2,0:T(2,128)}, u32[]{:S(2)}) copy-start(s32[1,4,2]{1,2,0:T(2,128)} %param.15) | copy-start | bytes 100
  0.7 22.6 %copy-start = (bf16[1,2048,128]{2,1,0:T(8,128)(2,1)S(1)}, bf16[1,2048,128]{2,1,0:T(8,128)(2,1)}, u32[]{:S(2)}) copy-start(bf16[1,2048,128]{2,1,0:T(8,128)(2,1)} %param.8) | copy-start | bytes 1572868
  4.9 39.5 %copy-start.1 = (bf16[8,128,256]{2,1,0:T(8,128)(2,1)}, bf16[8,128,256]{2,1,0:T(8,128)(2,1)S(1)}, u32[]{:S(2)}) copy-start(bf16[8,128,256]{2,1,0:T(8,128)(2,1)S(1)} %get-tuple-element.35.refs_7_.refs_10_) | copy-start | bytes 1572868
  4.9 8.8 %collective-permute-start = (bf16[4,256,128]{2,1,0:T(8,128)(2,1)S(1)}, bf16[4,256,128]{2,1,0:T(8,128)(2,1)S(1)}, u32[]{:S(2)}, u32[]{:S(2)}) collective-permute-start(bf16[4,256,128]{2,1,0:T(8,128)(2,1)S(1)} %get-tuple-element.29), channel_id=1, source_target_pairs={{0,2},{1,3},{2,0},{3,1},{4,6},{5,7},{6,4},{7,5},{8,10},{9,11},{10,... | collective-permute-start | bytes 786440 | tf_op jit(solution)/shard_map/ppermute | solution.py:362
  8.7 14.5 %collective-permute-start.1 = (bf16[4,256,128]{2,1,0:T(8,128)(2,1)S(1)}, bf16[4,256,128]{2,1,0:T(8,128)(2,1)S(1)}, u32[]{:S(2)}, u32[]{:S(2)}) collective-permute-start(bf16[4,256,128]{2,1,0:T(8,128)(2,1)S(1)} %get-tuple-element.30), channel_id=1, source_target_pairs={{0,1},{1,0},{2,3},{3,2},{4,5},{5,4},{6,7},{7,6},{8,9},{9,8},{10,11... | collective-permute-start | bytes 786440 | tf_op jit(solution)/shard_map/ppermute | solution.py:362
  9.1 14.1 %collective-permute-start.2 = (bf16[4,256,128]{2,1,0:T(8,128)(2,1)S(1)}, bf16[4,256,128]{2,1,0:T(8,128)(2,1)S(1)}, u32[]{:S(2)}, u32[]{:S(2)}) collective-permute-start(bf16[4,256,128]{2,1,0:T(8,128)(2,1)S(1)} %get-tuple-element.31), channel_id=1, source_target_pairs={{1,2},{2,1},{3,4},{4,3},{5,6},{6,5},{7,8},{8,7},{9,10},{10,9},{11,... | collective-permute-start | bytes 786440 | tf_op jit(solution)/shard_map/ppermute | solution.py:362
  9.8 13.5 %collective-permute-start.3 = (bf16[4,256,128]{2,1,0:T(8,128)(2,1)S(1)}, bf16[4,256,128]{2,1,0:T(8,128)(2,1)S(1)}, u32[]{:S(2)}, u32[]{:S(2)}) collective-permute-start(bf16[4,256,128]{2,1,0:T(8,128)(2,1)S(1)} %get-tuple-element.32), channel_id=1, source_target_pairs={{2,4},{3,5},{4,2},{5,3},{6,8},{7,9},{8,6},{9,7},{10,12},{11,13},{1... | collective-permute-start | bytes 786440 | tf_op jit(solution)/shard_map/ppermute | solution.py:362
  26.0 18.4 %copy-start.2 = (bf16[8,256,128]{2,1,0:T(8,128)(2,1)}, bf16[8,256,128]{2,1,0:T(8,128)(2,1)S(1)}, u32[]{:S(2)}) copy-start(bf16[8,256,128]{2,1,0:T(8,128)(2,1)S(1)} %get-tuple-element.33.refs_5_) | copy-start | bytes 1572868
  26.0 18.4 %copy-start.3 = (bf16[8,128,256]{2,1,0:T(8,128)(2,1)}, bf16[8,128,256]{2,1,0:T(8,128)(2,1)S(1)}, u32[]{:S(2)}) copy-start(bf16[8,128,256]{2,1,0:T(8,128)(2,1)S(1)} %get-tuple-element.36.refs_9_.refs_8_) | copy-start | bytes 1572868
  26.0 8.4 %collective-permute-start.4 = (bf16[4,256,128]{2,1,0:T(8,128)(2,1)S(1)}, bf16[4,256,128]{2,1,0:T(8,128)(2,1)S(1)}, u32[]{:S(2)}, u32[]{:S(2)}) collective-permute-start(bf16[4,256,128]{2,1,0:T(8,128)(2,1)S(1)} %get-tuple-element.37), channel_id=1, source_target_pairs={{0,2},{1,3},{2,0},{3,1},{4,6},{5,7},{6,4},{7,5},{8,10},{9,11},{10,... | collective-permute-start | bytes 786440 | tf_op jit(solution)/shard_map/ppermute | solution.py:362
  30.6 9.4 %collective-permute-start.5 = (bf16[4,256,128]{2,1,0:T(8,128)(2,1)S(1)}, bf16[4,256,128]{2,1,0:T(8,128)(2,1)S(1)}, u32[]{:S(2)}, u32[]{:S(2)}) collective-permute-start(bf16[4,256,128]{2,1,0:T(8,128)(2,1)S(1)} %get-tuple-element.38), channel_id=1, source_target_pairs={{0,1},{1,0},{2,3},{3,2},{4,5},{5,4},{6,7},{7,6},{8,9},{9,8},{10,11... | collective-permute-start | bytes 786440 | tf_op jit(solution)/shard_map/ppermute | solution.py:362
  30.7 9.3 %collective-permute-start.6 = (bf16[4,256,128]{2,1,0:T(8,128)(2,1)S(1)}, bf16[4,256,128]{2,1,0:T(8,128)(2,1)S(1)}, u32[]{:S(2)}, u32[]{:S(2)}) collective-permute-start(bf16[4,256,128]{2,1,0:T(8,128)(2,1)S(1)} %get-tuple-element.39), channel_id=1, source_target_pairs={{1,2},{2,1},{3,4},{4,3},{5,6},{6,5},{7,8},{8,7},{9,10},{10,9},{11,... | collective-permute-start | bytes 786440 | tf_op jit(solution)/shard_map/ppermute | solution.py:362
  31.4 8.6 %collective-permute-start.7 = (bf16[4,256,128]{2,1,0:T(8,128)(2,1)S(1)}, bf16[4,256,128]{2,1,0:T(8,128)(2,1)S(1)}, u32[]{:S(2)}, u32[]{:S(2)}) collective-permute-start(bf16[4,256,128]{2,1,0:T(8,128)(2,1)S(1)} %get-tuple-element.40), channel_id=1, source_target_pairs={{2,4},{3,5},{4,2},{5,3},{6,8},{7,9},{8,6},{9,7},{10,12},{11,13},{1... | collective-permute-start | bytes 786440 | tf_op jit(solution)/shard_map/ppermute | solution.py:362
  44.5 22.5 %all-to-all-start = ((bf16[16,32,128]{2,1,0:T(8,128)(2,1)}), bf16[16,32,128]{2,1,0:T(8,128)(2,1)S(1)}, u32[]{:S(2)}, u32[]{:S(2)}) async-start(bf16[16,32,128]{2,1,0:T(8,128)(2,1)} %bitcast.22), calls=%async_computation | async-start | bytes 262144 | tf_op jit(solution)/shard_map/all_to_all | solution.py:382
  60.2 37.7 %collective-permute-start.8 = (bf16[4,256,128]{2,1,0:T(8,128)(2,1)}, bf16[4,256,128]{2,1,0:T(8,128)(2,1)}, u32[]{:S(2)}, u32[]{:S(2)}) collective-permute-start(bf16[4,256,128]{2,1,0:T(8,128)(2,1)} %get-tuple-element.41), channel_id=1, source_target_pairs={{0,2},{1,3},{2,0},{3,1},{4,6},{5,7},{6,4},{7,5},{8,10},{9,11},{10,... | collective-permute-start | bytes 786440 | tf_op jit(solution)/shard_map/ppermute | solution.py:362
  63.1 34.8 %collective-permute-start.9 = (bf16[4,256,128]{2,1,0:T(8,128)(2,1)}, bf16[4,256,128]{2,1,0:T(8,128)(2,1)}, u32[]{:S(2)}, u32[]{:S(2)}) collective-permute-start(bf16[4,256,128]{2,1,0:T(8,128)(2,1)} %get-tuple-element.42), channel_id=1, source_target_pairs={{0,1},{1,0},{2,3},{3,2},{4,5},{5,4},{6,7},{7,6},{8,9},{9,8},{10,11... | collective-permute-start | bytes 786440 | tf_op jit(solution)/shard_map/ppermute | solution.py:362
  63.4 34.5 %collective-permute-start.10 = (bf16[4,256,128]{2,1,0:T(8,128)(2,1)}, bf16[4,256,128]{2,1,0:T(8,128)(2,1)}, u32[]{:S(2)}, u32[]{:S(2)}) collective-permute-start(bf16[4,256,128]{2,1,0:T(8,128)(2,1)} %get-tuple-element.43), channel_id=1, source_target_pairs={{1,2},{2,1},{3,4},{4,3},{5,6},{6,5},{7,8},{8,7},{9,10},{10,9},{11,... | collective-permute-start | bytes 786440 | tf_op jit(solution)/shard_map/ppermute | solution.py:362
  64.7 33.2 %copy-start.7 = (bf16[4,128,128]{2,1,0:T(8,128)(2,1)S(1)}, bf16[4,128,128]{2,1,0:T(8,128)(2,1)}, u32[]{:S(2)}) copy-start(bf16[4,128,128]{2,1,0:T(8,128)(2,1)} %filters.1) | copy-start | bytes 393220
  64.7 33.2 %collective-permute-start.11 = (bf16[4,256,128]{2,1,0:T(8,128)(2,1)}, bf16[4,256,128]{2,1,0:T(8,128)(2,1)}, u32[]{:S(2)}, u32[]{:S(2)}) collective-permute-start(bf16[4,256,128]{2,1,0:T(8,128)(2,1)} %get-tuple-element.44), channel_id=1, source_target_pairs={{2,4},{3,5},{4,2},{5,3},{6,8},{7,9},{8,6},{9,7},{10,12},{11,13},{1... | collective-permute-start | bytes 786440 | tf_op jit(solution)/shard_map/ppermute | solution.py:362
  94.1 10.5 %all-to-all-start.2 = ((bf16[16,32,128]{2,1,0:T(8,128)(2,1)}), bf16[16,32,128]{2,1,0:T(8,128)(2,1)S(1)}, u32[]{:S(2)}, u32[]{:S(2)}) async-start(bf16[16,32,128]{2,1,0:T(8,128)(2,1)} %fold.3), calls=%async_computation.2 | async-start | bytes 262144 | tf_op jit(solution)/shard_map/all_to_all | solution.py:385
